TPU v7x, 256 devices: a whole 4x4x8 slice. The times are simulated.
256 devices in a mesh: tm: 16 (over y_hi, z), batch: 8 (over x, core), width: 2 (over y_lo).
Axes of the slice: x: 4, y: 4 (y_hi: 2, y_lo: 2; y = y_hi * 2 + y_lo), z: 8, core: 2. Of those that a mesh axis runs over, the one named last changes fastest.
Arguments:
- moves: int32 [16, 4096], P('batch', 'tm'), may hold values from 0 to 361
- lengths: int32 [16], P('batch'), may hold values from 1 to 4096
- outcomes: int32 [16], P('batch'), may hold values from -1 to 1
- embedded: bfloat16 [16, 4096, 2048], P('batch', 'tm', 'width'), may hold values from -6 to 6
- w_branches: bfloat16 [4, 2048, 2048], P(None, ('tm', 'batch'), 'width'), may hold values from -0.125 to 0.125
- conv_w: float32 [4, 2048], P(None, 'width'), may hold values from -3 to 3
- gate_bias: float32 [2, 2048], P(None, 'width'), may hold values from -4 to 4
- rates: float32 [2048], P('width'), may hold values from 0.001 to 0.105
- w_down: bfloat16 [2048, 2048], P(('tm', 'batch'), 'width'), may hold values from -0.125 to 0.125
- w_policy: bfloat16 [2048, 362], P('width'), may hold values from -12 to 12
- w_value: bfloat16 [2048], P('width'), may hold values from -0.125 to 0.125
Outputs:
- position_loss: float32 [16, 4096], P('batch', 'tm')
- value: float32 [16, 4096], P('batch', 'tm')
All inputs are finite; a program needn't handle non-finite values.
Results may differ from a plain program's by a relative error of at most 0.0033.
Values may be sent and summed in bfloat16 or wider, within the bound.
No kernel may reach another device: no remote copies, remote signals or barrier semaphores. Data moves between devices by JAX's collectives and lax.ppermute only.
A program may use at most 128 MiB of HBM per device.

v0:
```python
import jax
import jax.numpy as jnp
from jax import lax
from jax.sharding import PartitionSpec as P

D = 2048
KERNEL = 4


def from_behind(value, axis, steps):
    count = lax.axis_size(axis)
    initial, last = (max(0, -steps), min(count, count - steps))
    return lax.ppermute(value, axis, [(source, source + steps) for source in range(initial, last)])


def collected_together(x, axis):
    leaves = jax.tree.leaves(x)
    turns = sorted(range(len(leaves)), key=lambda k: -leaves[k].size)
    width = (1, *leaves[turns[0]].shape)[-1]
    lines = [
        jnp.pad(leaves[k].reshape(-1), (0, -leaves[k].size % width)).reshape(-1, width)
        for k in turns
    ]
    both, at, found = (lax.all_gather(jnp.concatenate(lines), axis), 0, {})
    for k, line in zip(turns, lines):
        share = both[:, at : at + len(line)].reshape(len(both), -1)
        found[k] = share[:, : leaves[k].size].reshape(-1, *leaves[k].shape)
        at += len(line)
    numbers = iter(range(len(leaves)))
    return jax.tree.map(lambda _: found[next(numbers)], x)


def prefix(x, axis, combine, identity):
    length, here = (lax.axis_size(axis), lax.axis_index(axis))
    everything = collected_together(x, axis)
    start = jax.tree.map(
        lambda part, zero: jnp.broadcast_to(jnp.asarray(zero, part.dtype), part.shape), x, identity
    )

    def turn(k, before):
        reached = k < here
        new = combine(before, jax.tree.map(lambda part: part[k], everything))
        return jax.tree.map(lambda a, b: jnp.where(reached, a, b), new, before)

    return lax.fori_loop(0, length, turn, start)


def in_blocks(x, dim, length):
    lengths = x.shape
    pieces = x.reshape(*lengths[:dim], length, lengths[dim] // length, *lengths[dim + 1 :])
    return jnp.moveaxis(pieces, dim, 0)


def sum_at_owner(x, axis, dim):
    length = lax.axis_size(axis)
    pieces = lax.all_to_all(in_blocks(x, dim, length), axis, 0, 0, tiled=True)
    return jnp.sum(pieces, axis=0)


def sent_to_all(x, axis):
    length = lax.axis_size(axis)
    return lax.all_to_all(jnp.broadcast_to(x[None], (length, *x.shape)), axis, 0, 0, tiled=True)


def over_copies(x, axis):
    return sent_to_all(x, axis).sum(axis=0)


def packed_total(arrays, axis):
    ends = [0]
    for a in arrays:
        ends.append(ends[-1] + a.size)
    total = over_copies(jnp.concatenate([a.ravel() for a in arrays]), axis)
    return tuple((total[b:e].reshape(a.shape) for a, b, e in zip(arrays, ends, ends[1:])))


def link(early, late):
    return (early[0] + late[0], jnp.exp(late[0]) * early[1] + late[1])


def compose(early, late):
    return (early[0] * late[0], late[0] * early[1] + late[1])


def shards(
    moves,
    lengths,
    outcomes,
    embedded,
    w_branches,
    conv_w,
    gate_bias,
    rates,
    w_down,
    w_policy,
    w_value,
):
    games, block_len, half = embedded.shape
    count = games * block_len
    chans = w_branches.shape[2]
    features = lax.all_gather(embedded, "width", axis=2, tiled=True).reshape(count, -1)
    proj = jnp.einsum(
        "td,kdn->ktn",
        features,
        lax.all_gather(w_branches, ("tm", "batch"), axis=1, tiled=True),
        preferred_element_type=jnp.float32,
    )
    proj = proj.reshape(4, games, block_len, chans)
    gated = jax.nn.gelu(proj[0])
    source = proj[1]
    prior = from_behind(source[:, block_len - (KERNEL - 1) :, :], "tm", 1)
    extended = jnp.concatenate([prior, source], 1)
    conv = jnp.zeros((games, block_len, chans), jnp.float32)
    for k in range(KERNEL):
        conv = conv + conv_w[k] * extended[:, KERNEL - 1 - k : KERNEL - 1 - k + block_len]
    recur = jax.nn.sigmoid(proj[2] + gate_bias[0])
    inflow = jax.nn.sigmoid(proj[3] + gate_bias[1])
    log_a = -8.0 * recur * rates
    decay = jnp.exp(log_a)
    drive = jnp.sqrt(1.0 - decay * decay) * inflow * conv
    summed, local = lax.associative_scan(link, (log_a, drive), axis=1)
    block_decay = jnp.exp(summed[:, -1])
    block_end = local[:, -1]
    identity = (jnp.ones_like(block_decay), jnp.zeros_like(block_end))
    _, incoming = prefix((block_decay, block_end), "tm", compose, identity)
    hidden = local + jnp.exp(summed) * incoming[:, None, :]
    mixed = (hidden * gated).astype(jnp.bfloat16).reshape(count, chans)
    partial_down = lax.dot_general(
        mixed,
        lax.all_gather(w_down, ("tm", "batch"), axis=0, tiled=True),
        (((1,), (1,)), ((), ())),
        preferred_element_type=jnp.float32,
    )
    down = sum_at_owner(partial_down, "width", 1)
    resid = (embedded.reshape(count, half).astype(jnp.float32) + down).astype(jnp.bfloat16)
    wide = resid.astype(jnp.float32)
    local_sq = jnp.sum(wide * wide, -1)
    local_logits = jnp.dot(resid, w_policy, preferred_element_type=jnp.float32)
    local_value = jnp.dot(resid, w_value, preferred_element_type=jnp.float32)
    raw_logits, raw_value, sumsq = packed_total((local_logits, local_value, local_sq), "width")
    norm = lax.rsqrt(sumsq / D + 1e-06)
    logits = raw_logits * norm[:, None]
    value = jnp.tanh(raw_value * norm)
    top = jnp.max(logits, -1, keepdims=True)
    lse = top[:, 0] + jnp.log(jnp.sum(jnp.exp(logits - top), -1))
    column = lax.broadcasted_iota(jnp.int32, logits.shape, 1)
    picked = jnp.sum(jnp.where(column == moves.reshape(count, 1), logits, 0.0), -1)
    target = jnp.broadcast_to(outcomes.astype(jnp.float32)[:, None], (games, block_len)).reshape(
        count
    )
    position = lax.axis_index("tm") * block_len + lax.broadcasted_iota(
        jnp.int32, (games, block_len), 1
    )
    where_live = (position < lengths[:, None]).reshape(count)
    loss = jnp.where(where_live, lse - picked + (value - target) ** 2, 0.0)
    return (loss.reshape(games, block_len), value.reshape(games, block_len))


def solution(mesh):
    in_specs = (
        P("batch", "tm"),
        P("batch"),
        P("batch"),
        P("batch", "tm", "width"),
        P(None, ("tm", "batch"), "width"),
        P(None, "width"),
        P(None, "width"),
        P("width"),
        P(("tm", "batch"), "width"),
        P("width", None),
        P("width"),
    )
    out_specs = (P("batch", "tm"), P("batch", "tm"))
    return jax.shard_map(shards, mesh=mesh, in_specs=in_specs, out_specs=out_specs, check_vma=False)
```

profile of v0, /device:TPU:16, one launch (start us, length us, event | category | flops | bytes accessed | tf_op | source)
XLA Modules:
  0.0 543.8 jit_solution(808997594253362417)
XLA Ops:
  11.1 39.5 %all-gather.8.cloned.1.call-done = bf16[2,256,2048]{2,1,0:T(8,128)(2,1)} async-done(((bf16[2,256,1024]{2,1,0:T(8,128)(2,1)}), bf16[2,256,2048]{2,1,0:T(8,128)(2,1)}) %all-gather.8.cloned.1.call-update) | async-done | bytes 2097168 | tf_op jit(solution)/shard_map/all_gather | solution.py:101
  50.5 150.2 %all-gather.6.cloned.1.call-done = bf16[4,2048,1024]{2,1,0:T(8,128)(2,1)} async-done(((bf16[4,16,1024]{2,1,0:T(8,128)(2,1)}), bf16[4,2048,1024]{2,1,0:T(8,128)(2,1)}) %all-gather.6.cloned.1.call-update) | async-done | bytes 16777232 | tf_op jit(solution)/shard_map/all_gather | solution.py:105
  200.7 12.5 %convolution_bitcast_fusion = f32[4,512,1024]{2,1,0:T(8,128)S(1)} fusion(bf16[512,2048,1]{1,0,2:T(8,128)(2,1)} %bitcast.96, bf16[4,2048,1024]{2,1,0:T(8,128)(2,1)} %all-gather.6.cloned.1.call-done), kind=kOutput, calls=%fused_computation.3 | convolution fusion | flops 8589934592 | bytes 27262976 | tf_op jit(solution)/shard_map/td,kdn->ktn/dot_general | solution.py:102
  217.5 3.5 collective-permute-start
  221.0 5.9 %collective-permute-done = f32[2,3,1024]{2,1,0:T(4,128)S(1)} collective-permute-done((f32[2,3,1024]{2,1,0:T(4,128)S(1)}, f32[2,3,1024]{2,1,0:T(4,128)S(1)}, u32[]{:S(2)}, u32[]{:S(2)}) %collective-permute-start) | collective-permute-done | bytes 24608 | tf_op jit(solution)/shard_map/ppermute | solution.py:13
  226.9 7.6 %fusion.5 = (f32[2,256,1024]{2,1,0:T(8,128)S(1)}, f32[2,256,1024]{2,1,0:T(8,128)}) fusion(f32[2,3,1024]{2,1,0:T(4,128)S(1)} %collective-permute-done, f32[2,256,1024]{2,1,0:T(8,128)} %bitcast.67, f32[2,256,1024]{2,1,0:T(8,128)} %bitcast.70, f32[1024]{0:T(1024)S(1)} %bitcast.88, f32[1024]{0:T(1024)S(1)} %bitcast.89, f32[1024]{0:T(1024)S(1)} %bitcast.87, ...), kind=kLoop, calls=%fused_computation.12 | loop fusion | flops 12058624 | bytes 10539008 | tf_op jit(solution)/shard_map/mul | solution.py:120
  240.3 5.4 slice.332
  245.7 5.4 slice.336
  251.1 4.1 multiply_add_fusion
  325.7 3.3 slice.337
  335.2 5.6 %slice.331 = f32[2,127,1024]{2,1,0:T(8,128)} slice(f32[2,256,1024]{2,1,0:T(8,128)} %get-tuple-element.128), slice={[0:2:1], [2:256:2], [0:1024:1]} | slice | bytes 2080768 | tf_op jit(solution)/shard_map/slice | solution.py:121
  356.1 5.4 pad.129
  375.3 5.4 pad.128
  381.6 5.4 pad.113
  389.3 5.5 %pad.112 = f32[2,256,1024]{2,1,0:T(8,128)} pad(f32[2,128,1024]{2,1,0:T(8,128)} %pad_maximum_fusion.1, f32[]{:T(128)} %constant.43.clone.1), padding=0_0_0x0_1_1x0_0_0 | pad | bytes 3145732 | tf_op jit(solution)/shard_map/pad | solution.py:121
  395.6 37.9 %all-gather.1 = f32[16,4,1024]{2,1,0:T(4,128)S(1)} all-gather(f32[1,4,1024]{2,1,0:T(4,128)S(1)} %maximum_bitcast_fusion), channel_id=2, replica_groups=mesh['tm'=16,'batch'=8,'width'=2] {'tm'}, dimensions={0}, use_global_device_ids=true | all-gather | bytes 278528 | tf_op jit(solution)/shard_map/all_gather | solution.py:24
  434.4 5.8 %fusion.17 = bf16[2,256,1024]{2,1,0:T(8,128)(2,1)} fusion(f32[2,256,1024]{2,1,0:T(8,128)} %bitcast.68, f32[2,256,1024]{2,1,0:T(8,128)} %pad.128, f32[2,256,1024]{2,1,0:T(8,128)S(1)} %copy-done.4, f32[2,256,1024]{2,1,0:T(8,128)} %pad.112, f32[2,256,1024]{2,1,0:T(8,128)} %pad.113, f32[2,1024]{1,0:T(2,128)S(1)} %get-tuple-element.96), kind=kLoop, calls=%fused_computation.24 | loop fusion | flops 7340032 | bytes 11542528 | tf_op jit(solution)/shard_map/convert_element_type | solution.py:127
  440.1 6.9 %convolution_bitcast_fusion.1 = f32[2,512,1024]{2,1,0:T(8,128)} fusion(bf16[512,1024,1]{1,0,2:T(8,128)(2,1)} %bitcast.71, bf16[2,1024,1024]{2,1,0:T(8,128)(2,1)} %bitcast.95), kind=kOutput, calls=%fused_computation.7 | convolution fusion | flops 2147483648 | bytes 9437184 | tf_op jit(solution)/shard_map/dot_general | solution.py:128
  447.0 5.8 %all-to-all-start = ((f32[2,512,1024]{2,1,0:T(8,128)}), f32[2,512,1024]{2,1,0:T(8,128)}, u32[]{:S(2)}, u32[]{:S(2)}) async-start(f32[2,512,1024]{2,1,0:T(8,128)} %convolution_bitcast_fusion.1), calls=%async_computation | async-start | bytes 8388608 | tf_op jit(solution)/shard_map/all_to_all | solution.py:56
  452.8 40.3 %all-to-all-done = f32[2,512,1024]{2,1,0:T(8,128)} async-done(((f32[2,512,1024]{2,1,0:T(8,128)}), f32[2,512,1024]{2,1,0:T(8,128)}, u32[]{:S(2)}, u32[]{:S(2)}) %all-to-all-start) | async-done | bytes 4194336 | tf_op jit(solution)/shard_map/all_to_all | solution.py:56
  506.3 4.3 broadcast_in_dim.14
  510.6 3.9 all-to-all-start.1
  514.5 11.4 %all-to-all-done.1 = f32[2,1,186368]{2,1,0:T(1,128)S(1)} async-done(((f32[2,1,186368]{2,1,0:T(1,128)}), f32[2,1,186368]{2,1,0:T(1,128)S(1)}, u32[]{:S(2)}, u32[]{:S(2)}) %all-to-all-start.1) | async-done | bytes 1490976 | tf_op jit(solution)/shard_map/all_to_all | solution.py:62
  526.0 7.0 %reduce_sum.53 = f32[186368]{0:T(1024)S(1)} reduce(f32[2,1,186368]{2,1,0:T(1,128)S(1)} %all-to-all-done.1, f32[]{:T(128)} %constant.43.clone.1), dimensions={0,1}, to_apply=%region_4.5 | reduce | flops 186368 | bytes 2236420 | tf_op jit(solution)/shard_map/reduce_sum | solution.py:66
  (239 shorter events, 141.8 us)
Async XLA Ops:
  7.2 491.3 %copy-start = (bf16[1024,362]{0,1:T(8,128)(2,1)S(1)}, bf16[1024,362]{0,1:T(8,128)(2,1)}, u32[]{:S(2)}) copy-start(bf16[1024,362]{0,1:T(8,128)(2,1)} %param.22) | copy-start | bytes 2224132
  7.2 43.4 %all-gather.8.cloned.1.call-start = ((), (), s32[]{:S(2)}) async-start(), calls=%async_computation.3 | async-start | bytes 3145728 | tf_op jit(solution)/shard_map/all_gather | solution.py:101
  7.9 192.8 %all-gather.6.cloned.1.call-start = ((), (), s32[]{:S(2)}) async-start(), calls=%async_computation.2 | async-start | bytes 16908288 | tf_op jit(solution)/shard_map/all_gather | solution.py:105
  8.7 431.5 %all-gather.10.cloned.1.call-start = ((), (), s32[]{:S(2)}) async-start(), calls=%async_computation.4 | async-start | bytes 4227072 | tf_op jit(solution)/shard_map/all_gather | solution.py:130
  213.2 7.8 %copy-start.30 = (f32[1024]{0:T(1024)S(1)}, f32[1024]{0:T(1024)}, u32[]{:S(2)}) copy-start(f32[1024]{0:T(1024)} %param.20) | copy-start | bytes 12292
  217.5 9.5 %collective-permute-start = (f32[2,3,1024]{2,1,0:T(4,128)S(1)}, f32[2,3,1024]{2,1,0:T(4,128)S(1)}, u32[]{:S(2)}, u32[]{:S(2)}) collective-permute-start(f32[2,3,1024]{2,1,0:T(4,128)S(1)} %slice.415), channel_id=1, source_target_pairs={{0,16},{16,32},{32,48},{48,64},{64,80},{80,96},{96,112},{112,128},... | collective-permute-start | bytes 73736 | tf_op jit(solution)/shard_map/ppermute | solution.py:13
  335.2 10.0 %copy-start.17 = (f32[2,2,1024]{2,1,0:T(2,128)S(1)}, f32[2,2,1024]{2,1,0:T(2,128)}, u32[]{:S(2)}) copy-start(f32[2,2,1024]{2,1,0:T(2,128)} %get-tuple-element.178) | copy-start | bytes 49156
  335.2 10.1 %copy-start.16 = (f32[2,2,1024]{2,1,0:T(2,128)S(1)}, f32[2,2,1024]{2,1,0:T(2,128)}, u32[]{:S(2)}) copy-start(f32[2,2,1024]{2,1,0:T(2,128)} %get-tuple-element.177) | copy-start | bytes 49156
  335.2 10.1 %copy-start.25 = (f32[2,1,1024]{2,1,0:T(1,128)S(1)}, f32[2,1,1024]{2,1,0:T(1,128)}, u32[]{:S(2)}) copy-start(f32[2,1,1024]{2,1,0:T(1,128)} %get-tuple-element.159) | copy-start | bytes 24580
  335.2 10.1 %copy-start.26 = (f32[2,1,1024]{2,1,0:T(1,128)S(1)}, f32[2,1,1024]{2,1,0:T(1,128)}, u32[]{:S(2)}) copy-start(f32[2,1,1024]{2,1,0:T(1,128)} %get-tuple-element.160) | copy-start | bytes 24580
  335.2 10.2 %copy-start.27 = (f32[2,1,1024]{2,1,0:T(1,128)S(1)}, f32[2,1,1024]{2,1,0:T(1,128)}, u32[]{:S(2)}) copy-start(f32[2,1,1024]{2,1,0:T(1,128)} %get-tuple-element.161) | copy-start | bytes 24580
  335.2 10.2 %copy-start.28 = (f32[2,1,1024]{2,1,0:T(1,128)S(1)}, f32[2,1,1024]{2,1,0:T(1,128)}, u32[]{:S(2)}) copy-start(f32[2,1,1024]{2,1,0:T(1,128)} %get-tuple-element.162) | copy-start | bytes 24580
  335.2 10.3 %copy-start.15 = (f32[2,3,1024]{2,1,0:T(4,128)S(1)}, f32[2,3,1024]{2,1,0:T(4,128)}, u32[]{:S(2)}) copy-start(f32[2,3,1024]{2,1,0:T(4,128)} %slice.378) | copy-start | bytes 73732
  340.8 6.4 %copy-start.13 = (f32[2,7,1024]{2,1,0:T(8,128)S(1)}, f32[2,7,1024]{2,1,0:T(8,128)}, u32[]{:S(2)}) copy-start(f32[2,7,1024]{2,1,0:T(8,128)} %slice.355) | copy-start | bytes 172036
  340.8 6.4 %copy-start.14 = (f32[2,7,1024]{2,1,0:T(8,128)S(1)}, f32[2,7,1024]{2,1,0:T(8,128)}, u32[]{:S(2)}) copy-start(f32[2,7,1024]{2,1,0:T(8,128)} %slice.380) | copy-start | bytes 172036
  343.8 5.2 copy-start.12
  356.1 5.4 copy-start.19
  375.3 5.4 copy-start.4
  447.0 5.8 %copy-start.31 = (bf16[1024]{0:T(1024)(128)(2,1)S(1)}, bf16[1024]{0:T(1024)(128)(2,1)}, u32[]{:S(2)}) copy-start(bf16[1024]{0:T(1024)(128)(2,1)} %param.23) | copy-start | bytes 6148
  447.0 46.1 %all-to-all-start = ((f32[2,512,1024]{2,1,0:T(8,128)}), f32[2,512,1024]{2,1,0:T(8,128)}, u32[]{:S(2)}, u32[]{:S(2)}) async-start(f32[2,512,1024]{2,1,0:T(8,128)} %convolution_bitcast_fusion.1), calls=%async_computation | async-start | bytes 8388608 | tf_op jit(solution)/shard_map/all_to_all | solution.py:56
  506.2 8.2 %copy-start.32 = (s32[2,256]{1,0:T(2,128)S(1)}, s32[2,256]{1,0:T(2,128)}, u32[]{:S(2)}) copy-start(s32[2,256]{1,0:T(2,128)} %param.13) | copy-start | bytes 6148
  506.3 8.3 %copy-start.34 = (s32[2]{0:T(128)S(1)}, s32[2]{0:T(128)}, u32[]{:S(2)}) copy-start(s32[2]{0:T(128)} %param.15) | copy-start | bytes 28
  510.6 15.4 %all-to-all-start.1 = ((f32[2,1,186368]{2,1,0:T(1,128)}), f32[2,1,186368]{2,1,0:T(1,128)S(1)}, u32[]{:S(2)}, u32[]{:S(2)}) async-start(f32[2,1,186368]{2,1,0:T(1,128)} %broadcast_in_dim.14), calls=%async_computation.1 | async-start | bytes 2981888 | tf_op jit(solution)/shard_map/all_to_all | solution.py:62
  532.9 3.7 copy-start.33
  (17 other events, 29.9 us)
Sparse Core Ops, SparseCore 0:
  9.8 40.6 all-gather.7
  54.2 146.4 all-gather.5
  204.4 115.7 all-gather.9
where the time goes:
time: 547 us; the launch traced here: 544 us
  waiting for transfers between devices  249 us (46%)
  local copies, waits for them, and re-layouts  142 us (26%)
  other arithmetic  64 us (12%)
  blocking collectives  37.9 us (7%)
  matrix products  22.7 us (4%)
  between operations  14.6 us (3%)
  starting transfers between devices  13.3 us (2%)
    all_gather x1, waiting for transfers between devices, shards(): lax.all_gather(w_branches, ('tm', 'batch'), axis=1, tiled=True)  150 us
    slice x52, local copies, waits for them, and re-layouts, shards(): summed, local = lax.associative_scan(link, (log_a, drive), axis=1)  94.2 us
    all_to_all x1, waiting for transfers between devices, sum_at_owner(): pieces = lax.all_to_all(in_blocks(x, dim, length), axis, 0, 0, tiled=True)  40.3 us
    all_gather x1, waiting for transfers between devices, shards(): lax.all_gather(embedded, 'width', axis=2, tiled=True).reshape(count, -1)  39.5 us
    all_gather x1, blocking collectives, collected_together(): both, at, found = (lax.all_gather(jnp.concatenate(lines), axis), 0, {})  37.9 us
    pad x28, local copies, waits for them, and re-layouts, shards(): summed, local = lax.associative_scan(link, (log_a, drive), axis=1)  29.1 us
    add x13, other arithmetic, link(): return (early[0] + late[0], jnp.exp(late[0]) * early[1] + late[1])  18.5 us
    dot_general x1, matrix products, shards(): jnp.einsum('td,kdn->ktn', features, lax.all_gather(w_branches, ('tm', 'ba...  12.5 us
  transfers between devices with their start and end apart: 6, of which 5 were waited for; matrix products, arithmetic and copies ran while one was open for 35% of the time, Pallas kernels for 0%

commit v1 on v0

v1 whole, which is shorter than its diff:
```python
import jax
import jax.numpy as jnp
from jax import lax
from jax.experimental import pallas as pl
from jax.experimental.pallas import tpu as pltpu
from jax.sharding import Mesh
from jax.sharding import PartitionSpec as P

D = 2048
HALF = 1024
KERNEL = 4
MOVES = 362
COLS = 384
STEPS = 256
CH = 256
SEQS = 8
LANES = CH // 128
TAIL = 8
VMEM_LIMIT = 56 * 1024 * 1024

F32 = jnp.float32
BF16 = jnp.bfloat16
ANY = pl.BlockSpec(memory_space=pl.ANY)
VM = pl.BlockSpec(memory_space=pltpu.VMEM)
SM = pl.BlockSpec(memory_space=pltpu.SMEM)

PAIR = [(0, 1), (1, 0), (2, 3), (3, 2)]
OTHER = [(0, 3), (3, 0), (1, 2), (2, 1)]
SWAP = [(0, 1), (1, 0)]


def dot(a, b):
    return jnp.dot(a, b, preferred_element_type=F32)


def piece_copies(pieces, xa, xb, sems):
    copies = []
    for core, (own, pair, other, far0, far1) in enumerate(pieces):
        first = pl.ds(core * 2, 2)
        second = pl.ds(4 + core * 2, 2)
        k = core * 5
        copies.append(pltpu.make_async_copy(own, xa.at[first], sems.at[k]))
        copies.append(pltpu.make_async_copy(pair, xb.at[first], sems.at[k + 1]))
        copies.append(pltpu.make_async_copy(far0, xa.at[4 + core * 2], sems.at[k + 2]))
        copies.append(pltpu.make_async_copy(far1, xa.at[5 + core * 2], sems.at[k + 3]))
        copies.append(pltpu.make_async_copy(other, xb.at[second], sems.at[k + 4]))
    return copies


def weight_copies(gathered, held, sems):
    copies = []
    for b in range(held.shape[0]):
        for h in range(2):
            copies.append(
                pltpu.make_async_copy(gathered.at[:, b, h], held.at[b, h], sems.at[b * 2 + h])
            )
    return copies


def half_of(held, branch, half):
    return held[branch, half].reshape(HALF, CH)


def recur_kernel(meta, *refs):
    pieces = (refs[0:5], refs[5:10])
    gathered, tail_a, tail_b, conv_w, bias, rates = refs[10:16]
    decays, states, ends = refs[16:19]
    xa, xb, held, ext, tails, x_sems, w_sems = refs[19:]
    w = meta[0]
    to_held = weight_copies(gathered, held, w_sems)
    to_x = piece_copies(pieces, xa, xb, x_sems)
    for copy in to_held:
        copy.start()
    for copy in to_x:
        copy.start()
    for copy in to_held:
        copy.wait()
    for copy in to_x:
        copy.wait()
    tails[...] = dot(tail_a[...], half_of(held, 0, w)) + dot(tail_b[...], half_of(held, 0, 1 - w))

    def one(i, carry):
        a, b = xa[i], xb[i]

        def proj(branch):
            return dot(a, half_of(held, branch, w)) + dot(b, half_of(held, branch, 1 - w))

        source = proj(0)
        ext[0:TAIL] = tails[pl.ds(pl.multiple_of(i * TAIL, TAIL), TAIL)]
        ext[TAIL:] = source
        conv = conv_w[0:1] * source
        for k in range(1, KERNEL):
            conv = conv + conv_w[k : k + 1] * ext[TAIL - k : TAIL - k + STEPS]
        recur = jax.nn.sigmoid(proj(1) + bias[0:1])
        inflow = jax.nn.sigmoid(proj(2) + bias[1:2])
        decay = jnp.exp(-8.0 * recur * rates[...])
        drive = jnp.sqrt(1.0 - decay * decay) * inflow * conv
        for lane in range(LANES):
            cols = slice(lane * 128, (lane + 1) * 128)
            decays[lane, pl.ds(i, STEPS, stride=SEQS), :] = decay[:, cols]
            states[lane, pl.ds(i, STEPS, stride=SEQS), :] = drive[:, cols]
        return carry

    lax.fori_loop(0, SEQS, one, 0)

    def step(t, carry):
        at = pl.ds(pl.multiple_of(t * SEQS, SEQS), SEQS)
        done = []
        for lane, (state, product) in enumerate(carry):
            decay = decays[lane, at]
            state = decay * state + states[lane, at]
            product = product * decay
            states[lane, at] = state
            decays[lane, at] = product
            done.append((state, product))
        return tuple(done)

    start = (jnp.zeros((SEQS, 128), F32), jnp.ones((SEQS, 128), F32))
    last = lax.fori_loop(0, STEPS, step, (start,) * LANES, unroll=8)
    for lane, (state, product) in enumerate(last):
        ends[0, :, lane * 128 : (lane + 1) * 128] = product
        ends[1, :, lane * 128 : (lane + 1) * 128] = state


def gate_kernel(meta, *refs):
    pieces = (refs[0:5], refs[5:10])
    gathered, gated = refs[10:12]
    xa, xb, held, x_sems, w_sems = refs[12:]
    w = meta[0]
    to_held = weight_copies(gathered, held, w_sems)
    to_x = piece_copies(pieces, xa, xb, x_sems)
    for copy in to_held:
        copy.start()
    for copy in to_x:
        copy.start()
    for copy in to_held:
        copy.wait()
    for copy in to_x:
        copy.wait()

    def one(i, carry):
        proj = dot(xa[i], half_of(held, 0, w)) + dot(xb[i], half_of(held, 0, 1 - w))
        gated[i] = jax.nn.gelu(proj)
        return carry

    lax.fori_loop(0, SEQS, one, 0)


def mix_kernel(meta, decays, states, gated, blocks, mixed):
    c, yh, z = meta[1], meta[2], meta[3]
    row = lax.broadcasted_iota(jnp.int32, (SEQS, CH), 0)
    late = jnp.where(row < 4, yh, 1 - yh) == 1
    whole = jnp.zeros((SEQS, CH), F32)
    for k in range(8):
        whole = blocks[k, 0] * whole + blocks[k, 1]
    incoming = jnp.where(late, pltpu.roll(whole, 4, 0), 0.0)
    for k in range(8):
        incoming = jnp.where(k < z, blocks[k, 0] * incoming + blocks[k, 1], incoming)
    for i in range(SEQS):
        block, core, game = i // 4, (i // 2) % 2, i % 2
        at = pl.ds(i, STEPS, stride=SEQS)
        yb = yh if block == 0 else 1 - yh
        cb = c if core == 0 else 1 - c
        target = (yb * 2 + cb) * 2 + game
        for lane in range(LANES):
            cols = slice(lane * 128, (lane + 1) * 128)
            hidden = states[lane, at, :] + decays[lane, at, :] * incoming[i : i + 1, cols]
            mixed[target, :, cols] = (hidden * gated[i, :, cols]).astype(BF16)


def head_kernel(
    meta, own, pair, mixed, wd_own, wd_oth, wp_own, wp_oth, moves, out, feat, down_w, resid, sems
):
    w, c, tm, length, outcome = meta[0], meta[1], meta[4], meta[5], meta[6]
    copies = [
        pltpu.make_async_copy(own.at[w], feat.at[w], sems.at[0]),
        pltpu.make_async_copy(pair.at[w], feat.at[1 - w], sems.at[1]),
    ]
    for k, (src, core) in enumerate(((wd_own, c), (wd_oth, 1 - c))):
        for h in range(2):
            for v in range(2):
                copies.append(
                    pltpu.make_async_copy(
                        src.at[:, h * 2 + v],
                        down_w.at[h, :, core, :, pl.ds(v * HALF, HALF)],
                        sems.at[2 + k * 4 + h * 2 + v],
                    )
                )
    for copy in copies:
        copy.start()
    order = [(h * 2 + k) * 2 + v for v in range(2) for h in range(2) for k in range(2)]
    mix = jnp.concatenate([mixed[j] for j in order], axis=1)
    for copy in copies:
        copy.wait()
    square = jnp.zeros((STEPS, 1), F32)
    width = 512
    for h in range(2):
        for j in range(2):
            rows = down_w[h, j * 16 : (j + 1) * 16].reshape(width, D)
            down = lax.dot_general(
                mix, rows, (((1,), (1,)), ((), ())), preferred_element_type=F32
            )
            at = slice(j * width, (j + 1) * width)
            value = (feat[h, :, at].astype(F32) + down).astype(BF16)
            resid[h, :, at] = value
            wide = value.astype(F32)
            square = square + jnp.sum(wide * wide, axis=1, keepdims=True)
    raw = dot(resid[w], wp_own[...]) + dot(resid[1 - w], wp_oth[...])
    norm = lax.rsqrt(square / D + 1e-06)
    logits = raw * norm
    column = lax.broadcasted_iota(jnp.int32, logits.shape, 1)
    policy = column < MOVES
    top = jnp.max(jnp.where(policy, logits, -jnp.inf), axis=1, keepdims=True)
    total = jnp.sum(jnp.where(policy, jnp.exp(logits - top), 0.0), axis=1, keepdims=True)
    lse = top + jnp.log(total)
    picked = jnp.sum(jnp.where(column == moves[...], logits, 0.0), axis=1, keepdims=True)
    score = jnp.sum(jnp.where(column == MOVES, logits, 0.0), axis=1, keepdims=True)
    value = jnp.tanh(score)
    place = tm * STEPS + lax.broadcasted_iota(jnp.int32, (STEPS, 1), 0)
    loss = jnp.where(place < length, lse - picked + (value - outcome.astype(F32)) ** 2, 0.0)
    lane = lax.broadcasted_iota(jnp.int32, (STEPS, 128), 1)
    both = jnp.where(lane == 0, loss, jnp.where(lane == 1, value, 0.0))
    out[...] = both.T[0:8]


def params():
    return pltpu.CompilerParams(vmem_limit_bytes=VMEM_LIMIT)


def sent_to_all(x, axis):
    length = lax.axis_size(axis)
    return lax.all_to_all(jnp.broadcast_to(x[None], (length, *x.shape)), axis, 0, 0, tiled=True)


def shards(
    moves,
    lengths,
    outcomes,
    embedded,
    w_branches,
    conv_w,
    gate_bias,
    rates,
    w_down,
    w_policy,
    w_value,
):
    yh, z, c, w = (lax.axis_index(a) for a in ("yh", "z", "c", "w"))
    tm = yh * 8 + z
    sel = lambda a: lax.dynamic_index_in_dim(a, w, 0, keepdims=False)
    meta = jnp.stack([w, c, yh, z, tm, sel(lengths), sel(outcomes)]).astype(jnp.int32)

    quarters = w_branches.reshape(4, 16, 4, CH).transpose(2, 0, 1, 3)
    quarters = lax.all_to_all(quarters, ("yh", "c"), 0, 0, tiled=True)
    shard = quarters.reshape(2, 2, 4, 16, CH).transpose(2, 0, 1, 3, 4).reshape(4, 2, 32, CH)
    w_recur = lax.all_gather(shard[1:], ("z", "x"), axis=0)
    w_gate = lax.all_gather(shard[:1], ("z", "x"), axis=0)
    downs = sent_to_all(w_down, ("yh", "w"))
    wd_own = lax.all_gather(downs, ("z", "x"), axis=0)
    wd_oth = lax.ppermute(wd_own, "c", SWAP)

    ring = ("yh", "w")
    own = embedded
    pair = lax.ppermute(own, ring, PAIR)
    other = lax.ppermute(own, ring, OTHER)
    far0 = lax.ppermute(other[0], ring, PAIR)
    far1 = lax.ppermute(pair[1], ring, OTHER)
    mine = (own, pair, other, far0, far1)
    theirs = tuple(lax.ppermute(p, "c", SWAP) for p in mine)

    tail_a = jnp.concatenate(
        [a.reshape(-1, STEPS, HALF)[:, STEPS - TAIL :] for a in (mine[0], theirs[0], mine[3], mine[4], theirs[3], theirs[4])]
    )
    tail_b = jnp.concatenate(
        [a[:, STEPS - TAIL :] for a in (mine[1], theirs[1], mine[2], theirs[2])]
    )
    tail = lax.ppermute(
        jnp.stack([tail_a, tail_b]).reshape(2, 2, 4 * TAIL, HALF), "z", [(k, (k + 1) % 8) for k in range(8)]
    )
    late = jnp.stack([yh, 1 - yh]).reshape(1, 2, 1, 1) == 1
    tail = jnp.where(z > 0, tail, jnp.where(late, tail[:, ::-1], jnp.zeros_like(tail)))
    tail = tail.reshape(2, SEQS * TAIL, HALF)

    q = (yh * 2 + c) * CH
    cut = lambda a: lax.dynamic_slice_in_dim(a, q, CH, a.ndim - 1)
    x_scratch = [
        pltpu.VMEM((SEQS, STEPS, HALF), BF16),
        pltpu.VMEM((SEQS, STEPS, HALF), BF16),
    ]
    decays, states, ends = pl.pallas_call(
        recur_kernel,
        name="recur",
        out_shape=(
            jax.ShapeDtypeStruct((LANES, STEPS * SEQS, 128), F32),
            jax.ShapeDtypeStruct((LANES, STEPS * SEQS, 128), F32),
            jax.ShapeDtypeStruct((2, SEQS, CH), F32),
        ),
        in_specs=[SM] + [ANY] * 11 + [VM] * 5,
        out_specs=(VM, VM, VM),
        scratch_shapes=x_scratch
        + [
            pltpu.VMEM((3, 2, 32, 32, CH), BF16),
            pltpu.VMEM((TAIL + STEPS, CH), F32),
            pltpu.VMEM((SEQS * TAIL, CH), F32),
            pltpu.SemaphoreType.DMA((10,)),
            pltpu.SemaphoreType.DMA((6,)),
        ],
        compiler_params=params(),
        cost_estimate=pl.CostEstimate(
            flops=2 * 2048 * 2048 * 768, bytes_accessed=15 << 20, transcendentals=5 << 19
        ),
    )(meta, *mine, *theirs, w_recur, tail[0], tail[1], cut(conv_w), cut(gate_bias), cut(rates[None]))

    blocks = sent_to_all(ends, "z")
    gated = pl.pallas_call(
        gate_kernel,
        name="gate",
        out_shape=jax.ShapeDtypeStruct((SEQS, STEPS, CH), F32),
        in_specs=[SM] + [ANY] * 11,
        out_specs=VM,
        scratch_shapes=x_scratch
        + [
            pltpu.VMEM((1, 2, 32, 32, CH), BF16),
            pltpu.SemaphoreType.DMA((10,)),
            pltpu.SemaphoreType.DMA((2,)),
        ],
        compiler_params=params(),
        cost_estimate=pl.CostEstimate(
            flops=2 * 2048 * 2048 * 256, bytes_accessed=11 << 20, transcendentals=1 << 19
        ),
    )(meta, *mine, *theirs, w_gate)

    mixed = pl.pallas_call(
        mix_kernel,
        name="mix",
        out_shape=jax.ShapeDtypeStruct((SEQS, STEPS, CH), BF16),
        in_specs=[SM] + [VM] * 4,
        out_specs=VM,
        compiler_params=params(),
        cost_estimate=pl.CostEstimate(flops=4 << 19, bytes_accessed=7 << 20, transcendentals=0),
    )(meta, decays, states, gated, blocks)
    mixed = lax.all_to_all(mixed, ("yh", "c", "w"), 0, 0, tiled=True)

    heads = jnp.concatenate(
        [w_policy, w_value[:, None], jnp.zeros((HALF, COLS - MOVES - 1), BF16)], axis=1
    )
    heads_oth = lax.ppermute(heads, "w", SWAP)
    out = pl.pallas_call(
        head_kernel,
        name="head",
        out_shape=jax.ShapeDtypeStruct((8, STEPS), F32),
        in_specs=[SM, ANY, ANY, VM, ANY, ANY, VM, VM, VM],
        out_specs=VM,
        scratch_shapes=[
            pltpu.VMEM((2, STEPS, HALF), BF16),
            pltpu.VMEM((2, 32, 2, 16, D), BF16),
            pltpu.VMEM((2, STEPS, HALF), BF16),
            pltpu.SemaphoreType.DMA((10,)),
        ],
        compiler_params=params(),
        cost_estimate=pl.CostEstimate(
            flops=2 * 256 * 2048 * 2432, bytes_accessed=12 << 20, transcendentals=1 << 17
        ),
    )(meta, own, pair, mixed, wd_own, wd_oth, heads, heads_oth, sel(moves)[:, None])
    here = out[:2]
    there = lax.ppermute(here, "w", SWAP)
    first = jnp.where(w == 0, here, there)
    second = jnp.where(w == 0, there, here)
    return (jnp.stack([first[0], second[0]]), jnp.stack([first[1], second[1]]))


def solution(mesh):
    fine = Mesh(mesh.devices.reshape(2, 8, 4, 2, 2), ("yh", "z", "x", "c", "w"))
    tm, batch = ("yh", "z"), ("x", "c")
    in_specs = (
        P(batch, tm),
        P(batch),
        P(batch),
        P(batch, tm, "w"),
        P(None, tm + batch, "w"),
        P(None, "w"),
        P(None, "w"),
        P("w"),
        P(tm + batch, "w"),
        P("w", None),
        P("w"),
    )
    out_specs = (P(batch, tm), P(batch, tm))
    return jax.shard_map(
        shards, mesh=fine, in_specs=in_specs, out_specs=out_specs, check_vma=False
    )
```

time: 547 us -> 331 us (0.61)
  local copies, waits for them, and re-layouts: 142 us -> 23.9 us
  other arithmetic: 64 us -> 3.44 us
  Pallas kernels: 0 us -> 41.7 us
  waiting for transfers between devices: 249 us -> 208 us
  matrix products: 22.7 us -> 0 us
  blocking collectives: 37.9 us -> 16.5 us
  starting transfers between devices: 13.3 us -> 23.1 us
    slice x58 -> x10, local copies, waits for them, and re-layouts: 99.8 us -> 4.24 us  [the longest x4 1.53 us: shards(): a[:, STEPS - TAIL:]]
    ppermute x1 -> x13, waiting for transfers between devices: 5.88 us -> 55.4 us  [the longest x1 28 us: shards(): heads_oth = lax.ppermute(heads, 'w', SWAP)]
    pallas_call x0 -> x4, Pallas kernels: none -> 41.7 us  [the longest x1 17.7 us: shards(): pl.pallas_call(recur_kernel, name='recur', out_shape=(jax.ShapeDtypeStruc...]
    all_to_all x1, waiting for transfers between devices: 40.3 us -> 0.01 us  [shards(): mixed = lax.all_to_all(mixed, ('yh', 'c', 'w'), 0, 0, tiled=True)]
    all_gather x1 -> x0, blocking collectives: 37.9 us -> none  [collected_together(): both, at, found = (lax.all_gather(jnp.concatenate(lines), axis), 0, {})]
    all_gather x3, waiting for transfers between devices: 190 us -> 152 us  [the longest x1 57.9 us: shards(): w_recur = lax.all_gather(shard[1:], ('z', 'x'), axis=0)]
    pad x28 -> x0, local copies, waits for them, and re-layouts: 29.1 us -> none  [shards(): summed, local = lax.associative_scan(link, (log_a, drive), axis=1)]
    add x28 -> x0, other arithmetic: 25.2 us -> none  [the longest x13 18.5 us: link(): return (early[0] + late[0], jnp.exp(late[0]) * early[1] + late[1])]
  transfers between devices with their start and end apart: 6 -> 18, of which waited for: 5 -> 8; matrix products, arithmetic and copies ran while one was open for 35% -> 6% of each run, Pallas kernels for 0% -> 10%
where the time goes in v1:
time: 331 us; the launch traced here: 330 us
  waiting for transfers between devices  208 us (63%)
  Pallas kernels  41.7 us (13%)
  local copies, waits for them, and re-layouts  23.9 us (7%)
  starting transfers between devices  23.1 us (7%)
  blocking collectives  16.5 us (5%)
  between operations  14 us (4%)
  other arithmetic  3.44 us (1%)
    all_gather x1, waiting for transfers between devices, shards(): w_recur = lax.all_gather(shard[1:], ('z', 'x'), axis=0)  57.9 us
    all_gather x1, waiting for transfers between devices, shards(): w_gate = lax.all_gather(shard[:1], ('z', 'x'), axis=0)  51.7 us
    all_gather x1, waiting for transfers between devices, shards(): wd_own = lax.all_gather(downs, ('z', 'x'), axis=0)  42.7 us
    ppermute x1, waiting for transfers between devices, shards(): heads_oth = lax.ppermute(heads, 'w', SWAP)  28 us
    ppermute x1, waiting for transfers between devices, shards(): other = lax.ppermute(own, ring, OTHER)  21.1 us
    pallas_call x1, Pallas kernels, shards(): pl.pallas_call(recur_kernel, name='recur', out_shape=(jax.ShapeDtypeStruc...  17.7 us
    pallas_call x1, Pallas kernels, shards(): pl.pallas_call(gate_kernel, name='gate', out_shape=jax.ShapeDtypeStruct((...  9.58 us
    pallas_call x1, Pallas kernels, shards(): pl.pallas_call(head_kernel, name='head', out_shape=jax.ShapeDtypeStruct((...  9.41 us
  transfers between devices with their start and end apart: 18, of which 8 were waited for; matrix products, arithmetic and copies ran while one was open for 6% of the time, Pallas kernels for 10%

profile of v1, /device:TPU:16, one launch (start us, length us, event | category | flops | bytes accessed | tf_op | source)
XLA Modules:
  0.0 330.4 jit_solution(14500878389922795800)
XLA Ops:
  8.0 8.4 %all_to_all.20 = bf16[4,16,1024]{2,1,0:T(8,128)(2,1)} all-to-all(bf16[4,16,1024]{2,1,0:T(8,128)(2,1)S(1)} %broadcast_in_dim.36), channel_id=1, replica_groups=mesh['yh'=2,'z'=8,'x'=4,'c'=2,'w'=2] {'yh','w'}, dimensions={0} | all-to-all | bytes 262144 | tf_op jit(solution)/shard_map/all_to_all | solution.py:232
  17.5 8.1 %all_to_all.21 = bf16[4,4,16,256]{3,2,1,0:T(8,128)(2,1)S(1)} all-to-all(bf16[4,4,16,256]{3,2,1,0:T(8,128)(2,1)S(1)} %copy.23), channel_id=1, replica_groups=mesh['yh'=2,'z'=8,'x'=4,'c'=2,'w'=2] {'yh','c'}, dimensions={0} | all-to-all | bytes 262144 | tf_op jit(solution)/shard_map/all_to_all | solution.py:254
  26.3 2.5 collective-permute-start.1
  28.8 1.9 collective-permute-start
  30.7 21.1 %collective-permute-done.1.refs_2_ = bf16[2,256,1024]{2,1,0:T(8,128)(2,1)S(1)} collective-permute-done((bf16[2,256,1024]{2,1,0:T(8,128)(2,1)}, bf16[2,256,1024]{2,1,0:T(8,128)(2,1)S(1)}, u32[]{:S(2)}, u32[]{:S(2)}) %collective-permute-start.1) | collective-permute-done | bytes 1048608 | tf_op jit(solution)/shard_map/ppermute | solution.py:265
  52.7 2.3 collective-permute-start.2
  56.4 2.0 collective-permute-start.3
  58.3 42.7 %all-gather.9.cloned.1.call-done = bf16[128,16,1024]{2,1,0:T(8,128)(2,1)} async-done(((bf16[4,16,1024]{2,1,0:T(8,128)(2,1)}), bf16[128,16,1024]{2,1,0:T(8,128)(2,1)}) %all-gather.9.cloned.1.call-update) | async-done | bytes 4194320 | tf_op jit(solution)/shard_map/all_gather | solution.py:259
  106.2 3.0 collective-permute-done.7.refs_8_
  110.8 1.9 collective-permute-start.9
  115.4 1.3 dynamic-slice.3
  116.7 1.9 stack.47.meta
  123.0 57.9 %all-gather.5.cloned.1.call-done.refs_10_ = bf16[32,3,2,32,256]{4,3,2,1,0:T(8,128)(2,1)} async-done(((bf16[1,3,2,32,256]{4,3,2,1,0:T(8,128)(2,1)}), bf16[32,3,2,32,256]{4,3,2,1,0:T(8,128)(2,1)}) %all-gather.5.cloned.1.call-update) | async-done | bytes 3145744 | tf_op jit(solution)/shard_map/all_gather | solution.py:256
  180.9 17.7 %recur.1 = (f32[2,2048,128]{2,1,0:T(8,128)}, f32[2,2048,128]{2,1,0:T(8,128)}, f32[2,8,256]{2,1,0:T(8,128)}) custom-call(s32[7]{0:T(128)} %stack.47.meta, bf16[2,256,1024]{2,1,0:T(8,128)(2,1)} %own.1, bf16[2,256,1024]{2,1,0:T(8,128)(2,1)} %copy-done.1, bf16[2,256,1024]{2,1,0:T(8,128)(2,1)} %copy-done.4, bf16[256,1024]{1,0:T(8,128)(2,1)} %collective-permute-done.2.refs_3_, ...), custom_call_target="tpu_custom_call" | custom-call | flops 6442450944 | bytes 15728640 | tf_op jit(solution)/shard_map/recur/pallas_call | solution.py:290
  198.6 1.4 broadcast_in_dim.35
  200.0 4.0 %all-to-all-start.1 = ((f32[8,2,8,256]{3,2,1,0:T(8,128)}), f32[8,2,8,256]{3,2,1,0:T(8,128)S(1)}, u32[]{:S(2)}, u32[]{:S(2)}) async-start(f32[8,2,8,256]{3,2,1,0:T(8,128)} %broadcast_in_dim.35), calls=%async_computation.1 | async-start | bytes 262144 | tf_op jit(solution)/shard_map/all_to_all | solution.py:232
  204.6 51.7 %all-gather.7.cloned.1.call-done.refs_10_ = bf16[32,1,2,32,256]{4,3,2,1,0:T(8,128)(2,1)} async-done(((bf16[1,1,2,32,256]{4,3,2,1,0:T(8,128)(2,1)}), bf16[32,1,2,32,256]{4,3,2,1,0:T(8,128)(2,1)}) %all-gather.7.cloned.1.call-update) | async-done | bytes 1048592 | tf_op jit(solution)/shard_map/all_gather | solution.py:257
  256.3 9.6 %gate.1.gated = f32[8,256,256]{2,1,0:T(8,128)} custom-call(s32[7]{0:T(128)} %stack.47.meta, bf16[2,256,1024]{2,1,0:T(8,128)(2,1)} %own.1, bf16[2,256,1024]{2,1,0:T(8,128)(2,1)} %copy-done.1, bf16[2,256,1024]{2,1,0:T(8,128)(2,1)} %copy-done.4, bf16[256,1024]{1,0:T(8,128)(2,1)} %collective-permute-done.2.refs_3_, ...), custom_call_target="tpu_custom_call" | custom-call | flops 2147483648 | bytes 11534336 | tf_op jit(solution)/shard_map/gate/pallas_call | solution.py:315
  266.6 5.0 %mix.1 = bf16[8,256,256]{2,1,0:T(8,128)(2,1)} custom-call(s32[7]{0:T(128)} %stack.47.meta, f32[2,2048,128]{2,1,0:T(8,128)} %get-tuple-element.5.decays, f32[2,2048,128]{2,1,0:T(8,128)} %get-tuple-element.6.states, f32[8,256,256]{2,1,0:T(8,128)} %gate.1.gated, f32[8,2,8,256]{3,2,1,0:T(8,128)} %copy-done.10), custom_call_target="tpu_custom_call" | custom-call | flops 2097152 | bytes 7340032 | tf_op jit(solution)/shard_map/mix/pallas_call | solution.py:333
  271.6 4.9 %all-to-all-start.2 = ((bf16[8,256,256]{2,1,0:T(8,128)(2,1)}), bf16[8,256,256]{2,1,0:T(8,128)(2,1)S(1)}, u32[]{:S(2)}, u32[]{:S(2)}) async-start(bf16[8,256,256]{2,1,0:T(8,128)(2,1)} %mix.1), calls=%async_computation.2 | async-start | bytes 2097152 | tf_op jit(solution)/shard_map/all_to_all | solution.py:342
  276.8 1.4 collective-permute-start.11
  279.0 28.0 %collective-permute-done.11.wp_oth = bf16[1024,384]{1,0:T(8,128)(2,1)S(1)} collective-permute-done((bf16[1024,384]{1,0:T(8,128)(2,1)S(1)}, bf16[1024,384]{1,0:T(8,128)(2,1)S(1)}, u32[]{:S(2)}, u32[]{:S(2)}) %collective-permute-start.11) | collective-permute-done | bytes 786464 | tf_op jit(solution)/shard_map/ppermute | solution.py:347
  308.3 9.4 %head.1 = f32[8,256]{1,0:T(8,128)} custom-call(s32[7]{0:T(128)} %stack.47.meta, bf16[2,256,1024]{2,1,0:T(8,128)(2,1)} %own.1, bf16[2,256,1024]{2,1,0:T(8,128)(2,1)} %copy-done.1, bf16[8,256,256]{2,1,0:T(8,128)(2,1)} %copy-done.2, bf16[32,4,16,1024]{3,2,1,0:T(8,128)(2,1)} %bitcast.29, bf16[32,4,16,1024]{3,2,1,0:T(8,128)(2,1)} %collective-permute-done.10.wd_oth, ...), custom_call_target="tpu_custom_call" | custom-call | flops 2550136832 | bytes 12582912 | tf_op jit(solution)/shard_map/head/pallas_call | solution.py:348
  319.2 2.7 collective-permute-done.12
  (89 shorter events, 25.7 us)
Async XLA Ops:
  7.2 112.7 %copy-start = (f32[4,1024]{1,0:T(4,128)S(1)}, f32[4,1024]{1,0:T(4,128)}, u32[]{:S(2)}) copy-start(f32[4,1024]{1,0:T(4,128)} %param.16) | copy-start | bytes 49156
  7.2 93.9 %all-gather.9.cloned.1.call-start = ((), (), s32[]{:S(2)}) async-start(), calls=%async_computation.6 | async-start | bytes 4325376 | tf_op jit(solution)/shard_map/all_gather | solution.py:259
  16.4 164.5 %all-gather.5.cloned.1.call-start = ((), (), s32[]{:S(2)}) async-start(), calls=%async_computation.4 | async-start | bytes 3244032 | tf_op jit(solution)/shard_map/all_gather | solution.py:256
  26.2 230.1 %all-gather.7.cloned.1.call-start = ((), (), s32[]{:S(2)}) async-start(), calls=%async_computation.5 | async-start | bytes 1081344 | tf_op jit(solution)/shard_map/all_gather | solution.py:257
  26.3 25.5 %collective-permute-start.1 = (bf16[2,256,1024]{2,1,0:T(8,128)(2,1)}, bf16[2,256,1024]{2,1,0:T(8,128)(2,1)S(1)}, u32[]{:S(2)}, u32[]{:S(2)}) collective-permute-start(bf16[2,256,1024]{2,1,0:T(8,128)(2,1)} %own.1), channel_id=1, source_target_pairs={{0,129},{129,0},{1,128},{128,1},{2,131},{131,2},{3,130},{130,3},{4... | collective-permute-start | bytes 3145736 | tf_op jit(solution)/shard_map/ppermute | solution.py:265
  28.8 26.2 %collective-permute-start = (bf16[2,256,1024]{2,1,0:T(8,128)(2,1)}, bf16[2,256,1024]{2,1,0:T(8,128)(2,1)S(1)}, u32[]{:S(2)}, u32[]{:S(2)}) collective-permute-start(bf16[2,256,1024]{2,1,0:T(8,128)(2,1)} %own.1), channel_id=1, source_target_pairs={{0,1},{1,0},{128,129},{129,128},{2,3},{3,2},{130,131},{131,130},{4... | collective-permute-start | bytes 3145736 | tf_op jit(solution)/shard_map/ppermute | solution.py:264
  30.7 27.6 %collective-permute-start.4 = (bf16[2,256,1024]{2,1,0:T(8,128)(2,1)}, bf16[2,256,1024]{2,1,0:T(8,128)(2,1)S(1)}, u32[]{:S(2)}, u32[]{:S(2)}) collective-permute-start(bf16[2,256,1024]{2,1,0:T(8,128)(2,1)} %own.1), channel_id=1, source_target_pairs={{0,2},{2,0},{1,3},{3,1},{4,6},{6,4},{5,7},{7,5},{8,10},{10,8},{9,1... | collective-permute-start | bytes 3145736 | tf_op jit(solution)/shard_map/ppermute | solution.py:269
  51.8 71.2 %copy-start.4 = (bf16[2,256,1024]{2,1,0:T(8,128)(2,1)}, bf16[2,256,1024]{2,1,0:T(8,128)(2,1)S(1)}, u32[]{:S(2)}) copy-start(bf16[2,256,1024]{2,1,0:T(8,128)(2,1)S(1)} %collective-permute-done.1.refs_2_) | copy-start | bytes 3145732
  52.7 49.8 %collective-permute-start.2 = (bf16[256,1024]{1,0:T(8,128)(2,1)}, bf16[256,1024]{1,0:T(8,128)(2,1)}, u32[]{:S(2)}, u32[]{:S(2)}) collective-permute-start(bf16[256,1024]{1,0:T(8,128)(2,1)} %slice_bitcast_fusion.1), channel_id=1, source_target_pairs={{0,1},{1,0},{128,129},{129,128},{2,3},{3,2},{130,131},{131,130},{4... | collective-permute-start | bytes 1572872 | tf_op jit(solution)/shard_map/ppermute | solution.py:266
  55.0 50.4 %collective-permute-start.6 = (bf16[2,256,1024]{2,1,0:T(8,128)(2,1)S(1)}, bf16[2,256,1024]{2,1,0:T(8,128)(2,1)}, u32[]{:S(2)}, u32[]{:S(2)}) collective-permute-start(bf16[2,256,1024]{2,1,0:T(8,128)(2,1)S(1)} %collective-permute-done.1.refs_2_), channel_id=1, source_target_pairs={{0,2},{2,0},{1,3},{3,1},{4,6},{6,4},{5,7},{7,5},{8,10},{10,8},{9,1... | collective-permute-start | bytes 3145736 | tf_op jit(solution)/shard_map/ppermute | solution.py:269
  55.0 125.9 %copy-start.1 = (bf16[2,256,1024]{2,1,0:T(8,128)(2,1)}, bf16[2,256,1024]{2,1,0:T(8,128)(2,1)S(1)}, u32[]{:S(2)}) copy-start(bf16[2,256,1024]{2,1,0:T(8,128)(2,1)S(1)} %collective-permute-done.refs_1_.pair) | copy-start | bytes 3145732
  55.0 49.6 %collective-permute-start.5 = (bf16[2,256,1024]{2,1,0:T(8,128)(2,1)S(1)}, bf16[2,256,1024]{2,1,0:T(8,128)(2,1)}, u32[]{:S(2)}, u32[]{:S(2)}) collective-permute-start(bf16[2,256,1024]{2,1,0:T(8,128)(2,1)S(1)} %collective-permute-done.refs_1_.pair), channel_id=1, source_target_pairs={{0,2},{2,0},{1,3},{3,1},{4,6},{6,4},{5,7},{7,5},{8,10},{10,8},{9,1... | collective-permute-start | bytes 3145736 | tf_op jit(solution)/shard_map/ppermute | solution.py:269
  56.4 46.7 %collective-permute-start.3 = (bf16[256,1024]{1,0:T(8,128)(2,1)}, bf16[256,1024]{1,0:T(8,128)(2,1)}, u32[]{:S(2)}, u32[]{:S(2)}) collective-permute-start(bf16[256,1024]{1,0:T(8,128)(2,1)} %slice_bitcast_fusion), channel_id=1, source_target_pairs={{0,129},{129,0},{1,128},{128,1},{2,131},{131,2},{3,130},{130,3},{4... | collective-permute-start | bytes 1572872 | tf_op jit(solution)/shard_map/ppermute | solution.py:267
  58.3 122.6 %copy-start.5 = (bf16[2,256,1024]{2,1,0:T(8,128)(2,1)}, bf16[2,256,1024]{2,1,0:T(8,128)(2,1)S(1)}, u32[]{:S(2)}) copy-start(bf16[2,256,1024]{2,1,0:T(8,128)(2,1)S(1)} %collective-permute-done.4.refs_5_) | copy-start | bytes 3145732
  101.1 206.0 %collective-permute-start.10 = (bf16[32,4,16,1024]{3,2,1,0:T(8,128)(2,1)}, bf16[32,4,16,1024]{3,2,1,0:T(8,128)(2,1)}, u32[]{:S(2)}, u32[]{:S(2)}) collective-permute-start(bf16[32,4,16,1024]{3,2,1,0:T(8,128)(2,1)} %bitcast.28), channel_id=1, source_target_pairs={{0,2},{2,0},{1,3},{3,1},{4,6},{6,4},{5,7},{7,5},{8,10},{10,8},{9,1... | collective-permute-start | bytes 12582920 | tf_op jit(solution)/shard_map/ppermute | solution.py:260
  102.5 6.7 %collective-permute-start.7 = (bf16[256,1024]{1,0:T(8,128)(2,1)}, bf16[256,1024]{1,0:T(8,128)(2,1)S(1)}, u32[]{:S(2)}, u32[]{:S(2)}) collective-permute-start(bf16[256,1024]{1,0:T(8,128)(2,1)} %collective-permute-done.2.refs_3_), channel_id=1, source_target_pairs={{0,2},{2,0},{1,3},{3,1},{4,6},{6,4},{5,7},{7,5},{8,10},{10,8},{9,1... | collective-permute-start | bytes 1572872 | tf_op jit(solution)/shard_map/ppermute | solution.py:269
  103.1 6.9 %collective-permute-start.8 = (bf16[256,1024]{1,0:T(8,128)(2,1)}, bf16[256,1024]{1,0:T(8,128)(2,1)S(1)}, u32[]{:S(2)}, u32[]{:S(2)}) collective-permute-start(bf16[256,1024]{1,0:T(8,128)(2,1)} %collective-permute-done.3.refs_4_), channel_id=1, source_target_pairs={{0,2},{2,0},{1,3},{3,1},{4,6},{6,4},{5,7},{7,5},{8,10},{10,8},{9,1... | collective-permute-start | bytes 1572872 | tf_op jit(solution)/shard_map/ppermute | solution.py:269
  110.8 10.3 %collective-permute-start.9 = (bf16[2,2,32,1024]{3,2,1,0:T(8,128)(2,1)S(1)}, bf16[2,2,32,1024]{3,2,1,0:T(8,128)(2,1)}, u32[]{:S(2)}, u32[]{:S(2)}) collective-permute-start(bf16[2,2,32,1024]{3,2,1,0:T(8,128)(2,1)S(1)} %pad_maximum_fusion), channel_id=1, source_target_pairs={{0,16},{16,32},{32,48},{48,64},{64,80},{80,96},{96,112},{112,0},{1... | collective-permute-start | bytes 786440 | tf_op jit(solution)/shard_map/ppermute | solution.py:277
  180.9 23.4 %copy-start.11 = (bf16[1024]{0:T(1024)(128)(2,1)S(1)}, bf16[1024]{0:T(1024)(128)(2,1)}, u32[]{:S(2)}) copy-start(bf16[1024]{0:T(1024)(128)(2,1)} %param.21) | copy-start | bytes 6148
  200.0 65.9 %all-to-all-start.1 = ((f32[8,2,8,256]{3,2,1,0:T(8,128)}), f32[8,2,8,256]{3,2,1,0:T(8,128)S(1)}, u32[]{:S(2)}, u32[]{:S(2)}) async-start(f32[8,2,8,256]{3,2,1,0:T(8,128)} %broadcast_in_dim.35), calls=%async_computation.1 | async-start | bytes 262144 | tf_op jit(solution)/shard_map/all_to_all | solution.py:232
  271.6 35.4 %all-to-all-start.2 = ((bf16[8,256,256]{2,1,0:T(8,128)(2,1)}), bf16[8,256,256]{2,1,0:T(8,128)(2,1)S(1)}, u32[]{:S(2)}, u32[]{:S(2)}) async-start(bf16[8,256,256]{2,1,0:T(8,128)(2,1)} %mix.1), calls=%async_computation.2 | async-start | bytes 2097152 | tf_op jit(solution)/shard_map/all_to_all | solution.py:342
  276.8 30.3 %copy-start.3 = (bf16[1024,384]{1,0:T(8,128)(2,1)}, bf16[1024,384]{1,0:T(8,128)(2,1)S(1)}, u32[]{:S(2)}) copy-start(bf16[1024,384]{1,0:T(8,128)(2,1)S(1)} %maximum_maximum_fusion.wp_own) | copy-start | bytes 2359300
  276.8 30.2 %collective-permute-start.11 = (bf16[1024,384]{1,0:T(8,128)(2,1)S(1)}, bf16[1024,384]{1,0:T(8,128)(2,1)S(1)}, u32[]{:S(2)}, u32[]{:S(2)}) collective-permute-start(bf16[1024,384]{1,0:T(8,128)(2,1)S(1)} %maximum_maximum_fusion.wp_own), channel_id=1, source_target_pairs={{0,1},{1,0},{2,3},{3,2},{4,5},{5,4},{6,7},{7,6},{8,9},{9,8},{10,11... | collective-permute-start | bytes 2359304 | tf_op jit(solution)/shard_map/ppermute | solution.py:347
  318.4 3.6 %collective-permute-start.12 = (f32[2,256]{1,0:T(2,128)S(1)}, f32[2,256]{1,0:T(2,128)S(1)}, u32[]{:S(2)}, u32[]{:S(2)}) collective-permute-start(f32[2,256]{1,0:T(2,128)S(1)} %slice.103), channel_id=1, source_target_pairs={{0,1},{1,0},{2,3},{3,2},{4,5},{5,4},{6,7},{7,6},{8,9},{9,8},{10,11... | collective-permute-start | bytes 6152 | tf_op jit(solution)/shard_map/ppermute | solution.py:366
  (7 other events, 34.1 us)
Sparse Core Ops, SparseCore 0:
  16.5 84.4 all-gather.8
  103.6 77.1 all-gather.4
  183.5 72.7 all-gather.6

commit v2 on v1

v2 whole, which is shorter than its diff:
```python
import jax
import jax.numpy as jnp
from jax import lax
from jax.experimental import pallas as pl
from jax.experimental.pallas import tpu as pltpu
from jax.sharding import Mesh
from jax.sharding import PartitionSpec as P

D = 2048
HALF = 1024
KERNEL = 4
MOVES = 362
COLS = 384
STEPS = 256
HALO = 16
ROWS = HALO + STEPS
CH = 256
LANES = CH // 128
SEQS = 8
VMEM_LIMIT = 56 * 1024 * 1024

F32 = jnp.float32
BF16 = jnp.bfloat16
ANY = pl.BlockSpec(memory_space=pl.ANY)
VM = pl.BlockSpec(memory_space=pltpu.VMEM)
SM = pl.BlockSpec(memory_space=pltpu.SMEM)

PAIR = [(0, 1), (1, 0), (2, 3), (3, 2)]
OTHER = [(0, 3), (3, 0), (1, 2), (2, 1)]
SWAP = [(0, 1), (1, 0)]


def turn(n, k):
    return [(i, (i + k) % n) for i in range(n)]


def dot(a, b):
    return jnp.dot(a, b, preferred_element_type=F32)


def piece_copies(pieces, held, sems, w):
    mine = pl.ds(pl.multiple_of(w * HALF, HALF), HALF)
    theirs = pl.ds(pl.multiple_of((1 - w) * HALF, HALF), HALF)
    groups = []
    for block in range(2):
        for core, (own, pair, other, far0, far1) in enumerate(pieces):
            s = block * 4 + core * 2
            k = (block * 2 + core) * 3
            if block == 0:
                moved = ((own, pl.ds(s, 2), mine), (pair, pl.ds(s, 2), theirs))
            else:
                moved = ((far0, s, mine), (far1, s + 1, mine), (other, pl.ds(s, 2), theirs))
            groups.append(
                [
                    pltpu.make_async_copy(src, held.at[at, :, cols], sems.at[k + n])
                    for n, (src, at, cols) in enumerate(moved)
                ]
            )
    return groups


def weight_copies(pieces, branches, held, z, sems):
    copies = []
    for n, b in enumerate(branches):
        for h in range(2):
            for k, dz in enumerate((0, 7, 6, 5, 1, 2, 3, 4)):
                src = pieces[k].at[h, :, :, b] if k < 7 else pieces[7 + h].at[0, :, :, b]
                to = held.at[n, h, lax.rem(z + dz, 8)]
                copies.append(pltpu.make_async_copy(src, to, sems.at[n, h * 8 + k]))
    return copies


def weights_of(held, n):
    return held[n].reshape(D, CH)


def recur_kernel(meta, *refs):
    pieces = (refs[0:5], refs[5:10])
    conv_w, bias, rates = refs[19:22]
    decays, states, ends = refs[22:25]
    feat, held, ext, x_sems, w_sems = refs[25:]
    w, z, q = meta[0], meta[3], meta[4]
    to_held = weight_copies(refs[10:19], (1, 2, 3), held, z, w_sems)
    groups = piece_copies(pieces, feat, x_sems, w)
    for copy in to_held:
        copy.start()
    for group in groups:
        for copy in group:
            copy.start()
    for copy in to_held:
        copy.wait()
    chans = pl.ds(pl.multiple_of(q * CH, CH), CH)
    taps, biases, rate = conv_w[:, chans], bias[:, chans], rates[:, chans]

    def one(i, carry):
        ext[...] = dot(feat[i], weights_of(held, 0))
        conv = taps[0:1] * ext[HALO:]
        for k in range(1, KERNEL):
            conv = conv + taps[k : k + 1] * ext[HALO - k : HALO - k + STEPS]
        main = feat[i, HALO:]
        recur = jax.nn.sigmoid(dot(main, weights_of(held, 1)) + biases[0:1])
        inflow = jax.nn.sigmoid(dot(main, weights_of(held, 2)) + biases[1:2])
        decay = jnp.exp(-8.0 * recur * rate)
        drive = jnp.sqrt(1.0 - decay * decay) * inflow * conv
        for lane in range(LANES):
            cols = slice(lane * 128, (lane + 1) * 128)
            decays[lane, pl.ds(i, STEPS, stride=SEQS), :] = decay[:, cols]
            states[lane, pl.ds(i, STEPS, stride=SEQS), :] = drive[:, cols]
        return carry

    for n, group in enumerate(groups):
        for copy in group:
            copy.wait()
        lax.fori_loop(n * 2, n * 2 + 2, one, 0)

    def step(t, carry):
        at = pl.ds(pl.multiple_of(t * SEQS, SEQS), SEQS)
        done = []
        for lane, (state, product) in enumerate(carry):
            decay = decays[lane, at]
            state = decay * state + states[lane, at]
            product = product * decay
            states[lane, at] = state
            decays[lane, at] = product
            done.append((state, product))
        return tuple(done)

    start = (jnp.zeros((SEQS, 128), F32), jnp.ones((SEQS, 128), F32))
    last = lax.fori_loop(0, STEPS, step, (start,) * LANES, unroll=8)
    for lane, (state, product) in enumerate(last):
        ends[0, :, lane * 128 : (lane + 1) * 128] = product
        ends[1, :, lane * 128 : (lane + 1) * 128] = state


def gate_kernel(meta, *refs):
    pieces = (refs[0:5], refs[5:10])
    decays, states = refs[19:21]
    scaled, base = refs[22:24]
    feat, held, x_sems, w_sems = refs[24:]
    w, z = meta[0], meta[3]
    to_held = weight_copies(refs[10:19], (0,), held, z, w_sems)
    groups = piece_copies(pieces, feat, x_sems, w)
    for copy in to_held:
        copy.start()
    for group in groups:
        for copy in group:
            copy.start()
    for copy in to_held:
        copy.wait()

    def one(i, carry):
        gated = jax.nn.gelu(dot(feat[i, HALO:], weights_of(held, 0)))
        at = pl.ds(i, STEPS, stride=SEQS)
        for lane in range(LANES):
            cols = slice(lane * 128, (lane + 1) * 128)
            scaled[i, :, cols] = decays[lane, at, :] * gated[:, cols]
            base[i, :, cols] = states[lane, at, :] * gated[:, cols]
        return carry

    for n, group in enumerate(groups):
        for copy in group:
            copy.wait()
        lax.fori_loop(n * 2, n * 2 + 2, one, 0)


def mix_kernel(meta, scaled, base, blocks, mixed):
    c, yh, z = meta[1], meta[2], meta[3]
    row = lax.broadcasted_iota(jnp.int32, (SEQS, CH), 0)
    late = jnp.where(row < 4, yh, 1 - yh) == 1
    whole = jnp.zeros((SEQS, CH), F32)
    for k in range(8):
        whole = blocks[k, 0] * whole + blocks[k, 1]
    incoming = jnp.where(late, pltpu.roll(whole, 4, 0), 0.0)
    for k in range(8):
        incoming = jnp.where(k < z, blocks[k, 0] * incoming + blocks[k, 1], incoming)
    for i in range(SEQS):
        block, core, game = i // 4, (i // 2) % 2, i % 2
        yb = yh if block == 0 else 1 - yh
        cb = c if core == 0 else 1 - c
        mix = base[i] + scaled[i] * incoming[i : i + 1]
        mixed[(yb * 2 + cb) * 2 + game] = mix.astype(BF16)


def head_kernel(
    meta,
    lengths,
    outcomes,
    moves,
    own,
    pair,
    mixed,
    wd_own,
    wd_oth,
    wp_own,
    wp_oth,
    out,
    feat,
    down_w,
    resid,
    f_sems,
    w_sems,
):
    w, c, yh, z = meta[0], meta[1], meta[2], meta[3]
    to_feat = [
        pltpu.make_async_copy(own.at[w], feat.at[w], f_sems.at[0]),
        pltpu.make_async_copy(pair.at[w], feat.at[1 - w], f_sems.at[1]),
    ]
    to_down = []
    for n, rel in enumerate((((0, w), (1, 1 - w)), ((3, w), (2, 1 - w)))):
        h = yh if n == 0 else 1 - yh
        copies = []
        for src, core in ((wd_own, c), (wd_oth, 1 - c)):
            for r, v in rel:
                to = down_w.at[h, :, core, :, pl.ds(pl.multiple_of(v * HALF, HALF), HALF)]
                copies.append(
                    pltpu.make_async_copy(src.at[:, r], to, w_sems.at[n, len(copies)])
                )
        to_down.append(copies)
    for copy in to_feat + to_down[0] + to_down[1]:
        copy.start()
    order = [(h * 2 + k) * 2 + v for v in range(2) for h in range(2) for k in range(2)]
    mix = jnp.concatenate([mixed[j] for j in order], axis=1)
    for copy in to_feat:
        copy.wait()
    square = jnp.zeros((STEPS, 1), F32)
    width = 512
    for n, copies in enumerate(to_down):
        for copy in copies:
            copy.wait()
        h = yh if n == 0 else 1 - yh
        for j in range(2):
            rows = down_w[h, j * 16 : (j + 1) * 16].reshape(width, D)
            down = lax.dot_general(
                mix, rows, (((1,), (1,)), ((), ())), preferred_element_type=F32
            )
            at = slice(j * width, (j + 1) * width)
            value = (feat[h, HALO:, at].astype(F32) + down).astype(BF16)
            resid[h, :, at] = value
            wide = value.astype(F32)
            square = square + jnp.sum(wide * wide, axis=1, keepdims=True)
    raw = dot(resid[w], wp_own[...]) + dot(resid[1 - w], wp_oth[...])
    norm = lax.rsqrt(square / D + 1e-06)
    logits = raw * norm
    column = lax.broadcasted_iota(jnp.int32, logits.shape, 1)
    policy = column < MOVES
    top = jnp.max(jnp.where(policy, logits, -jnp.inf), axis=1, keepdims=True)
    total = jnp.sum(jnp.where(policy, jnp.exp(logits - top), 0.0), axis=1, keepdims=True)
    lse = top + jnp.log(total)
    played = jnp.broadcast_to(moves[pl.ds(w, 1), :].astype(F32), (128, STEPS)).T
    played = jnp.concatenate([played] * (COLS // 128), axis=1).astype(jnp.int32)
    picked = jnp.sum(jnp.where(column == played, logits, 0.0), axis=1, keepdims=True)
    score = jnp.sum(jnp.where(column == MOVES, logits, 0.0), axis=1, keepdims=True)
    value = jnp.tanh(score)
    place = (yh * 8 + z) * STEPS + lax.broadcasted_iota(jnp.int32, (STEPS, 1), 0)
    miss = value - outcomes[w].astype(F32)
    loss = jnp.where(place < lengths[w], lse - picked + miss * miss, 0.0)
    lane = lax.broadcasted_iota(jnp.int32, (STEPS, 128), 1)
    both = jnp.where(lane == 0, loss, jnp.where(lane == 1, value, 0.0))
    out[...] = both.T[0:8]


def params():
    return pltpu.CompilerParams(vmem_limit_bytes=VMEM_LIMIT)


def sent_to_all(x, axis):
    length = lax.axis_size(axis)
    return lax.all_to_all(jnp.broadcast_to(x[None], (length, *x.shape)), axis, 0, 0, tiled=True)


def shards(
    moves,
    lengths,
    outcomes,
    embedded,
    w_branches,
    conv_w,
    gate_bias,
    rates,
    w_down,
    w_policy,
    w_value,
):
    yh, z, c, w = (lax.axis_index(a) for a in ("yh", "z", "c", "w"))
    meta = jnp.stack([w, c, yh, z, yh * 2 + c]).astype(jnp.int32)
    ring = ("yh", "w")
    together = lax.optimization_barrier

    halo = lax.ppermute(embedded[:, STEPS - HALO :], ("yh", "z"), [(k, k + 1) for k in range(15)])
    quarters = w_branches.reshape(4, 16, 2, 2, CH).transpose(2, 3, 0, 1, 4)
    quarters = jnp.broadcast_to(quarters[:, None], (2, 4, 2, 4, 16, CH)).reshape(16, 4, 16, CH)
    rows = lax.all_to_all(quarters, ("yh", "x", "c"), 0, 0, tiled=True)
    halo, rows, part = together((halo, rows, w_down))
    rows = rows.reshape(2, 4, 2, 4, 16, CH)

    own = jnp.concatenate([halo, embedded], axis=1)
    parts = [part] + [lax.ppermute(part, ring, p) for p in (PAIR, OTHER, turn(4, 2))]

    def on_z(up, down):
        return lax.ppermute(up, "z", turn(8, 1)), lax.ppermute(down, "z", turn(8, 7))

    swap = lambda a: lax.ppermute(a, "c", SWAP)
    pair, other = lax.ppermute(own, ring, PAIR), lax.ppermute(own, ring, OTHER)
    up1, down1 = on_z(rows, rows)
    up2, down2 = on_z(up1, down1)
    pair, other, up2, down2, parts, here = together((pair, other, up2, down2, parts, own))
    wd_own = lax.all_gather(jnp.stack(parts), ("z", "x"), axis=0)
    far0 = lax.ppermute(other[0], ring, PAIR)
    far1 = lax.ppermute(pair[1], ring, OTHER)
    own_c = swap(here)
    up3, down3 = on_z(up2, down2)
    far0, far1, own_c, up3, down3, near, late = together((far0, far1, own_c, up3, down3, pair, other))
    low, high = on_z(up3[:1], down3[1:])
    pair_c, other_c = swap(near), swap(late)
    low, high, pair_c, other_c, gone0, gone1 = together((low, high, pair_c, other_c, far0, far1))
    far0_c, far1_c = swap(gone0), swap(gone1)
    mine = (own, pair, other, far0, far1)
    theirs = (own_c, pair_c, other_c, far0_c, far1_c)
    weights = (rows, up1, up2, up3, down1, down2, down3, low, high)

    x_scratch = pltpu.VMEM((SEQS, ROWS, D), BF16)
    decays, states, ends = pl.pallas_call(
        recur_kernel,
        name="recur",
        out_shape=(
            jax.ShapeDtypeStruct((LANES, STEPS * SEQS, 128), F32),
            jax.ShapeDtypeStruct((LANES, STEPS * SEQS, 128), F32),
            jax.ShapeDtypeStruct((2, SEQS, CH), F32),
        ),
        in_specs=[SM] + [ANY] * 19 + [VM] * 3,
        out_specs=(VM, VM, VM),
        scratch_shapes=[
            x_scratch,
            pltpu.VMEM((3, 2, 8, 4, 2, 16, CH), BF16),
            pltpu.VMEM((ROWS, CH), F32),
            pltpu.SemaphoreType.DMA((12,)),
            pltpu.SemaphoreType.DMA((3, 16)),
        ],
        compiler_params=params(),
        cost_estimate=pl.CostEstimate(
            flops=2 * 2048 * 2048 * 768, bytes_accessed=15 << 20, transcendentals=5 << 19
        ),
    )(meta, *mine, *theirs, *weights, conv_w, gate_bias, rates[None])

    heads = jnp.concatenate(
        [w_policy, w_value[:, None], jnp.zeros((HALF, COLS - MOVES - 1), BF16)], axis=1
    )
    heads, _ = lax.optimization_barrier((heads, far0))
    heads_oth = lax.ppermute(heads, "w", SWAP)
    blocks = sent_to_all(ends, "z")
    scaled, base = pl.pallas_call(
        gate_kernel,
        name="gate",
        out_shape=(
            jax.ShapeDtypeStruct((SEQS, STEPS, CH), F32),
            jax.ShapeDtypeStruct((SEQS, STEPS, CH), F32),
        ),
        in_specs=[SM] + [ANY] * 19 + [VM, VM, ANY],
        out_specs=(VM, VM),
        scratch_shapes=[
            x_scratch,
            pltpu.VMEM((1, 2, 8, 4, 2, 16, CH), BF16),
            pltpu.SemaphoreType.DMA((12,)),
            pltpu.SemaphoreType.DMA((1, 16)),
        ],
        compiler_params=params(),
        cost_estimate=pl.CostEstimate(
            flops=2 * 2048 * 2048 * 2048, bytes_accessed=60 << 20, transcendentals=1 << 19
        ),
    )(meta, *mine, *theirs, *weights, decays, states, heads_oth)

    mixed = pl.pallas_call(
        mix_kernel,
        name="mix",
        out_shape=jax.ShapeDtypeStruct((SEQS, STEPS, CH), BF16),
        in_specs=[SM] + [VM] * 3,
        out_specs=VM,
        compiler_params=params(),
        cost_estimate=pl.CostEstimate(flops=4 << 19, bytes_accessed=5 << 20, transcendentals=0),
    )(meta, scaled, base, blocks)
    wd_own, mixed = together((wd_own, mixed))
    mixed = lax.all_to_all(mixed, ("yh", "c", "w"), 0, 0, tiled=True)

    wd_oth = lax.ppermute(wd_own, "c", SWAP)
    out = pl.pallas_call(
        head_kernel,
        name="head",
        out_shape=jax.ShapeDtypeStruct((8, STEPS), F32),
        in_specs=[SM, SM, SM, VM, ANY, ANY, VM, ANY, ANY, VM, VM],
        out_specs=VM,
        scratch_shapes=[
            pltpu.VMEM((2, ROWS, HALF), BF16),
            pltpu.VMEM((2, 32, 2, 16, D), BF16),
            pltpu.VMEM((2, STEPS, HALF), BF16),
            pltpu.SemaphoreType.DMA((2,)),
            pltpu.SemaphoreType.DMA((2, 4)),
        ],
        compiler_params=params(),
        cost_estimate=pl.CostEstimate(
            flops=2 * 256 * 2048 * 2432, bytes_accessed=12 << 20, transcendentals=1 << 17
        ),
    )(meta, lengths, outcomes, moves, own, pair, mixed, wd_own, wd_oth, heads, heads_oth)
    here = out[:2]
    there = lax.ppermute(here, "w", SWAP)
    first = jnp.where(w == 0, here, there)
    second = jnp.where(w == 0, there, here)
    return (jnp.stack([first[0], second[0]]), jnp.stack([first[1], second[1]]))


def solution(mesh):
    fine = Mesh(mesh.devices.reshape(2, 8, 4, 2, 2), ("yh", "z", "x", "c", "w"))
    tm, batch = ("yh", "z"), ("x", "c")
    in_specs = (
        P(batch, tm),
        P(batch),
        P(batch),
        P(batch, tm, "w"),
        P(None, tm + batch, "w"),
        P(None, "w"),
        P(None, "w"),
        P("w"),
        P(tm + batch, "w"),
        P("w", None),
        P("w"),
    )
    out_specs = (P(batch, tm), P(batch, tm))
    return jax.shard_map(
        shards, mesh=fine, in_specs=in_specs, out_specs=out_specs, check_vma=False
    )
```

time: 331 us -> 196 us (0.59)
  waiting for transfers between devices: 208 us -> 50.8 us
  starting transfers between devices: 23.1 us -> 52.1 us
  local copies, waits for them, and re-layouts: 23.9 us -> 13.8 us
    all_gather x3 -> x1, waiting for transfers between devices: 152 us -> 3.66 us  [shards(): wd_own = lax.all_gather(jnp.stack(parts), ('z', 'x'), axis=0)]
    ppermute x1, waiting for transfers between devices: 28 us -> 0.01 us  [shards(): heads_oth = lax.ppermute(heads, 'w', SWAP)]
    ppermute x8 -> x19, starting transfers between devices: 7.54 us -> 31.5 us  [the longest x4 14.7 us: on_z(): lax.ppermute(down, 'z', turn(8, 7))]
    ppermute x8 -> x19, waiting for transfers between devices: 24.7 us -> 45.6 us  [the longest x4 31.5 us: on_z(): lax.ppermute(up, 'z', turn(8, 1))]
    dynamic_slice x4 -> x0, local copies, waits for them, and re-layouts: 4.42 us -> none  [the longest x2 2.57 us: shards(): sel = lambda a: lax.dynamic_index_in_dim(a, w, 0, keepdims=False)]
    slice x8 -> x3, local copies, waits for them, and re-layouts: 3.53 us -> 0.04 us  [the longest x2 0.04 us: shards(): low, high = on_z(up3[:1], down3[1:])]
    unnamed x32 -> x58, local copies, waits for them, and re-layouts: 6.05 us -> 8.66 us
    all_to_all x2 -> x1, blocking collectives: 16.5 us -> 17.9 us  [shards(): mixed = lax.all_to_all(mixed, ('yh', 'c', 'w'), 0, 0, tiled=True)]
  transfers between devices with their start and end apart: 18 -> 27, of which waited for: 8 -> 9; matrix products, arithmetic and copies ran while one was open for 6% -> 2% of each run, Pallas kernels for 10% -> 17%
where the time goes in v2:
time: 196 us; the launch traced here: 194 us
  starting transfers between devices  52.1 us (27%)
  waiting for transfers between devices  50.8 us (26%)
  Pallas kernels  41.8 us (21%)
  blocking collectives  17.9 us (9%)
  between operations  14.4 us (7%)
  local copies, waits for them, and re-layouts  13.8 us (7%)
  other arithmetic  2.81 us (1%)
    ppermute x4, waiting for transfers between devices, on_z(): lax.ppermute(up, 'z', turn(8, 1))  31.5 us
    all_to_all x1, blocking collectives, shards(): mixed = lax.all_to_all(mixed, ('yh', 'c', 'w'), 0, 0, tiled=True)  17.9 us
    pallas_call x1, Pallas kernels, shards(): pl.pallas_call(recur_kernel, name='recur', out_shape=(jax.ShapeDtypeStruc...  17.3 us
    ppermute x4, starting transfers between devices, on_z(): lax.ppermute(down, 'z', turn(8, 7))  14.7 us
    pallas_call x1, Pallas kernels, shards(): pl.pallas_call(gate_kernel, name='gate', out_shape=(jax.ShapeDtypeStruct(...  12.4 us
    unnamed x58, local copies, waits for them, and re-layouts  8.66 us
    pallas_call x1, Pallas kernels, shards(): pl.pallas_call(head_kernel, name='head', out_shape=jax.ShapeDtypeStruct((...  8.54 us
    ppermute x3, waiting for transfers between devices, shards(): lax.ppermute(part, ring, p)  7.47 us
  transfers between devices with their start and end apart: 27, of which 9 were waited for; matrix products, arithmetic and copies ran while one was open for 2% of the time, Pallas kernels for 17%

profile of v2, /device:TPU:16, one launch (start us, length us, event | category | flops | bytes accessed | tf_op | source)
XLA Modules:
  0.0 193.7 jit_solution(17402682634452001089)
XLA Ops:
  9.1 7.3 %all-to-all-start = ((bf16[16,4,16,256]{3,2,1,0:T(8,128)(2,1)}), bf16[16,4,16,256]{3,2,1,0:T(8,128)(2,1)S(1)}, u32[]{:S(2)}, u32[]{:S(2)}) async-start(bf16[16,4,16,256]{3,2,1,0:T(8,128)(2,1)} %bitcast.6), calls=%async_computation | async-start | bytes 1048576 | tf_op jit(solution)/shard_map/all_to_all | solution.py:292
  16.5 3.8 %collective-permute-start = (bf16[2,16,1024]{2,1,0:T(8,128)(2,1)S(1)}, bf16[2,16,1024]{2,1,0:T(8,128)(2,1)S(1)}, u32[]{:S(2)}, u32[]{:S(2)}) collective-permute-start(bf16[2,16,1024]{2,1,0:T(8,128)(2,1)S(1)} %slice.30), channel_id=1, source_target_pairs={{0,16},{16,32},{32,48},{48,64},{64,80},{80,96},{96,112},{112,128},... | collective-permute-start | bytes 196616 | tf_op jit(solution)/shard_map/ppermute | solution.py:289
  20.3 6.6 %collective-permute-done = bf16[2,16,1024]{2,1,0:T(8,128)(2,1)S(1)} collective-permute-done((bf16[2,16,1024]{2,1,0:T(8,128)(2,1)S(1)}, bf16[2,16,1024]{2,1,0:T(8,128)(2,1)S(1)}, u32[]{:S(2)}, u32[]{:S(2)}) %collective-permute-start) | collective-permute-done | bytes 65568 | tf_op jit(solution)/shard_map/ppermute | solution.py:289
  31.5 3.9 %collective-permute-start.5 = (bf16[2,4,2,4,16,256]{5,4,3,2,1,0:T(8,128)(2,1)S(1)}, bf16[2,4,2,4,16,256]{5,4,3,2,1,0:T(8,128)(2,1)S(1)}, u32[]{:S(2)}, u32[]{:S(2)}) collective-permute-start(bf16[2,4,2,4,16,256]{5,4,3,2,1,0:T(8,128)(2,1)S(1)} %bitcast.21), channel_id=1, source_target_pairs={{0,112},{16,0},{32,16},{48,32},{64,48},{80,64},{96,80},{112,96},{1... | collective-permute-start | bytes 1572872 | tf_op jit(solution)/shard_map/ppermute | solution.py:300
  35.5 11.0 %collective-permute-done.3.refs_11_ = bf16[2,4,2,4,16,256]{5,4,3,2,1,0:T(8,128)(2,1)S(1)} collective-permute-done((bf16[2,4,2,4,16,256]{5,4,3,2,1,0:T(8,128)(2,1)S(1)}, bf16[2,4,2,4,16,256]{5,4,3,2,1,0:T(8,128)(2,1)S(1)}, u32[]{:S(2)}, u32[]{:S(2)}) %collective-permute-start.3) | collective-permute-done | bytes 524320 | tf_op jit(solution)/shard_map/ppermute | solution.py:300
  46.5 3.2 %collective-permute-start.6 = (bf16[2,4,2,4,16,256]{5,4,3,2,1,0:T(8,128)(2,1)S(1)}, bf16[2,4,2,4,16,256]{5,4,3,2,1,0:T(8,128)(2,1)S(1)}, u32[]{:S(2)}, u32[]{:S(2)}) collective-permute-start(bf16[2,4,2,4,16,256]{5,4,3,2,1,0:T(8,128)(2,1)S(1)} %collective-permute-done.5.refs_14_), channel_id=1, source_target_pairs={{0,112},{16,0},{32,16},{48,32},{64,48},{80,64},{96,80},{112,96},{1... | collective-permute-start | bytes 1572872 | tf_op jit(solution)/shard_map/ppermute | solution.py:300
  51.0 2.6 %collective-permute-done.7 = bf16[16,1024]{1,0:T(8,128)(2,1)S(1)} collective-permute-done((bf16[16,1024]{1,0:T(8,128)(2,1)S(1)}, bf16[16,1024]{1,0:T(8,128)(2,1)S(1)}, u32[]{:S(2)}, u32[]{:S(2)}) %collective-permute-start.7) | collective-permute-done | bytes 32800 | tf_op jit(solution)/shard_map/ppermute | solution.py:297
  54.9 2.7 %collective-permute-done.8 = bf16[16,1024]{1,0:T(8,128)(2,1)S(1)} collective-permute-done((bf16[16,1024]{1,0:T(8,128)(2,1)S(1)}, bf16[16,1024]{1,0:T(8,128)(2,1)S(1)}, u32[]{:S(2)}, u32[]{:S(2)}) %collective-permute-start.8) | collective-permute-done | bytes 32800 | tf_op jit(solution)/shard_map/ppermute | solution.py:297
  57.5 3.3 %collective-permute-start.9 = (bf16[16,1024]{1,0:T(8,128)(2,1)S(1)}, bf16[16,1024]{1,0:T(8,128)(2,1)S(1)}, u32[]{:S(2)}, u32[]{:S(2)}) collective-permute-start(bf16[16,1024]{1,0:T(8,128)(2,1)S(1)} %copy-done.13), channel_id=1, source_target_pairs={{0,128},{1,129},{128,0},{129,1},{2,130},{3,131},{130,2},{131,3},{4... | collective-permute-start | bytes 98312 | tf_op jit(solution)/shard_map/ppermute | solution.py:297
  60.8 2.2 %collective-permute-done.9 = bf16[16,1024]{1,0:T(8,128)(2,1)S(1)} collective-permute-done((bf16[16,1024]{1,0:T(8,128)(2,1)S(1)}, bf16[16,1024]{1,0:T(8,128)(2,1)S(1)}, u32[]{:S(2)}, u32[]{:S(2)}) %collective-permute-start.9) | collective-permute-done | bytes 32800 | tf_op jit(solution)/shard_map/ppermute | solution.py:297
  66.6 3.3 %collective-permute-start.10 = (bf16[272,1024]{1,0:T(8,128)(2,1)S(1)}, bf16[272,1024]{1,0:T(8,128)(2,1)}, u32[]{:S(2)}, u32[]{:S(2)}) collective-permute-start(bf16[272,1024]{1,0:T(8,128)(2,1)S(1)} %slice_bitcast_fusion.1), channel_id=1, source_target_pairs={{0,1},{1,0},{128,129},{129,128},{2,3},{3,2},{130,131},{131,130},{4... | collective-permute-start | bytes 1671176 | tf_op jit(solution)/shard_map/ppermute | solution.py:308
  71.8 4.0 %collective-permute-start.14 = (bf16[2,4,2,4,16,256]{5,4,3,2,1,0:T(8,128)(2,1)S(1)}, bf16[2,4,2,4,16,256]{5,4,3,2,1,0:T(8,128)(2,1)S(1)}, u32[]{:S(2)}, u32[]{:S(2)}) collective-permute-start(bf16[2,4,2,4,16,256]{5,4,3,2,1,0:T(8,128)(2,1)S(1)} %copy-done.25), channel_id=1, source_target_pairs={{0,112},{16,0},{32,16},{48,32},{64,48},{80,64},{96,80},{112,96},{1... | collective-permute-start | bytes 1572872 | tf_op jit(solution)/shard_map/ppermute | solution.py:300
  75.8 13.0 %collective-permute-done.13.refs_13_ = bf16[2,4,2,4,16,256]{5,4,3,2,1,0:T(8,128)(2,1)S(1)} collective-permute-done((bf16[2,4,2,4,16,256]{5,4,3,2,1,0:T(8,128)(2,1)S(1)}, bf16[2,4,2,4,16,256]{5,4,3,2,1,0:T(8,128)(2,1)S(1)}, u32[]{:S(2)}, u32[]{:S(2)}) %collective-permute-start.13) | collective-permute-done | bytes 524320 | tf_op jit(solution)/shard_map/ppermute | solution.py:300
  90.0 3.5 %collective-permute-start.16 = (bf16[1,4,2,4,16,256]{5,4,3,2,1,0:T(8,128)(2,1)S(1)}, bf16[1,4,2,4,16,256]{5,4,3,2,1,0:T(8,128)(2,1)S(1)}, u32[]{:S(2)}, u32[]{:S(2)}) collective-permute-start(bf16[1,4,2,4,16,256]{5,4,3,2,1,0:T(8,128)(2,1)S(1)} %slice.34), channel_id=1, source_target_pairs={{0,112},{16,0},{32,16},{48,32},{64,48},{80,64},{96,80},{112,96},{1... | collective-permute-start | bytes 786440 | tf_op jit(solution)/shard_map/ppermute | solution.py:300
  93.5 7.6 %collective-permute-done.15.refs_17_ = bf16[1,4,2,4,16,256]{5,4,3,2,1,0:T(8,128)(2,1)S(1)} collective-permute-done((bf16[1,4,2,4,16,256]{5,4,3,2,1,0:T(8,128)(2,1)S(1)}, bf16[1,4,2,4,16,256]{5,4,3,2,1,0:T(8,128)(2,1)S(1)}, u32[]{:S(2)}, u32[]{:S(2)}) %collective-permute-start.15) | collective-permute-done | bytes 262176 | tf_op jit(solution)/shard_map/ppermute | solution.py:300
  106.3 17.3 %recur.1 = (f32[2,2048,128]{2,1,0:T(8,128)}, f32[2,2048,128]{2,1,0:T(8,128)}, f32[2,8,256]{2,1,0:T(8,128)}) custom-call(s32[5]{0:T(128)} %stack.44.meta, bf16[2,272,1024]{2,1,0:T(8,128)(2,1)} %copy-done.3, bf16[2,272,1024]{2,1,0:T(8,128)(2,1)} %copy-done.2, bf16[2,272,1024]{2,1,0:T(8,128)(2,1)} %copy-done.9, ...), custom_call_target="tpu_custom_call" | custom-call | flops 6442450944 | bytes 15728640 | tf_op jit(solution)/shard_map/recur/pallas_call | solution.py:322
  125.0 5.9 %all-to-all-start.1 = ((f32[8,2,8,256]{3,2,1,0:T(8,128)}), f32[8,2,8,256]{3,2,1,0:T(8,128)S(1)}, u32[]{:S(2)}, u32[]{:S(2)}) async-start(f32[8,2,8,256]{3,2,1,0:T(8,128)} %broadcast_in_dim.25), calls=%async_computation.1 | async-start | bytes 262144 | tf_op jit(solution)/shard_map/all_to_all | solution.py:268
  131.8 12.4 %gate.1 = (f32[8,256,256]{2,1,0:T(8,128)}, f32[8,256,256]{2,1,0:T(8,128)}) custom-call(s32[5]{0:T(128)} %stack.44.meta, bf16[2,272,1024]{2,1,0:T(8,128)(2,1)} %copy-done.3, bf16[2,272,1024]{2,1,0:T(8,128)(2,1)} %copy-done.2, bf16[2,272,1024]{2,1,0:T(8,128)(2,1)} %copy-done.9, bf16[272,1024]{1,0:T(8,128)(2,1)} %collective-permute-done.10.refs_3_, ...), custom_call_target="tpu_custom_call" | custom-call | flops 17179869184 | bytes 62914560 | tf_op jit(solution)/shard_map/gate/pallas_call | solution.py:351
  144.9 3.5 %mix.1 = bf16[8,256,256]{2,1,0:T(8,128)(2,1)} custom-call(s32[5]{0:T(128)} %stack.44.meta, f32[8,256,256]{2,1,0:T(8,128)} %get-tuple-element.63.scaled, f32[8,256,256]{2,1,0:T(8,128)} %get-tuple-element.64.base, f32[8,2,8,256]{3,2,1,0:T(8,128)} %copy-done.7), custom_call_target="tpu_custom_call" | custom-call | flops 2097152 | bytes 5242880 | tf_op jit(solution)/shard_map/mix/pallas_call | solution.py:372
  148.4 3.7 %all-gather.3.cloned.1.call-done = bf16[128,16,1024]{2,1,0:T(8,128)(2,1)} async-done(((bf16[4,16,1024]{2,1,0:T(8,128)(2,1)}), bf16[128,16,1024]{2,1,0:T(8,128)(2,1)}) %all-gather.3.cloned.1.call-update) | async-done | bytes 4194320 | tf_op jit(solution)/shard_map/all_gather | solution.py:307
  152.0 17.9 %all_to_all.15.mixed = bf16[8,256,256]{2,1,0:T(8,128)(2,1)} all-to-all(bf16[8,256,256]{2,1,0:T(8,128)(2,1)} %mix.1), channel_id=1, replica_groups=mesh['yh'=2,'z'=8,'x'=4,'c'=2,'w'=2] {'yh','c','w'}, dimensions={0} | all-to-all | bytes 2097152 | tf_op jit(solution)/shard_map/all_to_all | solution.py:382
  169.9 2.0 %copy-done = bf16[32,4,16,1024]{3,2,1,0:T(8,128)(2,1)} copy-done((bf16[32,4,16,1024]{3,2,1,0:T(8,128)(2,1)}, bf16[32,4,16,1024]{3,2,1,0:T(8,128)(2,1)S(1)}, u32[]{:S(2)}) %copy-start) | copy-done | bytes 4194328
  171.9 8.5 %head.1 = f32[8,256]{1,0:T(8,128)} custom-call(s32[5]{0:T(128)} %stack.44.meta, s32[2]{0:T(128)} %lengths.1, s32[2]{0:T(128)} %outcomes.1, s32[2,256]{1,0:T(2,128)} %moves.1, bf16[2,272,1024]{2,1,0:T(8,128)(2,1)} %copy-done.3, bf16[2,272,1024]{2,1,0:T(8,128)(2,1)} %copy-done.2, bf16[8,256,256]{2,1,0:T(8,128)(2,1)} %all_to_all.15.mixed, ...), custom_call_target="tpu_custom_call" | custom-call | flops 2550136832 | bytes 12582912 | tf_op jit(solution)/shard_map/head/pallas_call | solution.py:385
  181.2 2.2 %collective-permute-start.23 = (f32[2,256]{1,0:T(2,128)S(1)}, f32[2,256]{1,0:T(2,128)S(1)}, u32[]{:S(2)}, u32[]{:S(2)}) collective-permute-start(f32[2,256]{1,0:T(2,128)S(1)} %slice.40), channel_id=1, source_target_pairs={{0,1},{1,0},{2,3},{3,2},{4,5},{5,4},{6,7},{7,6},{8,9},{9,8},{10,11... | collective-permute-start | bytes 6152 | tf_op jit(solution)/shard_map/ppermute | solution.py:404
  (115 shorter events, 28.0 us)
Async XLA Ops:
  9.1 17.8 %all-to-all-start = ((bf16[16,4,16,256]{3,2,1,0:T(8,128)(2,1)}), bf16[16,4,16,256]{3,2,1,0:T(8,128)(2,1)S(1)}, u32[]{:S(2)}, u32[]{:S(2)}) async-start(bf16[16,4,16,256]{3,2,1,0:T(8,128)(2,1)} %bitcast.6), calls=%async_computation | async-start | bytes 1048576 | tf_op jit(solution)/shard_map/all_to_all | solution.py:292
  16.4 135.6 %all-gather.3.cloned.1.call-start = ((), (), s32[]{:S(2)}) async-start(), calls=%async_computation.3 | async-start | bytes 4325376 | tf_op jit(solution)/shard_map/all_gather | solution.py:307
  16.5 10.4 %collective-permute-start = (bf16[2,16,1024]{2,1,0:T(8,128)(2,1)S(1)}, bf16[2,16,1024]{2,1,0:T(8,128)(2,1)S(1)}, u32[]{:S(2)}, u32[]{:S(2)}) collective-permute-start(bf16[2,16,1024]{2,1,0:T(8,128)(2,1)S(1)} %slice.30), channel_id=1, source_target_pairs={{0,16},{16,32},{32,48},{48,64},{64,80},{80,96},{96,112},{112,128},... | collective-permute-start | bytes 196616 | tf_op jit(solution)/shard_map/ppermute | solution.py:289
  27.0 36.0 %collective-permute-start.1 = (bf16[2,272,1024]{2,1,0:T(8,128)(2,1)S(1)}, bf16[2,272,1024]{2,1,0:T(8,128)(2,1)S(1)}, u32[]{:S(2)}, u32[]{:S(2)}) collective-permute-start(bf16[2,272,1024]{2,1,0:T(8,128)(2,1)S(1)} %constant_dynamic-update-slice_fusion.refs_0_.own), channel_id=1, source_target_pairs={{0,1},{1,0},{128,129},{129,128},{2,3},{3,2},{130,131},{131,130},{4... | collective-permute-start | bytes 3342344 | tf_op jit(solution)/shard_map/ppermute | solution.py:303
  28.4 34.6 %collective-permute-start.2 = (bf16[2,272,1024]{2,1,0:T(8,128)(2,1)S(1)}, bf16[2,272,1024]{2,1,0:T(8,128)(2,1)S(1)}, u32[]{:S(2)}, u32[]{:S(2)}) collective-permute-start(bf16[2,272,1024]{2,1,0:T(8,128)(2,1)S(1)} %constant_dynamic-update-slice_fusion.refs_0_.own), channel_id=1, source_target_pairs={{0,129},{129,0},{1,128},{128,1},{2,131},{131,2},{3,130},{130,3},{4... | collective-permute-start | bytes 3342344 | tf_op jit(solution)/shard_map/ppermute | solution.py:303
  29.6 16.8 %collective-permute-start.3 = (bf16[2,4,2,4,16,256]{5,4,3,2,1,0:T(8,128)(2,1)S(1)}, bf16[2,4,2,4,16,256]{5,4,3,2,1,0:T(8,128)(2,1)S(1)}, u32[]{:S(2)}, u32[]{:S(2)}) collective-permute-start(bf16[2,4,2,4,16,256]{5,4,3,2,1,0:T(8,128)(2,1)S(1)} %bitcast.20), channel_id=1, source_target_pairs={{0,16},{16,32},{32,48},{48,64},{64,80},{80,96},{96,112},{112,0},{1... | collective-permute-start | bytes 1572872 | tf_op jit(solution)/shard_map/ppermute | solution.py:300
  31.5 14.9 %collective-permute-start.5 = (bf16[2,4,2,4,16,256]{5,4,3,2,1,0:T(8,128)(2,1)S(1)}, bf16[2,4,2,4,16,256]{5,4,3,2,1,0:T(8,128)(2,1)S(1)}, u32[]{:S(2)}, u32[]{:S(2)}) collective-permute-start(bf16[2,4,2,4,16,256]{5,4,3,2,1,0:T(8,128)(2,1)S(1)} %bitcast.21), channel_id=1, source_target_pairs={{0,112},{16,0},{32,16},{48,32},{64,48},{80,64},{96,80},{112,96},{1... | collective-permute-start | bytes 1572872 | tf_op jit(solution)/shard_map/ppermute | solution.py:300
  46.4 16.5 %collective-permute-start.4 = (bf16[2,4,2,4,16,256]{5,4,3,2,1,0:T(8,128)(2,1)S(1)}, bf16[2,4,2,4,16,256]{5,4,3,2,1,0:T(8,128)(2,1)S(1)}, u32[]{:S(2)}, u32[]{:S(2)}) collective-permute-start(bf16[2,4,2,4,16,256]{5,4,3,2,1,0:T(8,128)(2,1)S(1)} %collective-permute-done.3.refs_11_), channel_id=1, source_target_pairs={{0,16},{16,32},{32,48},{48,64},{64,80},{80,96},{96,112},{112,0},{1... | collective-permute-start | bytes 1572872 | tf_op jit(solution)/shard_map/ppermute | solution.py:300
  46.5 16.5 %collective-permute-start.6 = (bf16[2,4,2,4,16,256]{5,4,3,2,1,0:T(8,128)(2,1)S(1)}, bf16[2,4,2,4,16,256]{5,4,3,2,1,0:T(8,128)(2,1)S(1)}, u32[]{:S(2)}, u32[]{:S(2)}) collective-permute-start(bf16[2,4,2,4,16,256]{5,4,3,2,1,0:T(8,128)(2,1)S(1)} %collective-permute-done.5.refs_14_), channel_id=1, source_target_pairs={{0,112},{16,0},{32,16},{48,32},{64,48},{80,64},{96,80},{112,96},{1... | collective-permute-start | bytes 1572872 | tf_op jit(solution)/shard_map/ppermute | solution.py:300
  49.7 3.9 %collective-permute-start.7 = (bf16[16,1024]{1,0:T(8,128)(2,1)S(1)}, bf16[16,1024]{1,0:T(8,128)(2,1)S(1)}, u32[]{:S(2)}, u32[]{:S(2)}) collective-permute-start(bf16[16,1024]{1,0:T(8,128)(2,1)S(1)} %copy-done.13), channel_id=1, source_target_pairs={{0,1},{1,0},{128,129},{129,128},{2,3},{3,2},{130,131},{131,130},{4... | collective-permute-start | bytes 98312 | tf_op jit(solution)/shard_map/ppermute | solution.py:297
  53.6 3.9 %collective-permute-start.8 = (bf16[16,1024]{1,0:T(8,128)(2,1)S(1)}, bf16[16,1024]{1,0:T(8,128)(2,1)S(1)}, u32[]{:S(2)}, u32[]{:S(2)}) collective-permute-start(bf16[16,1024]{1,0:T(8,128)(2,1)S(1)} %copy-done.13), channel_id=1, source_target_pairs={{0,129},{129,0},{1,128},{128,1},{2,131},{131,2},{3,130},{130,3},{4... | collective-permute-start | bytes 98312 | tf_op jit(solution)/shard_map/ppermute | solution.py:297
  57.5 5.4 %collective-permute-start.9 = (bf16[16,1024]{1,0:T(8,128)(2,1)S(1)}, bf16[16,1024]{1,0:T(8,128)(2,1)S(1)}, u32[]{:S(2)}, u32[]{:S(2)}) collective-permute-start(bf16[16,1024]{1,0:T(8,128)(2,1)S(1)} %copy-done.13), channel_id=1, source_target_pairs={{0,128},{1,129},{128,0},{129,1},{2,130},{3,131},{130,2},{131,3},{4... | collective-permute-start | bytes 98312 | tf_op jit(solution)/shard_map/ppermute | solution.py:297
  65.0 23.8 %collective-permute-start.12 = (bf16[2,272,1024]{2,1,0:T(8,128)(2,1)S(1)}, bf16[2,272,1024]{2,1,0:T(8,128)(2,1)S(1)}, u32[]{:S(2)}, u32[]{:S(2)}) collective-permute-start(bf16[2,272,1024]{2,1,0:T(8,128)(2,1)S(1)} %constant_dynamic-update-slice_fusion.refs_0_.own), channel_id=1, source_target_pairs={{0,2},{2,0},{1,3},{3,1},{4,6},{6,4},{5,7},{7,5},{8,10},{10,8},{9,1... | collective-permute-start | bytes 3342344 | tf_op jit(solution)/shard_map/ppermute | solution.py:302
  65.2 23.6 %collective-permute-start.11 = (bf16[272,1024]{1,0:T(8,128)(2,1)S(1)}, bf16[272,1024]{1,0:T(8,128)(2,1)S(1)}, u32[]{:S(2)}, u32[]{:S(2)}) collective-permute-start(bf16[272,1024]{1,0:T(8,128)(2,1)S(1)} %slice_bitcast_fusion), channel_id=1, source_target_pairs={{0,129},{129,0},{1,128},{128,1},{2,131},{131,2},{3,130},{130,3},{4... | collective-permute-start | bytes 1671176 | tf_op jit(solution)/shard_map/ppermute | solution.py:309
  66.6 22.2 %collective-permute-start.10 = (bf16[272,1024]{1,0:T(8,128)(2,1)S(1)}, bf16[272,1024]{1,0:T(8,128)(2,1)}, u32[]{:S(2)}, u32[]{:S(2)}) collective-permute-start(bf16[272,1024]{1,0:T(8,128)(2,1)S(1)} %slice_bitcast_fusion.1), channel_id=1, source_target_pairs={{0,1},{1,0},{128,129},{129,128},{2,3},{3,2},{130,131},{131,130},{4... | collective-permute-start | bytes 1671176 | tf_op jit(solution)/shard_map/ppermute | solution.py:308
  69.8 18.9 %collective-permute-start.13 = (bf16[2,4,2,4,16,256]{5,4,3,2,1,0:T(8,128)(2,1)S(1)}, bf16[2,4,2,4,16,256]{5,4,3,2,1,0:T(8,128)(2,1)S(1)}, u32[]{:S(2)}, u32[]{:S(2)}) collective-permute-start(bf16[2,4,2,4,16,256]{5,4,3,2,1,0:T(8,128)(2,1)S(1)} %copy-done.23), channel_id=1, source_target_pairs={{0,16},{16,32},{32,48},{48,64},{64,80},{80,96},{96,112},{112,0},{1... | collective-permute-start | bytes 1572872 | tf_op jit(solution)/shard_map/ppermute | solution.py:300
  71.8 17.0 %collective-permute-start.14 = (bf16[2,4,2,4,16,256]{5,4,3,2,1,0:T(8,128)(2,1)S(1)}, bf16[2,4,2,4,16,256]{5,4,3,2,1,0:T(8,128)(2,1)S(1)}, u32[]{:S(2)}, u32[]{:S(2)}) collective-permute-start(bf16[2,4,2,4,16,256]{5,4,3,2,1,0:T(8,128)(2,1)S(1)} %copy-done.25), channel_id=1, source_target_pairs={{0,112},{16,0},{32,16},{48,32},{64,48},{80,64},{96,80},{112,96},{1... | collective-permute-start | bytes 1572872 | tf_op jit(solution)/shard_map/ppermute | solution.py:300
  88.8 12.2 %collective-permute-start.17 = (bf16[2,272,1024]{2,1,0:T(8,128)(2,1)S(1)}, bf16[2,272,1024]{2,1,0:T(8,128)(2,1)S(1)}, u32[]{:S(2)}, u32[]{:S(2)}) collective-permute-start(bf16[2,272,1024]{2,1,0:T(8,128)(2,1)S(1)} %collective-permute-done.1.refs_1_.pair), channel_id=1, source_target_pairs={{0,2},{2,0},{1,3},{3,1},{4,6},{6,4},{5,7},{7,5},{8,10},{10,8},{9,1... | collective-permute-start | bytes 3342344 | tf_op jit(solution)/shard_map/ppermute | solution.py:302
  88.9 13.0 %collective-permute-start.18 = (bf16[2,272,1024]{2,1,0:T(8,128)(2,1)S(1)}, bf16[2,272,1024]{2,1,0:T(8,128)(2,1)S(1)}, u32[]{:S(2)}, u32[]{:S(2)}) collective-permute-start(bf16[2,272,1024]{2,1,0:T(8,128)(2,1)S(1)} %copy-done.10), channel_id=1, source_target_pairs={{0,2},{2,0},{1,3},{3,1},{4,6},{6,4},{5,7},{7,5},{8,10},{10,8},{9,1... | collective-permute-start | bytes 3342344 | tf_op jit(solution)/shard_map/ppermute | solution.py:302
  90.0 11.1 %collective-permute-start.15 = (bf16[1,4,2,4,16,256]{5,4,3,2,1,0:T(8,128)(2,1)S(1)}, bf16[1,4,2,4,16,256]{5,4,3,2,1,0:T(8,128)(2,1)S(1)}, u32[]{:S(2)}, u32[]{:S(2)}) collective-permute-start(bf16[1,4,2,4,16,256]{5,4,3,2,1,0:T(8,128)(2,1)S(1)} %slice.33), channel_id=1, source_target_pairs={{0,16},{16,32},{32,48},{48,64},{64,80},{80,96},{96,112},{112,0},{1... | collective-permute-start | bytes 786440 | tf_op jit(solution)/shard_map/ppermute | solution.py:300
  90.0 11.1 %collective-permute-start.16 = (bf16[1,4,2,4,16,256]{5,4,3,2,1,0:T(8,128)(2,1)S(1)}, bf16[1,4,2,4,16,256]{5,4,3,2,1,0:T(8,128)(2,1)S(1)}, u32[]{:S(2)}, u32[]{:S(2)}) collective-permute-start(bf16[1,4,2,4,16,256]{5,4,3,2,1,0:T(8,128)(2,1)S(1)} %slice.34), channel_id=1, source_target_pairs={{0,112},{16,0},{32,16},{48,32},{64,48},{80,64},{96,80},{112,96},{1... | collective-permute-start | bytes 786440 | tf_op jit(solution)/shard_map/ppermute | solution.py:300
  104.2 26.7 %collective-permute-start.21 = (bf16[1024,384]{1,0:T(8,128)(2,1)S(1)}, bf16[1024,384]{1,0:T(8,128)(2,1)S(1)}, u32[]{:S(2)}, u32[]{:S(2)}) collective-permute-start(bf16[1024,384]{1,0:T(8,128)(2,1)S(1)} %maximum_maximum_fusion.wp_own), channel_id=1, source_target_pairs={{0,1},{1,0},{2,3},{3,2},{4,5},{5,4},{6,7},{7,6},{8,9},{9,8},{10,11... | collective-permute-start | bytes 2359304 | tf_op jit(solution)/shard_map/ppermute | solution.py:349
  125.0 19.2 %all-to-all-start.1 = ((f32[8,2,8,256]{3,2,1,0:T(8,128)}), f32[8,2,8,256]{3,2,1,0:T(8,128)S(1)}, u32[]{:S(2)}, u32[]{:S(2)}) async-start(f32[8,2,8,256]{3,2,1,0:T(8,128)} %broadcast_in_dim.25), calls=%async_computation.1 | async-start | bytes 262144 | tf_op jit(solution)/shard_map/all_to_all | solution.py:268
  152.0 17.9 %collective-permute-start.22 = (bf16[32,4,16,1024]{3,2,1,0:T(8,128)(2,1)}, bf16[32,4,16,1024]{3,2,1,0:T(8,128)(2,1)S(1)}, u32[]{:S(2)}, u32[]{:S(2)}) collective-permute-start(bf16[32,4,16,1024]{3,2,1,0:T(8,128)(2,1)} %bitcast.18), channel_id=1, source_target_pairs={{0,2},{2,0},{1,3},{3,1},{4,6},{6,4},{5,7},{7,5},{8,10},{10,8},{9,1... | collective-permute-start | bytes 12582920 | tf_op jit(solution)/shard_map/ppermute | solution.py:384
  (31 other events, 297.8 us)
Sparse Core Ops, SparseCore 0:
  65.1 86.8 all-gather.2

commit v3 on v2

v3 whole, which is shorter than its diff:
```python
import jax
import jax.numpy as jnp
from jax import lax
from jax.experimental import pallas as pl
from jax.experimental.pallas import tpu as pltpu
from jax.sharding import Mesh
from jax.sharding import PartitionSpec as P

D = 2048
HALF = 1024
KERNEL = 4
MOVES = 362
COLS = 384
STEPS = 256
HALO = 16
ROWS = HALO + STEPS
CH = 256
LANES = CH // 128
SEQS = 8
VMEM_LIMIT = 56 * 1024 * 1024

F32 = jnp.float32
BF16 = jnp.bfloat16
ANY = pl.BlockSpec(memory_space=pl.ANY)
VM = pl.BlockSpec(memory_space=pltpu.VMEM)
SM = pl.BlockSpec(memory_space=pltpu.SMEM)

PAIR = [(0, 1), (1, 0), (2, 3), (3, 2)]
OTHER = [(0, 3), (3, 0), (1, 2), (2, 1)]
SWAP = [(0, 1), (1, 0)]


def turn(n, k):
    return [(i, (i + k) % n) for i in range(n)]


def dot(a, b):
    return jnp.dot(a, b, preferred_element_type=F32)


def piece_copies(pieces, held, sems, w):
    mine = pl.ds(pl.multiple_of(w * HALF, HALF), HALF)
    theirs = pl.ds(pl.multiple_of((1 - w) * HALF, HALF), HALF)
    groups = []
    for block in range(2):
        for core, (own, pair, other, far0, far1) in enumerate(pieces):
            s = block * 4 + core * 2
            k = (block * 2 + core) * 3
            if block == 0:
                moved = ((own, pl.ds(s, 2), mine), (pair, pl.ds(s, 2), theirs))
            else:
                moved = ((far0, s, mine), (far1, s + 1, mine), (other, pl.ds(s, 2), theirs))
            groups.append(
                [
                    pltpu.make_async_copy(src, held.at[at, :, cols], sems.at[k + n])
                    for n, (src, at, cols) in enumerate(moved)
                ]
            )
    return groups


def weight_copies(pieces, first, held, x, sems):
    some = pl.ds(first, held.shape[4])
    copies = []
    for k, dx in enumerate((0, 3, 1)):
        to = held.at[:, :, lax.rem(x + dx, 4)]
        copies.append(pltpu.make_async_copy(pieces[k].at[:, :, :, some], to, sems.at[k]))
    for h in range(2):
        to = held.at[h, :, lax.rem(x + 2, 4)]
        src = pieces[3 + h].at[0, :, :, some]
        copies.append(pltpu.make_async_copy(src, to, sems.at[3 + h]))
    return copies


def weights_of(held, n):
    return held[:, :, :, :, n].reshape(D, CH)


def start(copies):
    for copy in copies:
        copy.start()


def wait(copies):
    for copy in copies:
        copy.wait()


def recur_kernel(meta, *refs):
    pieces = (refs[0:5], refs[5:10])
    conv_w, bias, rates = refs[15:18]
    decays_out, states_out, ends = refs[18:21]
    feat, held, exts, decays, states, x_sems, w_sems, out_sems = refs[21:]
    w, x, q = meta[0], meta[4], meta[2] * 2 + meta[1]
    to_held = weight_copies(refs[10:15], 1, held, x, w_sems)
    groups = piece_copies(pieces, feat, x_sems, w)
    start(groups[0] + to_held)
    start(groups[1] + groups[2] + groups[3])
    chans = pl.ds(pl.multiple_of(q * CH, CH), CH)
    taps, biases, rate = conv_w[:, chans], bias[:, chans], rates[:, chans]

    def one(i):
        ext = exts.at[i % 2]
        ext[...] = dot(feat[i], weights_of(held, 0))
        conv = taps[0:1] * ext[HALO:]
        for k in range(1, KERNEL):
            conv = conv + taps[k : k + 1] * ext[HALO - k : HALO - k + STEPS]
        main = feat[i, HALO:]
        recur = jax.nn.sigmoid(dot(main, weights_of(held, 1)) + biases[0:1])
        inflow = jax.nn.sigmoid(dot(main, weights_of(held, 2)) + biases[1:2])
        decay = jnp.exp(-8.0 * recur * rate)
        drive = jnp.sqrt(1.0 - decay * decay) * inflow * conv
        for lane in range(LANES):
            cols = slice(lane * 128, (lane + 1) * 128)
            decays[lane, pl.ds(i, STEPS, stride=SEQS), :] = decay[:, cols]
            states[lane, pl.ds(i, STEPS, stride=SEQS), :] = drive[:, cols]

    wait(to_held)
    for n, group in enumerate(groups):
        wait(group)
        one(n * 2)
        one(n * 2 + 1)

    def step(t, carry):
        at = pl.ds(pl.multiple_of(t * SEQS, SEQS), SEQS)
        done = []
        for lane, (state, product) in enumerate(carry):
            decay = decays[lane, at]
            state = decay * state + states[lane, at]
            product = product * decay
            states[lane, at] = state
            decays[lane, at] = product
            done.append((state, product))
        return tuple(done)

    last = ((jnp.zeros((SEQS, 128), F32), jnp.ones((SEQS, 128), F32)),) * LANES
    to_out = []
    for k in range(4):
        last = lax.fori_loop(k * STEPS // 4, (k + 1) * STEPS // 4, step, last, unroll=8)
        at = pl.ds(k * STEPS * SEQS // 4, STEPS * SEQS // 4)
        moved = [
            pltpu.make_async_copy(src.at[:, at], to.at[:, at], out_sems.at[k * 2 + n])
            for n, (src, to) in enumerate(((decays, decays_out), (states, states_out)))
        ]
        start(moved)
        to_out += moved
    for lane, (state, product) in enumerate(last):
        for k in range(8):
            ends[k, 0, :, lane * 128 : (lane + 1) * 128] = product
            ends[k, 1, :, lane * 128 : (lane + 1) * 128] = state
    wait(to_out)


def gate_kernel(meta, *refs):
    pieces = (refs[0:5], refs[5:10])
    decays_in, states_in = refs[15:17]
    out = refs[18]
    feat, held, decays, states, both, x_sems, w_sems, in_sems, out_sems = refs[19:]
    w, x = meta[0], meta[4]
    to_held = weight_copies(refs[10:15], 0, held, x, w_sems)
    groups = piece_copies(pieces, feat, x_sems, w)
    to_in = [
        pltpu.make_async_copy(decays_in, decays, in_sems.at[0]),
        pltpu.make_async_copy(states_in, states, in_sems.at[1]),
    ]
    start(groups[0] + to_held + to_in)
    start(groups[1] + groups[2] + groups[3])

    def moved(i):
        return pltpu.make_async_copy(both.at[i], out.at[i], out_sems.at[i])

    def one(i, carry):
        gated = jax.nn.gelu(dot(feat[i, HALO:], weights_of(held, 0)))
        at = pl.ds(i, STEPS, stride=SEQS)
        for lane in range(LANES):
            cols = slice(lane * 128, (lane + 1) * 128)
            both[i, 0, :, cols] = decays[lane, at, :] * gated[:, cols]
            both[i, 1, :, cols] = states[lane, at, :] * gated[:, cols]
        moved(i).start()
        return carry

    wait(to_held)
    for n, group in enumerate(groups):
        wait(group)
        if n == 0:
            wait(to_in)
        lax.fori_loop(n * 2, n * 2 + 2, one, 0)
    wait([moved(i) for i in range(SEQS)])


def mix_kernel(meta, gated, blocks, out, both, mixed, in_sems, out_sems):
    c, yh, z = meta[1], meta[2], meta[3]
    to_both = [
        pltpu.make_async_copy(gated.at[i], both.at[i], in_sems.at[i]) for i in range(SEQS)
    ]
    start(to_both)
    row = lax.broadcasted_iota(jnp.int32, (SEQS, CH), 0)
    late = jnp.where(row < 4, yh, 1 - yh) == 1
    whole = jnp.zeros((SEQS, CH), F32)
    for k in range(8):
        whole = blocks[k, 0] * whole + blocks[k, 1]
    incoming = jnp.where(late, pltpu.roll(whole, 4, 0), 0.0)
    for k in range(8):
        incoming = jnp.where(k < z, blocks[k, 0] * incoming + blocks[k, 1], incoming)
    to_out = []
    for i in range(SEQS):
        block, core, game = i // 4, (i // 2) % 2, i % 2
        yb = yh if block == 0 else 1 - yh
        cb = c if core == 0 else 1 - c
        to_both[i].wait()
        mixed[i] = (both[i, 1] + both[i, 0] * incoming[i : i + 1]).astype(BF16)
        to = out.at[(yb * 2 + cb) * 2 + game]
        to_out.append(pltpu.make_async_copy(mixed.at[i], to, out_sems.at[i]))
        to_out[i].start()
    wait(to_out)


def down_copies(pieces, down_w, w, c, yh, x, sems):
    column, beside, beside_c, across, across_c = pieces
    gathered = (
        (column, 0, 0),
        (beside, 3 - 2 * c, 0),
        (beside_c, 1 + 2 * c, 0),
        (across, 2, 4 * c),
        (across_c, 2, 4 - 4 * c),
    )
    groups = []
    for n, (h, rel) in enumerate(((yh, ((0, w), (1, 1 - w))), (1 - yh, ((3, w), (2, 1 - w))))):
        copies = []
        for r, v in rel:
            at = pl.ds(pl.multiple_of(v * HALF, HALF), HALF)
            for src, dx, first in gathered:
                to = down_w.at[h, pl.ds(first, src.shape[0]), lax.rem(x + dx, 4), :, :, at]
                sem = sems.at[n, len(copies)]
                copies.append(pltpu.make_async_copy(src.at[:, :, r], to, sem))
        groups.append(copies)
    return groups


def head_kernel(
    meta,
    lengths,
    outcomes,
    moves,
    own,
    pair,
    mixed,
    column,
    beside,
    beside_c,
    across,
    across_c,
    heads,
    heads_oth,
    out,
    feat,
    mix,
    down_w,
    resid,
    wp,
    f_sems,
    m_sems,
    d_sems,
):
    w, c, yh, z, x = meta[0], meta[1], meta[2], meta[3], meta[4]
    to_mix = []
    for j in range(SEQS):
        to = mix.at[:, pl.ds((j % 2) * HALF + (j // 2) * CH, CH)]
        to_mix.append(pltpu.make_async_copy(mixed.at[j], to, m_sems.at[j]))
    pieces = (column, beside, beside_c, across, across_c)
    to_down = down_copies(pieces, down_w, w, c, yh, x, d_sems)
    to_feat = [
        pltpu.make_async_copy(own.at[w], feat.at[w], f_sems.at[0]),
        pltpu.make_async_copy(pair.at[w], feat.at[1 - w], f_sems.at[1]),
    ]
    to_wp = [
        pltpu.make_async_copy(heads, wp.at[w], f_sems.at[2]),
        pltpu.make_async_copy(heads_oth, wp.at[1 - w], f_sems.at[3]),
    ]
    start(to_mix + to_down[0] + to_feat + to_down[1] + to_wp)
    wait(to_mix)
    square = jnp.zeros((STEPS, 1), F32)
    width = 512
    for k in range(4):
        h, j = (yh if k < 2 else 1 - yh), k % 2
        if j == 0:
            wait(to_down[k // 2])
        rows = down_w[h, j * 4 : (j + 1) * 4].reshape(width, D)
        down = lax.dot_general(
            mix[...], rows, (((1,), (1,)), ((), ())), preferred_element_type=F32
        )
        if k == 0:
            wait(to_feat)
        at = slice(j * width, (j + 1) * width)
        value = (feat[h, HALO:, at].astype(F32) + down).astype(BF16)
        resid[h, :, at] = value
        wide = value.astype(F32)
        square = square + jnp.sum(wide * wide, axis=1, keepdims=True)
    wait(to_wp)
    raw = dot(resid[0], wp[0]) + dot(resid[1], wp[1])
    norm = lax.rsqrt(square / D + 1e-06)
    logits = raw * norm
    column = lax.broadcasted_iota(jnp.int32, logits.shape, 1)
    policy = column < MOVES
    top = jnp.max(jnp.where(policy, logits, -jnp.inf), axis=1, keepdims=True)
    total = jnp.sum(jnp.where(policy, jnp.exp(logits - top), 0.0), axis=1, keepdims=True)
    lse = top + jnp.log(total)
    played = jnp.broadcast_to(moves[pl.ds(w, 1), :].astype(F32), (128, STEPS)).T
    played = jnp.concatenate([played] * (COLS // 128), axis=1).astype(jnp.int32)
    picked = jnp.sum(jnp.where(column == played, logits, 0.0), axis=1, keepdims=True)
    score = jnp.sum(jnp.where(column == MOVES, logits, 0.0), axis=1, keepdims=True)
    value = jnp.tanh(score)
    place = (yh * 8 + z) * STEPS + lax.broadcasted_iota(jnp.int32, (STEPS, 1), 0)
    miss = value - outcomes[w].astype(F32)
    loss = jnp.where(place < lengths[w], lse - picked + miss * miss, 0.0)
    lane = lax.broadcasted_iota(jnp.int32, (STEPS, 128), 1)
    both = jnp.where(lane == 0, loss, jnp.where(lane == 1, value, 0.0))
    out[...] = both.T[0:2]


def params():
    return pltpu.CompilerParams(vmem_limit_bytes=VMEM_LIMIT)


def shards(
    moves,
    lengths,
    outcomes,
    embedded,
    w_branches,
    conv_w,
    gate_bias,
    rates,
    w_down,
    w_policy,
    w_value,
):
    yh, z, x, c, w = (lax.axis_index(a) for a in ("yh", "z", "x", "c", "w"))
    meta = jnp.stack([w, c, yh, z, x]).astype(jnp.int32)
    ring = ("yh", "w")
    together = lax.optimization_barrier

    halo = lax.ppermute(embedded[:, STEPS - HALO :], ("yh", "z"), [(k, k + 1) for k in range(15)])
    quarters = w_branches.reshape(4, 16, 2, 2, CH).transpose(2, 3, 0, 1, 4)
    quarters = jnp.broadcast_to(quarters[:, None], (2, 8, 2, 4, 16, CH)).reshape(32, 4, 16, CH)
    rows = lax.all_to_all(quarters, ("yh", "z", "c"), 0, 0, tiled=True)
    rows = rows.reshape(2, 8, 2, 4, 16, CH)
    parts = [w_down] + [lax.ppermute(w_down, ring, p) for p in (PAIR, OTHER, turn(4, 2))]
    halo, parts = together((halo, parts))

    own = jnp.concatenate([halo, embedded], axis=1)
    column = lax.all_gather(jnp.stack(parts), ("z", "c"), axis=0).reshape(8, 2, 4, 16, HALF)
    swap = lambda a: lax.ppermute(a, "c", SWAP)
    pair, other = lax.ppermute(own, ring, PAIR), lax.ppermute(own, ring, OTHER)
    behind, ahead = lax.ppermute(rows, "x", turn(4, 1)), lax.ppermute(rows, "x", turn(4, 3))
    own_c = swap(own)
    heads = jnp.concatenate(
        [w_policy, w_value[:, None], jnp.zeros((HALF, COLS - MOVES - 1), BF16)], axis=1
    )
    pair, other, behind, ahead, own_c, heads, pair_half, other_half, meta = together(
        (pair, other, behind, ahead, own_c, heads, pair[1], other[0], meta)
    )
    far0 = lax.ppermute(other_half, ring, PAIR)
    far1 = lax.ppermute(pair_half, ring, OTHER)
    low = lax.ppermute(behind[:1], "x", turn(4, 1))
    high = lax.ppermute(ahead[1:], "x", turn(4, 3))
    pair_c = swap(pair)
    far0, far1, low, high, pair_c, late, column = together(
        (far0, far1, low, high, pair_c, other, column)
    )
    apart = [(k, (k + 2 if k % 2 == 0 else k - 2) % 8) for k in range(8)]
    other_c, far0_c, far1_c = swap(late), swap(far0), swap(far1)
    beside = lax.ppermute(column, ("x", "c"), apart)
    mine = (own, pair, other, far0, far1)
    theirs = (own_c, pair_c, other_c, far0_c, far1_c)
    weights = (rows, behind, ahead, low, high)

    x_scratch = pltpu.VMEM((SEQS, ROWS, D), BF16)
    w_scratch = lambda n: pltpu.VMEM((2, 8, 4, 2, n, 16, CH), BF16)
    by_step = (LANES, STEPS * SEQS, 128)
    sems = lambda n: pltpu.SemaphoreType.DMA((n,))
    decays, states, ends = pl.pallas_call(
        recur_kernel,
        name="recur",
        out_shape=(
            jax.ShapeDtypeStruct(by_step, F32),
            jax.ShapeDtypeStruct(by_step, F32),
            jax.ShapeDtypeStruct((8, 2, SEQS, CH), F32),
        ),
        in_specs=[SM] + [ANY] * 15 + [VM] * 3,
        out_specs=(ANY, ANY, VM),
        scratch_shapes=[
            x_scratch,
            w_scratch(3),
            pltpu.VMEM((2, ROWS, CH), F32),
            pltpu.VMEM(by_step, F32),
            pltpu.VMEM(by_step, F32),
            sems(12),
            sems(5),
            sems(8),
        ],
        compiler_params=params(),
        cost_estimate=pl.CostEstimate(
            flops=2 * 2048 * 2048 * 768, bytes_accessed=15 << 20, transcendentals=5 << 19
        ),
    )(meta, *mine, *theirs, *weights, conv_w, gate_bias, rates[None])

    beside, _ = together((beside, ends))
    beside_c = swap(beside)
    across = lax.dynamic_slice_in_dim(beside, c * 4, 4, 0)
    across = lax.ppermute(across, ("x", "c"), apart)
    heads, _ = together((heads, far0))
    heads_oth = lax.ppermute(heads, "w", SWAP)
    blocks = lax.all_to_all(ends, "z", 0, 0, tiled=True)
    gated = pl.pallas_call(
        gate_kernel,
        name="gate",
        out_shape=jax.ShapeDtypeStruct((SEQS, 2, STEPS, CH), F32),
        in_specs=[SM] + [ANY] * 18,
        out_specs=ANY,
        scratch_shapes=[
            x_scratch,
            w_scratch(1),
            pltpu.VMEM(by_step, F32),
            pltpu.VMEM(by_step, F32),
            pltpu.VMEM((SEQS, 2, STEPS, CH), F32),
            sems(12),
            sems(5),
            sems(2),
            sems(8),
        ],
        compiler_params=params(),
        cost_estimate=pl.CostEstimate(
            flops=2 * 2048 * 2048 * 2048, bytes_accessed=60 << 20, transcendentals=1 << 19
        ),
    )(meta, *mine, *theirs, *weights, decays, states, heads_oth)

    mixed = pl.pallas_call(
        mix_kernel,
        name="mix",
        out_shape=jax.ShapeDtypeStruct((SEQS, STEPS, CH), BF16),
        in_specs=[SM, ANY, VM],
        out_specs=ANY,
        scratch_shapes=[
            pltpu.VMEM((SEQS, 2, STEPS, CH), F32),
            pltpu.VMEM((SEQS, STEPS, CH), BF16),
            sems(8),
            sems(8),
        ],
        compiler_params=params(),
        cost_estimate=pl.CostEstimate(flops=4 << 19, bytes_accessed=5 << 20, transcendentals=0),
    )(meta, gated, blocks)
    across, mixed = together((across, mixed))
    across_c = swap(across)
    mixed = lax.all_to_all(mixed, ("yh", "c", "w"), 0, 0, tiled=True)

    out = pl.pallas_call(
        head_kernel,
        name="head",
        out_shape=jax.ShapeDtypeStruct((2, STEPS), F32),
        in_specs=[SM, SM, SM, VM] + [ANY] * 10,
        out_specs=VM,
        scratch_shapes=[
            pltpu.VMEM((2, ROWS, HALF), BF16),
            pltpu.VMEM((STEPS, D), BF16),
            pltpu.VMEM((2, 8, 4, 2, 16, D), BF16),
            pltpu.VMEM((2, STEPS, HALF), BF16),
            pltpu.VMEM((2, HALF, COLS), BF16),
            sems(4),
            sems(8),
            pltpu.SemaphoreType.DMA((2, 10)),
        ],
        compiler_params=params(),
        cost_estimate=pl.CostEstimate(
            flops=2 * 256 * 2048 * 2432, bytes_accessed=12 << 20, transcendentals=1 << 17
        ),
    )(meta, lengths, outcomes, moves, own, pair, mixed, column, beside, beside_c, across, across_c, heads, heads_oth)
    here = out
    there = lax.ppermute(here, "w", SWAP)
    game = lax.broadcasted_iota(jnp.int32, (2, STEPS), 0) == w
    return (jnp.where(game, here[:1], there[:1]), jnp.where(game, here[1:], there[1:]))


def solution(mesh):
    fine = Mesh(mesh.devices.reshape(2, 8, 4, 2, 2), ("yh", "z", "x", "c", "w"))
    tm, batch = ("yh", "z"), ("x", "c")
    in_specs = (
        P(batch, tm),
        P(batch),
        P(batch),
        P(batch, tm, "w"),
        P(None, tm + batch, "w"),
        P(None, "w"),
        P(None, "w"),
        P("w"),
        P(tm + batch, "w"),
        P("w", None),
        P("w"),
    )
    out_specs = (P(batch, tm), P(batch, tm))
    return jax.shard_map(
        shards, mesh=fine, in_specs=in_specs, out_specs=out_specs, check_vma=False
    )
```

time: 196 us -> 189 us (0.964)
  waiting for transfers between devices: 50.8 us -> 72.4 us
  blocking collectives: 17.9 us -> 0 us
  starting transfers between devices: 52.1 us -> 47.1 us
  Pallas kernels: 41.8 us -> 37.8 us
    ppermute x14 -> x11, waiting for transfers between devices: 39 us -> 18.1 us  [the longest x1 10.6 us: shards(): low = lax.ppermute(behind[:1], 'x', turn(4, 1))]
    ppermute x1, waiting for transfers between devices: 0.01 us -> 20.4 us  [shards(): lax.ppermute(own, ring, OTHER)]
    all_to_all x1 -> x0, blocking collectives: 17.9 us -> none  [shards(): mixed = lax.all_to_all(mixed, ('yh', 'c', 'w'), 0, 0, tiled=True)]
    ppermute x14 -> x11, starting transfers between devices: 28.9 us -> 15.5 us  [the longest x3 4.18 us: shards(): lax.ppermute(w_down, ring, p)]
    all_to_all x2 -> x3, waiting for transfers between devices: 0.01 us -> 13 us  [the longest x1 12.9 us: shards(): mixed = lax.all_to_all(mixed, ('yh', 'c', 'w'), 0, 0, tiled=True)]
    ppermute x1, waiting for transfers between devices: 6.56 us -> 17.2 us  [shards(): lax.ppermute(embedded[:, STEPS - HALO:], ('yh', 'z'), [(k, k + 1) for k i...]
    all_to_all x2 -> x3, starting transfers between devices: 13.2 us -> 21.2 us  [the longest x1 11.8 us: shards(): rows = lax.all_to_all(quarters, ('yh', 'z', 'c'), 0, 0, tiled=True)]
    unnamed x58 -> x26, local copies, waits for them, and re-layouts: 8.66 us -> 3.45 us
  transfers between devices with their start and end apart: 27 -> 27, of which waited for: 9 -> 13; matrix products, arithmetic and copies ran while one was open for 2% -> 5% of each run, Pallas kernels for 17% -> 16%
where the time goes in v3:
time: 189 us; the launch traced here: 186 us
  waiting for transfers between devices  72.4 us (38%)
  starting transfers between devices  47.1 us (25%)
  Pallas kernels  37.8 us (20%)
  between operations  14.3 us (8%)
  local copies, waits for them, and re-layouts  12.6 us (7%)
    ppermute x1, waiting for transfers between devices, shards(): lax.ppermute(own, ring, OTHER)  20.4 us
    ppermute x1, waiting for transfers between devices, shards(): lax.ppermute(embedded[:, STEPS - HALO:], ('yh', 'z'), [(k, k + 1) for k i...  17.2 us
    pallas_call x1, Pallas kernels, shards(): pl.pallas_call(recur_kernel, name='recur', out_shape=(jax.ShapeDtypeStruc...  14.8 us
    all_to_all x1, waiting for transfers between devices, shards(): mixed = lax.all_to_all(mixed, ('yh', 'c', 'w'), 0, 0, tiled=True)  12.9 us
    all_to_all x1, starting transfers between devices, shards(): rows = lax.all_to_all(quarters, ('yh', 'z', 'c'), 0, 0, tiled=True)  11.8 us
    pallas_call x1, Pallas kernels, shards(): pl.pallas_call(gate_kernel, name='gate', out_shape=jax.ShapeDtypeStruct((...  10.9 us
    ppermute x1, waiting for transfers between devices, shards(): low = lax.ppermute(behind[:1], 'x', turn(4, 1))  10.6 us
    pallas_call x1, Pallas kernels, shards(): pl.pallas_call(head_kernel, name='head', out_shape=jax.ShapeDtypeStruct((...  8.08 us
  transfers between devices with their start and end apart: 27, of which 13 were waited for; matrix products, arithmetic and copies ran while one was open for 5% of the time, Pallas kernels for 16%

profile of v3, /device:TPU:16, one launch (start us, length us, event | category | flops | bytes accessed | tf_op | source)
XLA Modules:
  0.0 185.8 jit_solution(14672521320684925751)
XLA Ops:
  9.3 11.8 %all-to-all-start = ((bf16[32,4,16,256]{3,2,1,0:T(8,128)(2,1)}), bf16[32,4,16,256]{3,2,1,0:T(8,128)(2,1)}, u32[]{:S(2)}, u32[]{:S(2)}) async-start(bf16[32,4,16,256]{3,2,1,0:T(8,128)(2,1)} %bitcast.1), calls=%async_computation | async-start | bytes 2097152 | tf_op jit(solution)/shard_map/all_to_all | solution.py:346
  21.1 3.4 %collective-permute-start = (bf16[2,16,1024]{2,1,0:T(8,128)(2,1)S(1)}, bf16[2,16,1024]{2,1,0:T(8,128)(2,1)S(1)}, u32[]{:S(2)}, u32[]{:S(2)}) collective-permute-start(bf16[2,16,1024]{2,1,0:T(8,128)(2,1)S(1)} %slice.27), channel_id=1, source_target_pairs={{0,16},{16,32},{32,48},{48,64},{64,80},{80,96},{96,112},{112,128},... | collective-permute-start | bytes 196616 | tf_op jit(solution)/shard_map/ppermute | solution.py:343
  24.5 1.4 collective-permute-start.1
  25.9 2.8 %collective-permute-start.3 = (bf16[16,1024]{1,0:T(8,128)(2,1)S(1)}, bf16[16,1024]{1,0:T(8,128)(2,1)S(1)}, u32[]{:S(2)}, u32[]{:S(2)}) collective-permute-start(bf16[16,1024]{1,0:T(8,128)(2,1)S(1)} %copy-done.7), channel_id=1, source_target_pairs={{0,128},{1,129},{128,0},{129,1},{2,130},{3,131},{130,2},{131,3},{4... | collective-permute-start | bytes 98312 | tf_op jit(solution)/shard_map/ppermute | solution.py:348
  29.1 1.4 collective-permute-done.2
  31.4 17.2 %collective-permute-done = bf16[2,16,1024]{2,1,0:T(8,128)(2,1)S(1)} collective-permute-done((bf16[2,16,1024]{2,1,0:T(8,128)(2,1)S(1)}, bf16[2,16,1024]{2,1,0:T(8,128)(2,1)S(1)}, u32[]{:S(2)}, u32[]{:S(2)}) %collective-permute-start) | collective-permute-done | bytes 65568 | tf_op jit(solution)/shard_map/ppermute | solution.py:343
  52.3 1.5 collective-permute-start.6
  53.8 1.7 collective-permute-start.7
  57.1 20.4 %collective-permute-done.5.refs_2_ = bf16[2,272,1024]{2,1,0:T(8,128)(2,1)} collective-permute-done((bf16[2,272,1024]{2,1,0:T(8,128)(2,1)}, bf16[2,272,1024]{2,1,0:T(8,128)(2,1)}, u32[]{:S(2)}, u32[]{:S(2)}) %collective-permute-start.5) | collective-permute-done | bytes 1114144 | tf_op jit(solution)/shard_map/ppermute | solution.py:354
  79.4 2.6 %collective-permute-start.10 = (bf16[272,1024]{1,0:T(8,128)(2,1)S(1)}, bf16[272,1024]{1,0:T(8,128)(2,1)S(1)}, u32[]{:S(2)}, u32[]{:S(2)}) collective-permute-start(bf16[272,1024]{1,0:T(8,128)(2,1)S(1)} %slice_bitcast_fusion.1), channel_id=1, source_target_pairs={{0,129},{129,0},{1,128},{128,1},{2,131},{131,2},{3,130},{130,3},{4... | collective-permute-start | bytes 1671176 | tf_op jit(solution)/shard_map/ppermute | solution.py:364
  83.9 1.6 collective-permute-start.11
  86.5 1.8 collective-permute-start.12
  88.4 10.6 %collective-permute-done.11.refs_13_ = bf16[1,8,2,4,16,256]{5,4,3,2,1,0:T(8,128)(2,1)S(1)} collective-permute-done((bf16[1,8,2,4,16,256]{5,4,3,2,1,0:T(8,128)(2,1)S(1)}, bf16[1,8,2,4,16,256]{5,4,3,2,1,0:T(8,128)(2,1)S(1)}, u32[]{:S(2)}, u32[]{:S(2)}) %collective-permute-start.11) | collective-permute-done | bytes 524320 | tf_op jit(solution)/shard_map/ppermute | solution.py:365
  104.3 2.6 %collective-permute-done.16.refs_8_ = bf16[272,1024]{1,0:T(8,128)(2,1)} collective-permute-done((bf16[272,1024]{1,0:T(8,128)(2,1)}, bf16[272,1024]{1,0:T(8,128)(2,1)}, u32[]{:S(2)}, u32[]{:S(2)}) %collective-permute-start.16) | collective-permute-done | bytes 557088 | tf_op jit(solution)/shard_map/ppermute | solution.py:353
  106.9 14.8 %recur.1 = (f32[2,2048,128]{2,1,0:T(8,128)}, f32[2,2048,128]{2,1,0:T(8,128)}, f32[8,2,8,256]{3,2,1,0:T(8,128)}) custom-call(s32[5]{0:T(128)} %stack.38.meta, bf16[2,272,1024]{2,1,0:T(8,128)(2,1)} %constant_dynamic-update-slice_fusion.refs_0_.own, bf16[2,272,1024]{2,1,0:T(8,128)(2,1)} %copy-done.3, bf16[2,272,1024]{2,1,0:T(8,128)(2,1)} %collective-permute-done.5.refs_2_, ...), custom_call_target="tpu_custom_call" | custom-call | flops 6442450944 | bytes 15728640 | tf_op jit(solution)/shard_map/recur/pallas_call | solution.py:382
  121.7 4.6 %all-to-all-start.1 = ((f32[8,2,8,256]{3,2,1,0:T(8,128)}), f32[8,2,8,256]{3,2,1,0:T(8,128)S(1)}, u32[]{:S(2)}, u32[]{:S(2)}) async-start(f32[8,2,8,256]{3,2,1,0:T(8,128)} %get-tuple-element.50), calls=%async_computation.1 | async-start | bytes 262144 | tf_op jit(solution)/shard_map/all_to_all | solution.py:414
  126.3 2.2 %collective-permute-done.14.beside = bf16[8,2,4,16,1024]{4,3,2,1,0:T(8,128)(2,1)S(1)} collective-permute-done((bf16[8,2,4,16,1024]{4,3,2,1,0:T(8,128)(2,1)}, bf16[8,2,4,16,1024]{4,3,2,1,0:T(8,128)(2,1)S(1)}, u32[]{:S(2)}, u32[]{:S(2)}) %collective-permute-start.14) | collective-permute-done | bytes 2097184 | tf_op jit(solution)/shard_map/ppermute | solution.py:373
  129.6 10.9 %gate.1.gated = f32[8,2,256,256]{3,2,1,0:T(8,128)} custom-call(s32[5]{0:T(128)} %stack.38.meta, bf16[2,272,1024]{2,1,0:T(8,128)(2,1)} %constant_dynamic-update-slice_fusion.refs_0_.own, bf16[2,272,1024]{2,1,0:T(8,128)(2,1)} %copy-done.3, bf16[2,272,1024]{2,1,0:T(8,128)(2,1)} %collective-permute-done.5.refs_2_, ...), custom_call_target="tpu_custom_call" | custom-call | flops 17179869184 | bytes 62914560 | tf_op jit(solution)/shard_map/gate/pallas_call | solution.py:415
  141.2 4.0 %mix.1 = bf16[8,256,256]{2,1,0:T(8,128)(2,1)} custom-call(s32[5]{0:T(128)} %stack.38.meta, f32[8,2,256,256]{3,2,1,0:T(8,128)} %gate.1.gated, f32[8,2,8,256]{3,2,1,0:T(8,128)} %copy-done.6), custom_call_target="tpu_custom_call" | custom-call | flops 2097152 | bytes 5242880 | tf_op jit(solution)/shard_map/mix/pallas_call | solution.py:438
  145.9 1.5 collective-permute-start.21
  147.4 4.8 %all-to-all-start.2 = ((bf16[8,256,256]{2,1,0:T(8,128)(2,1)}), bf16[8,256,256]{2,1,0:T(8,128)(2,1)S(1)}, u32[]{:S(2)}, u32[]{:S(2)}) async-start(bf16[8,256,256]{2,1,0:T(8,128)(2,1)} %mix.1), calls=%async_computation.2 | async-start | bytes 2097152 | tf_op jit(solution)/shard_map/all_to_all | solution.py:455
  152.2 12.9 %all-to-all-done.2.mixed = bf16[8,256,256]{2,1,0:T(8,128)(2,1)S(1)} async-done(((bf16[8,256,256]{2,1,0:T(8,128)(2,1)}), bf16[8,256,256]{2,1,0:T(8,128)(2,1)S(1)}, u32[]{:S(2)}, u32[]{:S(2)}) %all-to-all-start.2) | async-done | bytes 1048608 | tf_op jit(solution)/shard_map/all_to_all | solution.py:455
  166.2 8.1 %head.1 = f32[2,256]{1,0:T(2,128)} custom-call(s32[5]{0:T(128)} %stack.38.meta, s32[2]{0:T(128)} %lengths.1, s32[2]{0:T(128)} %outcomes.1, s32[2,256]{1,0:T(2,128)} %moves.1, bf16[2,272,1024]{2,1,0:T(8,128)(2,1)} %constant_dynamic-update-slice_fusion.refs_0_.own, bf16[2,272,1024]{2,1,0:T(8,128)(2,1)} %copy-done.3, bf16[8,256,256]{2,1,0:T(8,128)(2,1)} %copy-done.1, ...), custom_call_target="tpu_custom_call" | custom-call | flops 2550136832 | bytes 12582912 | tf_op jit(solution)/shard_map/head/pallas_call | solution.py:457
  174.2 2.3 %collective-permute-start.22 = (f32[2,256]{1,0:T(2,128)}, f32[2,256]{1,0:T(2,128)S(1)}, u32[]{:S(2)}, u32[]{:S(2)}) collective-permute-start(f32[2,256]{1,0:T(2,128)} %head.1), channel_id=1, source_target_pairs={{0,1},{1,0},{2,3},{3,2},{4,5},{5,4},{6,7},{7,6},{8,9},{9,8},{10,11... | collective-permute-start | bytes 6152 | tf_op jit(solution)/shard_map/ppermute | solution.py:479
  (81 shorter events, 24.6 us)
Async XLA Ops:
  9.3 43.0 %all-to-all-start = ((bf16[32,4,16,256]{3,2,1,0:T(8,128)(2,1)}), bf16[32,4,16,256]{3,2,1,0:T(8,128)(2,1)}, u32[]{:S(2)}, u32[]{:S(2)}) async-start(bf16[32,4,16,256]{3,2,1,0:T(8,128)(2,1)} %bitcast.1), calls=%async_computation | async-start | bytes 2097152 | tf_op jit(solution)/shard_map/all_to_all | solution.py:346
  21.1 79.8 %all-gather.3.cloned.1.call-start = ((), (), s32[]{:S(2)}) async-start(), calls=%async_computation.3 | async-start | bytes 2228224 | tf_op jit(solution)/shard_map/all_gather | solution.py:352
  21.1 27.5 %collective-permute-start = (bf16[2,16,1024]{2,1,0:T(8,128)(2,1)S(1)}, bf16[2,16,1024]{2,1,0:T(8,128)(2,1)S(1)}, u32[]{:S(2)}, u32[]{:S(2)}) collective-permute-start(bf16[2,16,1024]{2,1,0:T(8,128)(2,1)S(1)} %slice.27), channel_id=1, source_target_pairs={{0,16},{16,32},{32,48},{48,64},{64,80},{80,96},{96,112},{112,128},... | collective-permute-start | bytes 196616 | tf_op jit(solution)/shard_map/ppermute | solution.py:343
  24.5 4.5 %collective-permute-start.1 = (bf16[16,1024]{1,0:T(8,128)(2,1)S(1)}, bf16[16,1024]{1,0:T(8,128)(2,1)S(1)}, u32[]{:S(2)}, u32[]{:S(2)}) collective-permute-start(bf16[16,1024]{1,0:T(8,128)(2,1)S(1)} %copy-done.7), channel_id=1, source_target_pairs={{0,1},{1,0},{128,129},{129,128},{2,3},{3,2},{130,131},{131,130},{4... | collective-permute-start | bytes 98312 | tf_op jit(solution)/shard_map/ppermute | solution.py:348
  25.9 4.6 %collective-permute-start.2 = (bf16[16,1024]{1,0:T(8,128)(2,1)S(1)}, bf16[16,1024]{1,0:T(8,128)(2,1)S(1)}, u32[]{:S(2)}, u32[]{:S(2)}) collective-permute-start(bf16[16,1024]{1,0:T(8,128)(2,1)S(1)} %copy-done.7), channel_id=1, source_target_pairs={{0,129},{129,0},{1,128},{128,1},{2,131},{131,2},{3,130},{130,3},{4... | collective-permute-start | bytes 98312 | tf_op jit(solution)/shard_map/ppermute | solution.py:348
  25.9 5.5 %collective-permute-start.3 = (bf16[16,1024]{1,0:T(8,128)(2,1)S(1)}, bf16[16,1024]{1,0:T(8,128)(2,1)S(1)}, u32[]{:S(2)}, u32[]{:S(2)}) collective-permute-start(bf16[16,1024]{1,0:T(8,128)(2,1)S(1)} %copy-done.7), channel_id=1, source_target_pairs={{0,128},{1,129},{128,0},{129,1},{2,130},{3,131},{130,2},{131,3},{4... | collective-permute-start | bytes 98312 | tf_op jit(solution)/shard_map/ppermute | solution.py:348
  51.0 26.5 %collective-permute-start.5 = (bf16[2,272,1024]{2,1,0:T(8,128)(2,1)}, bf16[2,272,1024]{2,1,0:T(8,128)(2,1)}, u32[]{:S(2)}, u32[]{:S(2)}) collective-permute-start(bf16[2,272,1024]{2,1,0:T(8,128)(2,1)} %constant_dynamic-update-slice_fusion.refs_0_.own), channel_id=1, source_target_pairs={{0,129},{129,0},{1,128},{128,1},{2,131},{131,2},{3,130},{130,3},{4... | collective-permute-start | bytes 3342344 | tf_op jit(solution)/shard_map/ppermute | solution.py:354
  51.0 27.6 %collective-permute-start.4 = (bf16[2,272,1024]{2,1,0:T(8,128)(2,1)}, bf16[2,272,1024]{2,1,0:T(8,128)(2,1)S(1)}, u32[]{:S(2)}, u32[]{:S(2)}) collective-permute-start(bf16[2,272,1024]{2,1,0:T(8,128)(2,1)} %constant_dynamic-update-slice_fusion.refs_0_.own), channel_id=1, source_target_pairs={{0,1},{1,0},{128,129},{129,128},{2,3},{3,2},{130,131},{131,130},{4... | collective-permute-start | bytes 3342344 | tf_op jit(solution)/shard_map/ppermute | solution.py:354
  52.3 26.4 %collective-permute-start.8 = (bf16[2,272,1024]{2,1,0:T(8,128)(2,1)}, bf16[2,272,1024]{2,1,0:T(8,128)(2,1)}, u32[]{:S(2)}, u32[]{:S(2)}) collective-permute-start(bf16[2,272,1024]{2,1,0:T(8,128)(2,1)} %constant_dynamic-update-slice_fusion.refs_0_.own), channel_id=1, source_target_pairs={{0,2},{2,0},{1,3},{3,1},{4,6},{6,4},{5,7},{7,5},{8,10},{10,8},{9,1... | collective-permute-start | bytes 3342344 | tf_op jit(solution)/shard_map/ppermute | solution.py:353
  52.3 27.1 %collective-permute-start.6 = (bf16[2,8,2,4,16,256]{5,4,3,2,1,0:T(8,128)(2,1)}, bf16[2,8,2,4,16,256]{5,4,3,2,1,0:T(8,128)(2,1)}, u32[]{:S(2)}, u32[]{:S(2)}) collective-permute-start(bf16[2,8,2,4,16,256]{5,4,3,2,1,0:T(8,128)(2,1)} %bitcast.2.refs_10_), channel_id=1, source_target_pairs={{0,4},{4,8},{8,12},{12,0},{1,5},{5,9},{9,13},{13,1},{2,6},{6,10},{... | collective-permute-start | bytes 3145736 | tf_op jit(solution)/shard_map/ppermute | solution.py:355
  53.8 25.6 %collective-permute-start.7 = (bf16[2,8,2,4,16,256]{5,4,3,2,1,0:T(8,128)(2,1)}, bf16[2,8,2,4,16,256]{5,4,3,2,1,0:T(8,128)(2,1)}, u32[]{:S(2)}, u32[]{:S(2)}) collective-permute-start(bf16[2,8,2,4,16,256]{5,4,3,2,1,0:T(8,128)(2,1)} %bitcast.2.refs_10_), channel_id=1, source_target_pairs={{0,12},{4,0},{8,4},{12,8},{1,13},{5,1},{9,5},{13,9},{2,14},{6,2},{... | collective-permute-start | bytes 3145736 | tf_op jit(solution)/shard_map/ppermute | solution.py:355
  79.4 21.5 %collective-permute-start.13 = (bf16[2,272,1024]{2,1,0:T(8,128)(2,1)S(1)}, bf16[2,272,1024]{2,1,0:T(8,128)(2,1)}, u32[]{:S(2)}, u32[]{:S(2)}) collective-permute-start(bf16[2,272,1024]{2,1,0:T(8,128)(2,1)S(1)} %collective-permute-done.4.refs_1_.pair), channel_id=1, source_target_pairs={{0,2},{2,0},{1,3},{3,1},{4,6},{6,4},{5,7},{7,5},{8,10},{10,8},{9,1... | collective-permute-start | bytes 3342344 | tf_op jit(solution)/shard_map/ppermute | solution.py:353
  79.4 20.7 %collective-permute-start.10 = (bf16[272,1024]{1,0:T(8,128)(2,1)S(1)}, bf16[272,1024]{1,0:T(8,128)(2,1)S(1)}, u32[]{:S(2)}, u32[]{:S(2)}) collective-permute-start(bf16[272,1024]{1,0:T(8,128)(2,1)S(1)} %slice_bitcast_fusion.1), channel_id=1, source_target_pairs={{0,129},{129,0},{1,128},{128,1},{2,131},{131,2},{3,130},{130,3},{4... | collective-permute-start | bytes 1671176 | tf_op jit(solution)/shard_map/ppermute | solution.py:364
  82.1 18.9 %collective-permute-start.9 = (bf16[272,1024]{1,0:T(8,128)(2,1)S(1)}, bf16[272,1024]{1,0:T(8,128)(2,1)}, u32[]{:S(2)}, u32[]{:S(2)}) collective-permute-start(bf16[272,1024]{1,0:T(8,128)(2,1)S(1)} %slice_bitcast_fusion), channel_id=1, source_target_pairs={{0,1},{1,0},{128,129},{129,128},{2,3},{3,2},{130,131},{131,130},{4... | collective-permute-start | bytes 1671176 | tf_op jit(solution)/shard_map/ppermute | solution.py:363
  83.9 15.1 %collective-permute-start.11 = (bf16[1,8,2,4,16,256]{5,4,3,2,1,0:T(8,128)(2,1)S(1)}, bf16[1,8,2,4,16,256]{5,4,3,2,1,0:T(8,128)(2,1)S(1)}, u32[]{:S(2)}, u32[]{:S(2)}) collective-permute-start(bf16[1,8,2,4,16,256]{5,4,3,2,1,0:T(8,128)(2,1)S(1)} %slice.30), channel_id=1, source_target_pairs={{0,4},{4,8},{8,12},{12,0},{1,5},{5,9},{9,13},{13,1},{2,6},{6,10},{... | collective-permute-start | bytes 1572872 | tf_op jit(solution)/shard_map/ppermute | solution.py:365
  86.5 13.6 %collective-permute-start.12 = (bf16[1,8,2,4,16,256]{5,4,3,2,1,0:T(8,128)(2,1)S(1)}, bf16[1,8,2,4,16,256]{5,4,3,2,1,0:T(8,128)(2,1)S(1)}, u32[]{:S(2)}, u32[]{:S(2)}) collective-permute-start(bf16[1,8,2,4,16,256]{5,4,3,2,1,0:T(8,128)(2,1)S(1)} %slice.31), channel_id=1, source_target_pairs={{0,12},{4,0},{8,4},{12,8},{1,13},{5,1},{9,5},{13,9},{2,14},{6,2},{... | collective-permute-start | bytes 1572872 | tf_op jit(solution)/shard_map/ppermute | solution.py:366
  100.9 27.5 %collective-permute-start.14 = (bf16[8,2,4,16,1024]{4,3,2,1,0:T(8,128)(2,1)}, bf16[8,2,4,16,1024]{4,3,2,1,0:T(8,128)(2,1)S(1)}, u32[]{:S(2)}, u32[]{:S(2)}) collective-permute-start(bf16[8,2,4,16,1024]{4,3,2,1,0:T(8,128)(2,1)} %bitcast.22), channel_id=1, source_target_pairs={{0,4},{2,14},{4,8},{6,2},{8,12},{10,6},{12,0},{14,10},{1,5},{3,15}... | collective-permute-start | bytes 6291464 | tf_op jit(solution)/shard_map/ppermute | solution.py:373
  102.2 4.7 %collective-permute-start.15 = (bf16[2,272,1024]{2,1,0:T(8,128)(2,1)}, bf16[2,272,1024]{2,1,0:T(8,128)(2,1)}, u32[]{:S(2)}, u32[]{:S(2)}) collective-permute-start(bf16[2,272,1024]{2,1,0:T(8,128)(2,1)} %collective-permute-done.5.refs_2_), channel_id=1, source_target_pairs={{0,2},{2,0},{1,3},{3,1},{4,6},{6,4},{5,7},{7,5},{8,10},{10,8},{9,1... | collective-permute-start | bytes 3342344 | tf_op jit(solution)/shard_map/ppermute | solution.py:353
  103.0 26.6 %collective-permute-start.19 = (bf16[1024,384]{1,0:T(8,128)(2,1)S(1)}, bf16[1024,384]{1,0:T(8,128)(2,1)}, u32[]{:S(2)}, u32[]{:S(2)}) collective-permute-start(bf16[1024,384]{1,0:T(8,128)(2,1)S(1)} %maximum_maximum_fusion.heads), channel_id=1, source_target_pairs={{0,1},{1,0},{2,3},{3,2},{4,5},{5,4},{6,7},{7,6},{8,9},{9,8},{10,11... | collective-permute-start | bytes 2359304 | tf_op jit(solution)/shard_map/ppermute | solution.py:413
  121.7 18.8 %all-to-all-start.1 = ((f32[8,2,8,256]{3,2,1,0:T(8,128)}), f32[8,2,8,256]{3,2,1,0:T(8,128)S(1)}, u32[]{:S(2)}, u32[]{:S(2)}) async-start(f32[8,2,8,256]{3,2,1,0:T(8,128)} %get-tuple-element.50), calls=%async_computation.1 | async-start | bytes 262144 | tf_op jit(solution)/shard_map/all_to_all | solution.py:414
  128.5 36.7 %collective-permute-start.20 = (bf16[8,2,4,16,1024]{4,3,2,1,0:T(8,128)(2,1)S(1)}, bf16[8,2,4,16,1024]{4,3,2,1,0:T(8,128)(2,1)}, u32[]{:S(2)}, u32[]{:S(2)}) collective-permute-start(bf16[8,2,4,16,1024]{4,3,2,1,0:T(8,128)(2,1)S(1)} %collective-permute-done.14.beside), channel_id=1, source_target_pairs={{0,2},{2,0},{1,3},{3,1},{4,6},{6,4},{5,7},{7,5},{8,10},{10,8},{9,1... | collective-permute-start | bytes 6291464 | tf_op jit(solution)/shard_map/ppermute | solution.py:353
  129.6 16.3 %collective-permute-start.18 = (bf16[4,2,4,16,1024]{4,3,2,1,0:T(8,128)(2,1)}, bf16[4,2,4,16,1024]{4,3,2,1,0:T(8,128)(2,1)}, u32[]{:S(2)}, u32[]{:S(2)}) collective-permute-start(bf16[4,2,4,16,1024]{4,3,2,1,0:T(8,128)(2,1)} %constant_dynamic-slice_fusion), channel_id=1, source_target_pairs={{0,4},{2,14},{4,8},{6,2},{8,12},{10,6},{12,0},{14,10},{1,5},{3,15}... | collective-permute-start | bytes 3145736 | tf_op jit(solution)/shard_map/ppermute | solution.py:411
  145.9 19.2 %collective-permute-start.21 = (bf16[4,2,4,16,1024]{4,3,2,1,0:T(8,128)(2,1)}, bf16[4,2,4,16,1024]{4,3,2,1,0:T(8,128)(2,1)}, u32[]{:S(2)}, u32[]{:S(2)}) collective-permute-start(bf16[4,2,4,16,1024]{4,3,2,1,0:T(8,128)(2,1)} %collective-permute-done.18.across), channel_id=1, source_target_pairs={{0,2},{2,0},{1,3},{3,1},{4,6},{6,4},{5,7},{7,5},{8,10},{10,8},{9,1... | collective-permute-start | bytes 3145736 | tf_op jit(solution)/shard_map/ppermute | solution.py:353
  147.4 17.8 %all-to-all-start.2 = ((bf16[8,256,256]{2,1,0:T(8,128)(2,1)}), bf16[8,256,256]{2,1,0:T(8,128)(2,1)S(1)}, u32[]{:S(2)}, u32[]{:S(2)}) async-start(bf16[8,256,256]{2,1,0:T(8,128)(2,1)} %mix.1), calls=%async_computation.2 | async-start | bytes 2097152 | tf_op jit(solution)/shard_map/all_to_all | solution.py:455
  (15 other events, 126.3 us)
Sparse Core Ops, SparseCore 0:
  49.5 38.6 all-gather.2

commit v4 on v3

--- a/solution.py
+++ b/solution.py
@@ -38,7 +38,7 @@
     return jnp.dot(a, b, preferred_element_type=F32)
 
 
-def piece_copies(pieces, held, sems, w):
+def piece_copies(pieces, held, sems, w, skip=0):
     mine = pl.ds(pl.multiple_of(w * HALF, HALF), HALF)
     theirs = pl.ds(pl.multiple_of((1 - w) * HALF, HALF), HALF)
     groups = []
@@ -52,7 +52,9 @@
                 moved = ((far0, s, mine), (far1, s + 1, mine), (other, pl.ds(s, 2), theirs))
             groups.append(
                 [
-                    pltpu.make_async_copy(src, held.at[at, :, cols], sems.at[k + n])
+                    pltpu.make_async_copy(
+                        src.at[..., pl.ds(skip, ROWS - skip), :], held.at[at, :, cols], sems.at[k + n]
+                    )
                     for n, (src, at, cols) in enumerate(moved)
                 ]
             )
@@ -158,7 +160,7 @@
     feat, held, decays, states, both, x_sems, w_sems, in_sems, out_sems = refs[19:]
     w, x = meta[0], meta[4]
     to_held = weight_copies(refs[10:15], 0, held, x, w_sems)
-    groups = piece_copies(pieces, feat, x_sems, w)
+    groups = piece_copies(pieces, feat, x_sems, w, HALO)
     to_in = [
         pltpu.make_async_copy(decays_in, decays, in_sems.at[0]),
         pltpu.make_async_copy(states_in, states, in_sems.at[1]),
@@ -169,22 +171,22 @@
     def moved(i):
         return pltpu.make_async_copy(both.at[i], out.at[i], out_sems.at[i])
 
-    def one(i, carry):
-        gated = jax.nn.gelu(dot(feat[i, HALO:], weights_of(held, 0)))
+    def one(i):
+        gated = jax.nn.gelu(dot(feat[i], weights_of(held, 0)))
         at = pl.ds(i, STEPS, stride=SEQS)
         for lane in range(LANES):
             cols = slice(lane * 128, (lane + 1) * 128)
             both[i, 0, :, cols] = decays[lane, at, :] * gated[:, cols]
             both[i, 1, :, cols] = states[lane, at, :] * gated[:, cols]
         moved(i).start()
-        return carry
 
     wait(to_held)
     for n, group in enumerate(groups):
         wait(group)
         if n == 0:
             wait(to_in)
-        lax.fori_loop(n * 2, n * 2 + 2, one, 0)
+        one(n * 2)
+        one(n * 2 + 1)
     wait([moved(i) for i in range(SEQS)])
 
 
@@ -419,7 +421,7 @@
         in_specs=[SM] + [ANY] * 18,
         out_specs=ANY,
         scratch_shapes=[
-            x_scratch,
+            pltpu.VMEM((SEQS, STEPS, D), BF16),
             w_scratch(1),
             pltpu.VMEM(by_step, F32),
             pltpu.VMEM(by_step, F32),

time: 189 us -> 187 us (0.989)
  Pallas kernels: 37.8 us -> 35.6 us
  waiting for transfers between devices: 72.4 us -> 74.6 us
    pallas_call x1, Pallas kernels: 10.9 us -> 8.74 us  [shards(): pl.pallas_call(gate_kernel, name='gate', out_shape=jax.ShapeDtypeStruct((...]
    ppermute x1, waiting for transfers between devices: 0.75 us -> 2.93 us  [shards(): across = lax.ppermute(across, ('x', 'c'), apart)]
  transfers between devices with their start and end apart: 27 -> 27, of which waited for: 13 -> 13; matrix products, arithmetic and copies ran while one was open for 5% -> 5% of each run, Pallas kernels for 16% -> 15%
where the time goes in v4:
time: 187 us; the launch traced here: 184 us
  waiting for transfers between devices  74.6 us (40%)
  starting transfers between devices  45.8 us (24%)
  Pallas kernels  35.6 us (19%)
  between operations  14.3 us (8%)
  local copies, waits for them, and re-layouts  12.6 us (7%)
    ppermute x1, waiting for transfers between devices, shards(): lax.ppermute(own, ring, OTHER)  20.4 us
    ppermute x1, waiting for transfers between devices, shards(): lax.ppermute(embedded[:, STEPS - HALO:], ('yh', 'z'), [(k, k + 1) for k i...  17.2 us
    pallas_call x1, Pallas kernels, shards(): pl.pallas_call(recur_kernel, name='recur', out_shape=(jax.ShapeDtypeStruc...  14.8 us
    all_to_all x1, waiting for transfers between devices, shards(): mixed = lax.all_to_all(mixed, ('yh', 'c', 'w'), 0, 0, tiled=True)  12.9 us
    all_to_all x1, starting transfers between devices, shards(): rows = lax.all_to_all(quarters, ('yh', 'z', 'c'), 0, 0, tiled=True)  11.8 us
    ppermute x1, waiting for transfers between devices, shards(): low = lax.ppermute(behind[:1], 'x', turn(4, 1))  10.6 us
    pallas_call x1, Pallas kernels, shards(): pl.pallas_call(gate_kernel, name='gate', out_shape=jax.ShapeDtypeStruct((...  8.74 us
    pallas_call x1, Pallas kernels, shards(): pl.pallas_call(head_kernel, name='head', out_shape=jax.ShapeDtypeStruct((...  8.08 us
  transfers between devices with their start and end apart: 27, of which 13 were waited for; matrix products, arithmetic and copies ran while one was open for 5% of the time, Pallas kernels for 15%

profile of v4, /device:TPU:16, one launch (start us, length us, event | category | flops | bytes accessed | tf_op | source)
XLA Modules:
  0.0 184.4 jit_solution(710773600916083941)
XLA Ops:
  9.3 11.8 %all-to-all-start = ((bf16[32,4,16,256]{3,2,1,0:T(8,128)(2,1)}), bf16[32,4,16,256]{3,2,1,0:T(8,128)(2,1)}, u32[]{:S(2)}, u32[]{:S(2)}) async-start(bf16[32,4,16,256]{3,2,1,0:T(8,128)(2,1)} %bitcast.1), calls=%async_computation | async-start | bytes 2097152 | tf_op jit(solution)/shard_map/all_to_all | solution.py:348
  21.1 3.4 %collective-permute-start = (bf16[2,16,1024]{2,1,0:T(8,128)(2,1)S(1)}, bf16[2,16,1024]{2,1,0:T(8,128)(2,1)S(1)}, u32[]{:S(2)}, u32[]{:S(2)}) collective-permute-start(bf16[2,16,1024]{2,1,0:T(8,128)(2,1)S(1)} %slice.27), channel_id=1, source_target_pairs={{0,16},{16,32},{32,48},{48,64},{64,80},{80,96},{96,112},{112,128},... | collective-permute-start | bytes 196616 | tf_op jit(solution)/shard_map/ppermute | solution.py:345
  24.5 1.4 collective-permute-start.1
  25.9 2.8 %collective-permute-start.3 = (bf16[16,1024]{1,0:T(8,128)(2,1)S(1)}, bf16[16,1024]{1,0:T(8,128)(2,1)S(1)}, u32[]{:S(2)}, u32[]{:S(2)}) collective-permute-start(bf16[16,1024]{1,0:T(8,128)(2,1)S(1)} %copy-done.7), channel_id=1, source_target_pairs={{0,128},{1,129},{128,0},{129,1},{2,130},{3,131},{130,2},{131,3},{4... | collective-permute-start | bytes 98312 | tf_op jit(solution)/shard_map/ppermute | solution.py:350
  29.1 1.4 collective-permute-done.2
  31.4 17.2 %collective-permute-done = bf16[2,16,1024]{2,1,0:T(8,128)(2,1)S(1)} collective-permute-done((bf16[2,16,1024]{2,1,0:T(8,128)(2,1)S(1)}, bf16[2,16,1024]{2,1,0:T(8,128)(2,1)S(1)}, u32[]{:S(2)}, u32[]{:S(2)}) %collective-permute-start) | collective-permute-done | bytes 65568 | tf_op jit(solution)/shard_map/ppermute | solution.py:345
  52.3 1.5 collective-permute-start.6
  53.8 1.7 collective-permute-start.7
  57.1 20.4 %collective-permute-done.5.refs_2_ = bf16[2,272,1024]{2,1,0:T(8,128)(2,1)} collective-permute-done((bf16[2,272,1024]{2,1,0:T(8,128)(2,1)}, bf16[2,272,1024]{2,1,0:T(8,128)(2,1)}, u32[]{:S(2)}, u32[]{:S(2)}) %collective-permute-start.5) | collective-permute-done | bytes 1114144 | tf_op jit(solution)/shard_map/ppermute | solution.py:356
  79.4 2.6 %collective-permute-start.10 = (bf16[272,1024]{1,0:T(8,128)(2,1)S(1)}, bf16[272,1024]{1,0:T(8,128)(2,1)S(1)}, u32[]{:S(2)}, u32[]{:S(2)}) collective-permute-start(bf16[272,1024]{1,0:T(8,128)(2,1)S(1)} %slice_bitcast_fusion.1), channel_id=1, source_target_pairs={{0,129},{129,0},{1,128},{128,1},{2,131},{131,2},{3,130},{130,3},{4... | collective-permute-start | bytes 1671176 | tf_op jit(solution)/shard_map/ppermute | solution.py:366
  83.9 1.6 collective-permute-start.11
  86.5 1.8 collective-permute-start.12
  88.4 10.6 %collective-permute-done.11.refs_13_ = bf16[1,8,2,4,16,256]{5,4,3,2,1,0:T(8,128)(2,1)S(1)} collective-permute-done((bf16[1,8,2,4,16,256]{5,4,3,2,1,0:T(8,128)(2,1)S(1)}, bf16[1,8,2,4,16,256]{5,4,3,2,1,0:T(8,128)(2,1)S(1)}, u32[]{:S(2)}, u32[]{:S(2)}) %collective-permute-start.11) | collective-permute-done | bytes 524320 | tf_op jit(solution)/shard_map/ppermute | solution.py:367
  104.3 2.6 %collective-permute-done.16.refs_8_ = bf16[272,1024]{1,0:T(8,128)(2,1)} collective-permute-done((bf16[272,1024]{1,0:T(8,128)(2,1)}, bf16[272,1024]{1,0:T(8,128)(2,1)}, u32[]{:S(2)}, u32[]{:S(2)}) %collective-permute-start.16) | collective-permute-done | bytes 557088 | tf_op jit(solution)/shard_map/ppermute | solution.py:355
  106.9 14.8 %recur.1 = (f32[2,2048,128]{2,1,0:T(8,128)}, f32[2,2048,128]{2,1,0:T(8,128)}, f32[8,2,8,256]{3,2,1,0:T(8,128)}) custom-call(s32[5]{0:T(128)} %stack.38.meta, bf16[2,272,1024]{2,1,0:T(8,128)(2,1)} %constant_dynamic-update-slice_fusion.refs_0_.own, bf16[2,272,1024]{2,1,0:T(8,128)(2,1)} %copy-done.3, bf16[2,272,1024]{2,1,0:T(8,128)(2,1)} %collective-permute-done.5.refs_2_, ...), custom_call_target="tpu_custom_call" | custom-call | flops 6442450944 | bytes 15728640 | tf_op jit(solution)/shard_map/recur/pallas_call | solution.py:384
  121.7 4.6 %all-to-all-start.1 = ((f32[8,2,8,256]{3,2,1,0:T(8,128)}), f32[8,2,8,256]{3,2,1,0:T(8,128)S(1)}, u32[]{:S(2)}, u32[]{:S(2)}) async-start(f32[8,2,8,256]{3,2,1,0:T(8,128)} %get-tuple-element.50), calls=%async_computation.1 | async-start | bytes 262144 | tf_op jit(solution)/shard_map/all_to_all | solution.py:416
  126.3 2.2 %collective-permute-done.14.beside = bf16[8,2,4,16,1024]{4,3,2,1,0:T(8,128)(2,1)S(1)} collective-permute-done((bf16[8,2,4,16,1024]{4,3,2,1,0:T(8,128)(2,1)}, bf16[8,2,4,16,1024]{4,3,2,1,0:T(8,128)(2,1)S(1)}, u32[]{:S(2)}, u32[]{:S(2)}) %collective-permute-start.14) | collective-permute-done | bytes 2097184 | tf_op jit(solution)/shard_map/ppermute | solution.py:375
  129.6 8.7 %gate.1.gated = f32[8,2,256,256]{3,2,1,0:T(8,128)} custom-call(s32[5]{0:T(128)} %stack.38.meta, bf16[2,272,1024]{2,1,0:T(8,128)(2,1)} %constant_dynamic-update-slice_fusion.refs_0_.own, bf16[2,272,1024]{2,1,0:T(8,128)(2,1)} %copy-done.3, bf16[2,272,1024]{2,1,0:T(8,128)(2,1)} %collective-permute-done.5.refs_2_, ...), custom_call_target="tpu_custom_call" | custom-call | flops 17179869184 | bytes 62914560 | tf_op jit(solution)/shard_map/gate/pallas_call | solution.py:417
  139.0 4.0 %mix.1 = bf16[8,256,256]{2,1,0:T(8,128)(2,1)} custom-call(s32[5]{0:T(128)} %stack.38.meta, f32[8,2,256,256]{3,2,1,0:T(8,128)} %gate.1.gated, f32[8,2,8,256]{3,2,1,0:T(8,128)} %copy-done.6), custom_call_target="tpu_custom_call" | custom-call | flops 2097152 | bytes 5242880 | tf_op jit(solution)/shard_map/mix/pallas_call | solution.py:440
  143.0 2.9 %collective-permute-done.18.across = bf16[4,2,4,16,1024]{4,3,2,1,0:T(8,128)(2,1)} collective-permute-done((bf16[4,2,4,16,1024]{4,3,2,1,0:T(8,128)(2,1)}, bf16[4,2,4,16,1024]{4,3,2,1,0:T(8,128)(2,1)}, u32[]{:S(2)}, u32[]{:S(2)}) %collective-permute-start.18) | collective-permute-done | bytes 1048608 | tf_op jit(solution)/shard_map/ppermute | solution.py:413
  145.9 4.9 %all-to-all-start.2 = ((bf16[8,256,256]{2,1,0:T(8,128)(2,1)}), bf16[8,256,256]{2,1,0:T(8,128)(2,1)S(1)}, u32[]{:S(2)}, u32[]{:S(2)}) async-start(bf16[8,256,256]{2,1,0:T(8,128)(2,1)} %mix.1), calls=%async_computation.2 | async-start | bytes 2097152 | tf_op jit(solution)/shard_map/all_to_all | solution.py:457
  150.8 12.9 %all-to-all-done.2.mixed = bf16[8,256,256]{2,1,0:T(8,128)(2,1)S(1)} async-done(((bf16[8,256,256]{2,1,0:T(8,128)(2,1)}), bf16[8,256,256]{2,1,0:T(8,128)(2,1)S(1)}, u32[]{:S(2)}, u32[]{:S(2)}) %all-to-all-start.2) | async-done | bytes 1048608 | tf_op jit(solution)/shard_map/all_to_all | solution.py:457
  164.8 8.1 %head.1 = f32[2,256]{1,0:T(2,128)} custom-call(s32[5]{0:T(128)} %stack.38.meta, s32[2]{0:T(128)} %lengths.1, s32[2]{0:T(128)} %outcomes.1, s32[2,256]{1,0:T(2,128)} %moves.1, bf16[2,272,1024]{2,1,0:T(8,128)(2,1)} %constant_dynamic-update-slice_fusion.refs_0_.own, bf16[2,272,1024]{2,1,0:T(8,128)(2,1)} %copy-done.3, bf16[8,256,256]{2,1,0:T(8,128)(2,1)} %copy-done.1, ...), custom_call_target="tpu_custom_call" | custom-call | flops 2550136832 | bytes 12582912 | tf_op jit(solution)/shard_map/head/pallas_call | solution.py:459
  172.9 2.3 %collective-permute-start.22 = (f32[2,256]{1,0:T(2,128)}, f32[2,256]{1,0:T(2,128)S(1)}, u32[]{:S(2)}, u32[]{:S(2)}) collective-permute-start(f32[2,256]{1,0:T(2,128)} %head.1), channel_id=1, source_target_pairs={{0,1},{1,0},{2,3},{3,2},{4,5},{5,4},{6,7},{7,6},{8,9},{9,8},{10,11... | collective-permute-start | bytes 6152 | tf_op jit(solution)/shard_map/ppermute | solution.py:481
  (81 shorter events, 23.8 us)
Async XLA Ops:
  9.3 43.0 %all-to-all-start = ((bf16[32,4,16,256]{3,2,1,0:T(8,128)(2,1)}), bf16[32,4,16,256]{3,2,1,0:T(8,128)(2,1)}, u32[]{:S(2)}, u32[]{:S(2)}) async-start(bf16[32,4,16,256]{3,2,1,0:T(8,128)(2,1)} %bitcast.1), calls=%async_computation | async-start | bytes 2097152 | tf_op jit(solution)/shard_map/all_to_all | solution.py:348
  21.1 79.8 %all-gather.3.cloned.1.call-start = ((), (), s32[]{:S(2)}) async-start(), calls=%async_computation.3 | async-start | bytes 2228224 | tf_op jit(solution)/shard_map/all_gather | solution.py:354
  21.1 27.5 %collective-permute-start = (bf16[2,16,1024]{2,1,0:T(8,128)(2,1)S(1)}, bf16[2,16,1024]{2,1,0:T(8,128)(2,1)S(1)}, u32[]{:S(2)}, u32[]{:S(2)}) collective-permute-start(bf16[2,16,1024]{2,1,0:T(8,128)(2,1)S(1)} %slice.27), channel_id=1, source_target_pairs={{0,16},{16,32},{32,48},{48,64},{64,80},{80,96},{96,112},{112,128},... | collective-permute-start | bytes 196616 | tf_op jit(solution)/shard_map/ppermute | solution.py:345
  24.5 4.5 %collective-permute-start.1 = (bf16[16,1024]{1,0:T(8,128)(2,1)S(1)}, bf16[16,1024]{1,0:T(8,128)(2,1)S(1)}, u32[]{:S(2)}, u32[]{:S(2)}) collective-permute-start(bf16[16,1024]{1,0:T(8,128)(2,1)S(1)} %copy-done.7), channel_id=1, source_target_pairs={{0,1},{1,0},{128,129},{129,128},{2,3},{3,2},{130,131},{131,130},{4... | collective-permute-start | bytes 98312 | tf_op jit(solution)/shard_map/ppermute | solution.py:350
  25.9 4.6 %collective-permute-start.2 = (bf16[16,1024]{1,0:T(8,128)(2,1)S(1)}, bf16[16,1024]{1,0:T(8,128)(2,1)S(1)}, u32[]{:S(2)}, u32[]{:S(2)}) collective-permute-start(bf16[16,1024]{1,0:T(8,128)(2,1)S(1)} %copy-done.7), channel_id=1, source_target_pairs={{0,129},{129,0},{1,128},{128,1},{2,131},{131,2},{3,130},{130,3},{4... | collective-permute-start | bytes 98312 | tf_op jit(solution)/shard_map/ppermute | solution.py:350
  25.9 5.5 %collective-permute-start.3 = (bf16[16,1024]{1,0:T(8,128)(2,1)S(1)}, bf16[16,1024]{1,0:T(8,128)(2,1)S(1)}, u32[]{:S(2)}, u32[]{:S(2)}) collective-permute-start(bf16[16,1024]{1,0:T(8,128)(2,1)S(1)} %copy-done.7), channel_id=1, source_target_pairs={{0,128},{1,129},{128,0},{129,1},{2,130},{3,131},{130,2},{131,3},{4... | collective-permute-start | bytes 98312 | tf_op jit(solution)/shard_map/ppermute | solution.py:350
  51.0 26.5 %collective-permute-start.5 = (bf16[2,272,1024]{2,1,0:T(8,128)(2,1)}, bf16[2,272,1024]{2,1,0:T(8,128)(2,1)}, u32[]{:S(2)}, u32[]{:S(2)}) collective-permute-start(bf16[2,272,1024]{2,1,0:T(8,128)(2,1)} %constant_dynamic-update-slice_fusion.refs_0_.own), channel_id=1, source_target_pairs={{0,129},{129,0},{1,128},{128,1},{2,131},{131,2},{3,130},{130,3},{4... | collective-permute-start | bytes 3342344 | tf_op jit(solution)/shard_map/ppermute | solution.py:356
  51.0 27.6 %collective-permute-start.4 = (bf16[2,272,1024]{2,1,0:T(8,128)(2,1)}, bf16[2,272,1024]{2,1,0:T(8,128)(2,1)S(1)}, u32[]{:S(2)}, u32[]{:S(2)}) collective-permute-start(bf16[2,272,1024]{2,1,0:T(8,128)(2,1)} %constant_dynamic-update-slice_fusion.refs_0_.own), channel_id=1, source_target_pairs={{0,1},{1,0},{128,129},{129,128},{2,3},{3,2},{130,131},{131,130},{4... | collective-permute-start | bytes 3342344 | tf_op jit(solution)/shard_map/ppermute | solution.py:356
  52.3 26.4 %collective-permute-start.8 = (bf16[2,272,1024]{2,1,0:T(8,128)(2,1)}, bf16[2,272,1024]{2,1,0:T(8,128)(2,1)}, u32[]{:S(2)}, u32[]{:S(2)}) collective-permute-start(bf16[2,272,1024]{2,1,0:T(8,128)(2,1)} %constant_dynamic-update-slice_fusion.refs_0_.own), channel_id=1, source_target_pairs={{0,2},{2,0},{1,3},{3,1},{4,6},{6,4},{5,7},{7,5},{8,10},{10,8},{9,1... | collective-permute-start | bytes 3342344 | tf_op jit(solution)/shard_map/ppermute | solution.py:355
  52.3 27.1 %collective-permute-start.6 = (bf16[2,8,2,4,16,256]{5,4,3,2,1,0:T(8,128)(2,1)}, bf16[2,8,2,4,16,256]{5,4,3,2,1,0:T(8,128)(2,1)}, u32[]{:S(2)}, u32[]{:S(2)}) collective-permute-start(bf16[2,8,2,4,16,256]{5,4,3,2,1,0:T(8,128)(2,1)} %bitcast.2.refs_10_), channel_id=1, source_target_pairs={{0,4},{4,8},{8,12},{12,0},{1,5},{5,9},{9,13},{13,1},{2,6},{6,10},{... | collective-permute-start | bytes 3145736 | tf_op jit(solution)/shard_map/ppermute | solution.py:357
  53.8 25.6 %collective-permute-start.7 = (bf16[2,8,2,4,16,256]{5,4,3,2,1,0:T(8,128)(2,1)}, bf16[2,8,2,4,16,256]{5,4,3,2,1,0:T(8,128)(2,1)}, u32[]{:S(2)}, u32[]{:S(2)}) collective-permute-start(bf16[2,8,2,4,16,256]{5,4,3,2,1,0:T(8,128)(2,1)} %bitcast.2.refs_10_), channel_id=1, source_target_pairs={{0,12},{4,0},{8,4},{12,8},{1,13},{5,1},{9,5},{13,9},{2,14},{6,2},{... | collective-permute-start | bytes 3145736 | tf_op jit(solution)/shard_map/ppermute | solution.py:357
  79.4 21.5 %collective-permute-start.13 = (bf16[2,272,1024]{2,1,0:T(8,128)(2,1)S(1)}, bf16[2,272,1024]{2,1,0:T(8,128)(2,1)}, u32[]{:S(2)}, u32[]{:S(2)}) collective-permute-start(bf16[2,272,1024]{2,1,0:T(8,128)(2,1)S(1)} %collective-permute-done.4.refs_1_.pair), channel_id=1, source_target_pairs={{0,2},{2,0},{1,3},{3,1},{4,6},{6,4},{5,7},{7,5},{8,10},{10,8},{9,1... | collective-permute-start | bytes 3342344 | tf_op jit(solution)/shard_map/ppermute | solution.py:355
  79.4 20.7 %collective-permute-start.10 = (bf16[272,1024]{1,0:T(8,128)(2,1)S(1)}, bf16[272,1024]{1,0:T(8,128)(2,1)S(1)}, u32[]{:S(2)}, u32[]{:S(2)}) collective-permute-start(bf16[272,1024]{1,0:T(8,128)(2,1)S(1)} %slice_bitcast_fusion.1), channel_id=1, source_target_pairs={{0,129},{129,0},{1,128},{128,1},{2,131},{131,2},{3,130},{130,3},{4... | collective-permute-start | bytes 1671176 | tf_op jit(solution)/shard_map/ppermute | solution.py:366
  82.1 18.9 %collective-permute-start.9 = (bf16[272,1024]{1,0:T(8,128)(2,1)S(1)}, bf16[272,1024]{1,0:T(8,128)(2,1)}, u32[]{:S(2)}, u32[]{:S(2)}) collective-permute-start(bf16[272,1024]{1,0:T(8,128)(2,1)S(1)} %slice_bitcast_fusion), channel_id=1, source_target_pairs={{0,1},{1,0},{128,129},{129,128},{2,3},{3,2},{130,131},{131,130},{4... | collective-permute-start | bytes 1671176 | tf_op jit(solution)/shard_map/ppermute | solution.py:365
  83.9 15.1 %collective-permute-start.11 = (bf16[1,8,2,4,16,256]{5,4,3,2,1,0:T(8,128)(2,1)S(1)}, bf16[1,8,2,4,16,256]{5,4,3,2,1,0:T(8,128)(2,1)S(1)}, u32[]{:S(2)}, u32[]{:S(2)}) collective-permute-start(bf16[1,8,2,4,16,256]{5,4,3,2,1,0:T(8,128)(2,1)S(1)} %slice.30), channel_id=1, source_target_pairs={{0,4},{4,8},{8,12},{12,0},{1,5},{5,9},{9,13},{13,1},{2,6},{6,10},{... | collective-permute-start | bytes 1572872 | tf_op jit(solution)/shard_map/ppermute | solution.py:367
  86.5 13.6 %collective-permute-start.12 = (bf16[1,8,2,4,16,256]{5,4,3,2,1,0:T(8,128)(2,1)S(1)}, bf16[1,8,2,4,16,256]{5,4,3,2,1,0:T(8,128)(2,1)S(1)}, u32[]{:S(2)}, u32[]{:S(2)}) collective-permute-start(bf16[1,8,2,4,16,256]{5,4,3,2,1,0:T(8,128)(2,1)S(1)} %slice.31), channel_id=1, source_target_pairs={{0,12},{4,0},{8,4},{12,8},{1,13},{5,1},{9,5},{13,9},{2,14},{6,2},{... | collective-permute-start | bytes 1572872 | tf_op jit(solution)/shard_map/ppermute | solution.py:368
  100.9 27.5 %collective-permute-start.14 = (bf16[8,2,4,16,1024]{4,3,2,1,0:T(8,128)(2,1)}, bf16[8,2,4,16,1024]{4,3,2,1,0:T(8,128)(2,1)S(1)}, u32[]{:S(2)}, u32[]{:S(2)}) collective-permute-start(bf16[8,2,4,16,1024]{4,3,2,1,0:T(8,128)(2,1)} %bitcast.22), channel_id=1, source_target_pairs={{0,4},{2,14},{4,8},{6,2},{8,12},{10,6},{12,0},{14,10},{1,5},{3,15}... | collective-permute-start | bytes 6291464 | tf_op jit(solution)/shard_map/ppermute | solution.py:375
  102.2 4.7 %collective-permute-start.15 = (bf16[2,272,1024]{2,1,0:T(8,128)(2,1)}, bf16[2,272,1024]{2,1,0:T(8,128)(2,1)}, u32[]{:S(2)}, u32[]{:S(2)}) collective-permute-start(bf16[2,272,1024]{2,1,0:T(8,128)(2,1)} %collective-permute-done.5.refs_2_), channel_id=1, source_target_pairs={{0,2},{2,0},{1,3},{3,1},{4,6},{6,4},{5,7},{7,5},{8,10},{10,8},{9,1... | collective-permute-start | bytes 3342344 | tf_op jit(solution)/shard_map/ppermute | solution.py:355
  103.0 26.6 %collective-permute-start.19 = (bf16[1024,384]{1,0:T(8,128)(2,1)S(1)}, bf16[1024,384]{1,0:T(8,128)(2,1)}, u32[]{:S(2)}, u32[]{:S(2)}) collective-permute-start(bf16[1024,384]{1,0:T(8,128)(2,1)S(1)} %maximum_maximum_fusion.heads), channel_id=1, source_target_pairs={{0,1},{1,0},{2,3},{3,2},{4,5},{5,4},{6,7},{7,6},{8,9},{9,8},{10,11... | collective-permute-start | bytes 2359304 | tf_op jit(solution)/shard_map/ppermute | solution.py:415
  121.7 16.7 %all-to-all-start.1 = ((f32[8,2,8,256]{3,2,1,0:T(8,128)}), f32[8,2,8,256]{3,2,1,0:T(8,128)S(1)}, u32[]{:S(2)}, u32[]{:S(2)}) async-start(f32[8,2,8,256]{3,2,1,0:T(8,128)} %get-tuple-element.50), calls=%async_computation.1 | async-start | bytes 262144 | tf_op jit(solution)/shard_map/all_to_all | solution.py:416
  128.5 35.3 %collective-permute-start.20 = (bf16[8,2,4,16,1024]{4,3,2,1,0:T(8,128)(2,1)S(1)}, bf16[8,2,4,16,1024]{4,3,2,1,0:T(8,128)(2,1)}, u32[]{:S(2)}, u32[]{:S(2)}) collective-permute-start(bf16[8,2,4,16,1024]{4,3,2,1,0:T(8,128)(2,1)S(1)} %collective-permute-done.14.beside), channel_id=1, source_target_pairs={{0,2},{2,0},{1,3},{3,1},{4,6},{6,4},{5,7},{7,5},{8,10},{10,8},{9,1... | collective-permute-start | bytes 6291464 | tf_op jit(solution)/shard_map/ppermute | solution.py:355
  129.6 16.3 %collective-permute-start.18 = (bf16[4,2,4,16,1024]{4,3,2,1,0:T(8,128)(2,1)}, bf16[4,2,4,16,1024]{4,3,2,1,0:T(8,128)(2,1)}, u32[]{:S(2)}, u32[]{:S(2)}) collective-permute-start(bf16[4,2,4,16,1024]{4,3,2,1,0:T(8,128)(2,1)} %constant_dynamic-slice_fusion), channel_id=1, source_target_pairs={{0,4},{2,14},{4,8},{6,2},{8,12},{10,6},{12,0},{14,10},{1,5},{3,15}... | collective-permute-start | bytes 3145736 | tf_op jit(solution)/shard_map/ppermute | solution.py:413
  145.9 17.9 %collective-permute-start.21 = (bf16[4,2,4,16,1024]{4,3,2,1,0:T(8,128)(2,1)}, bf16[4,2,4,16,1024]{4,3,2,1,0:T(8,128)(2,1)}, u32[]{:S(2)}, u32[]{:S(2)}) collective-permute-start(bf16[4,2,4,16,1024]{4,3,2,1,0:T(8,128)(2,1)} %collective-permute-done.18.across), channel_id=1, source_target_pairs={{0,2},{2,0},{1,3},{3,1},{4,6},{6,4},{5,7},{7,5},{8,10},{10,8},{9,1... | collective-permute-start | bytes 3145736 | tf_op jit(solution)/shard_map/ppermute | solution.py:355
  145.9 17.9 %all-to-all-start.2 = ((bf16[8,256,256]{2,1,0:T(8,128)(2,1)}), bf16[8,256,256]{2,1,0:T(8,128)(2,1)S(1)}, u32[]{:S(2)}, u32[]{:S(2)}) async-start(bf16[8,256,256]{2,1,0:T(8,128)(2,1)} %mix.1), calls=%async_computation.2 | async-start | bytes 2097152 | tf_op jit(solution)/shard_map/all_to_all | solution.py:457
  (15 other events, 124.1 us)
Sparse Core Ops, SparseCore 0:
  49.5 38.6 all-gather.2

commit v5 on v4

--- a/solution.py
+++ b/solution.py
@@ -219,23 +219,22 @@
 
 def down_copies(pieces, down_w, w, c, yh, x, sems):
     column, beside, beside_c, across, across_c = pieces
-    gathered = (
-        (column, 0, 0),
-        (beside, 3 - 2 * c, 0),
-        (beside_c, 1 + 2 * c, 0),
-        (across, 2, 4 * c),
-        (across_c, 2, 4 - 4 * c),
-    )
+    halves = ((across, 2, 4 * c), (across_c, 2, 4 - 4 * c))
+    wholes = ((column, 0), (beside, 3 - 2 * c), (beside_c, 1 + 2 * c))
     groups = []
     for n, (h, rel) in enumerate(((yh, ((0, w), (1, 1 - w))), (1 - yh, ((3, w), (2, 1 - w))))):
-        copies = []
-        for r, v in rel:
-            at = pl.ds(pl.multiple_of(v * HALF, HALF), HALF)
-            for src, dx, first in gathered:
-                to = down_w.at[h, pl.ds(first, src.shape[0]), lax.rem(x + dx, 4), :, :, at]
-                sem = sems.at[n, len(copies)]
-                copies.append(pltpu.make_async_copy(src.at[:, :, r], to, sem))
-        groups.append(copies)
+        for part in range(2):
+            copies = []
+            for r, v in rel:
+                at = pl.ds(pl.multiple_of(v * HALF, HALF), HALF)
+                moved = [(src.at[part * 4 : part * 4 + 4, :, r], dx, part * 4) for src, dx in wholes]
+                if part == 0:
+                    moved += [(src.at[:, :, r], dx, first) for src, dx, first in halves]
+                for src, dx, first in moved:
+                    to = down_w.at[h, pl.ds(first, 4), lax.rem(x + dx, 4), :, :, at]
+                    sem = sems.at[n * 2 + part, len(copies)]
+                    copies.append(pltpu.make_async_copy(src, to, sem))
+            groups.append(copies)
     return groups
 
 
@@ -279,14 +278,13 @@
         pltpu.make_async_copy(heads, wp.at[w], f_sems.at[2]),
         pltpu.make_async_copy(heads_oth, wp.at[1 - w], f_sems.at[3]),
     ]
-    start(to_mix + to_down[0] + to_feat + to_down[1] + to_wp)
+    start(to_mix + to_down[0] + to_feat + to_down[1] + to_down[2] + to_down[3] + to_wp)
     wait(to_mix)
     square = jnp.zeros((STEPS, 1), F32)
     width = 512
     for k in range(4):
         h, j = (yh if k < 2 else 1 - yh), k % 2
-        if j == 0:
-            wait(to_down[k // 2])
+        wait(to_down[k])
         rows = down_w[h, j * 4 : (j + 1) * 4].reshape(width, D)
         down = lax.dot_general(
             mix[...], rows, (((1,), (1,)), ((), ())), preferred_element_type=F32
@@ -470,7 +468,7 @@
             pltpu.VMEM((2, HALF, COLS), BF16),
             sems(4),
             sems(8),
-            pltpu.SemaphoreType.DMA((2, 10)),
+            pltpu.SemaphoreType.DMA((4, 10)),
         ],
         compiler_params=params(),
         cost_estimate=pl.CostEstimate(

time: 187 us -> 187 us (level)
  no operation moved by 1% of the time
where the time goes in v5:
time: 187 us; the launch traced here: 185 us
  waiting for transfers between devices  74.6 us (40%)
  starting transfers between devices  45.8 us (24%)
  Pallas kernels  35.8 us (19%)
  between operations  14.3 us (8%)
  local copies, waits for them, and re-layouts  12.6 us (7%)
    ppermute x1, waiting for transfers between devices, shards(): lax.ppermute(own, ring, OTHER)  20.4 us
    ppermute x1, waiting for transfers between devices, shards(): lax.ppermute(embedded[:, STEPS - HALO:], ('yh', 'z'), [(k, k + 1) for k i...  17.2 us
    pallas_call x1, Pallas kernels, shards(): pl.pallas_call(recur_kernel, name='recur', out_shape=(jax.ShapeDtypeStruc...  14.8 us
    all_to_all x1, waiting for transfers between devices, shards(): mixed = lax.all_to_all(mixed, ('yh', 'c', 'w'), 0, 0, tiled=True)  12.9 us
    all_to_all x1, starting transfers between devices, shards(): rows = lax.all_to_all(quarters, ('yh', 'z', 'c'), 0, 0, tiled=True)  11.8 us
    ppermute x1, waiting for transfers between devices, shards(): low = lax.ppermute(behind[:1], 'x', turn(4, 1))  10.6 us
    pallas_call x1, Pallas kernels, shards(): pl.pallas_call(gate_kernel, name='gate', out_shape=jax.ShapeDtypeStruct((...  8.74 us
    pallas_call x1, Pallas kernels, shards(): pl.pallas_call(head_kernel, name='head', out_shape=jax.ShapeDtypeStruct((...  8.27 us
  transfers between devices with their start and end apart: 27, of which 13 were waited for; matrix products, arithmetic and copies ran while one was open for 5% of the time, Pallas kernels for 15%

profile of v5, /device:TPU:16, one launch (start us, length us, event | category | flops | bytes accessed | tf_op | source)
XLA Modules:
  0.0 184.6 jit_solution(6823377001847102397)
XLA Ops:
  9.3 11.8 %all-to-all-start = ((bf16[32,4,16,256]{3,2,1,0:T(8,128)(2,1)}), bf16[32,4,16,256]{3,2,1,0:T(8,128)(2,1)}, u32[]{:S(2)}, u32[]{:S(2)}) async-start(bf16[32,4,16,256]{3,2,1,0:T(8,128)(2,1)} %bitcast.1), calls=%async_computation | async-start | bytes 2097152 | tf_op jit(solution)/shard_map/all_to_all | solution.py:346
  21.1 3.4 %collective-permute-start = (bf16[2,16,1024]{2,1,0:T(8,128)(2,1)S(1)}, bf16[2,16,1024]{2,1,0:T(8,128)(2,1)S(1)}, u32[]{:S(2)}, u32[]{:S(2)}) collective-permute-start(bf16[2,16,1024]{2,1,0:T(8,128)(2,1)S(1)} %slice.27), channel_id=1, source_target_pairs={{0,16},{16,32},{32,48},{48,64},{64,80},{80,96},{96,112},{112,128},... | collective-permute-start | bytes 196616 | tf_op jit(solution)/shard_map/ppermute | solution.py:343
  24.5 1.4 collective-permute-start.1
  25.9 2.8 %collective-permute-start.3 = (bf16[16,1024]{1,0:T(8,128)(2,1)S(1)}, bf16[16,1024]{1,0:T(8,128)(2,1)S(1)}, u32[]{:S(2)}, u32[]{:S(2)}) collective-permute-start(bf16[16,1024]{1,0:T(8,128)(2,1)S(1)} %copy-done.7), channel_id=1, source_target_pairs={{0,128},{1,129},{128,0},{129,1},{2,130},{3,131},{130,2},{131,3},{4... | collective-permute-start | bytes 98312 | tf_op jit(solution)/shard_map/ppermute | solution.py:348
  29.1 1.4 collective-permute-done.2
  31.4 17.2 %collective-permute-done = bf16[2,16,1024]{2,1,0:T(8,128)(2,1)S(1)} collective-permute-done((bf16[2,16,1024]{2,1,0:T(8,128)(2,1)S(1)}, bf16[2,16,1024]{2,1,0:T(8,128)(2,1)S(1)}, u32[]{:S(2)}, u32[]{:S(2)}) %collective-permute-start) | collective-permute-done | bytes 65568 | tf_op jit(solution)/shard_map/ppermute | solution.py:343
  52.3 1.5 collective-permute-start.6
  53.8 1.7 collective-permute-start.7
  57.1 20.4 %collective-permute-done.5.refs_2_ = bf16[2,272,1024]{2,1,0:T(8,128)(2,1)} collective-permute-done((bf16[2,272,1024]{2,1,0:T(8,128)(2,1)}, bf16[2,272,1024]{2,1,0:T(8,128)(2,1)}, u32[]{:S(2)}, u32[]{:S(2)}) %collective-permute-start.5) | collective-permute-done | bytes 1114144 | tf_op jit(solution)/shard_map/ppermute | solution.py:354
  79.4 2.6 %collective-permute-start.10 = (bf16[272,1024]{1,0:T(8,128)(2,1)S(1)}, bf16[272,1024]{1,0:T(8,128)(2,1)S(1)}, u32[]{:S(2)}, u32[]{:S(2)}) collective-permute-start(bf16[272,1024]{1,0:T(8,128)(2,1)S(1)} %slice_bitcast_fusion.1), channel_id=1, source_target_pairs={{0,129},{129,0},{1,128},{128,1},{2,131},{131,2},{3,130},{130,3},{4... | collective-permute-start | bytes 1671176 | tf_op jit(solution)/shard_map/ppermute | solution.py:364
  83.9 1.6 collective-permute-start.11
  86.5 1.8 collective-permute-start.12
  88.4 10.6 %collective-permute-done.11.refs_13_ = bf16[1,8,2,4,16,256]{5,4,3,2,1,0:T(8,128)(2,1)S(1)} collective-permute-done((bf16[1,8,2,4,16,256]{5,4,3,2,1,0:T(8,128)(2,1)S(1)}, bf16[1,8,2,4,16,256]{5,4,3,2,1,0:T(8,128)(2,1)S(1)}, u32[]{:S(2)}, u32[]{:S(2)}) %collective-permute-start.11) | collective-permute-done | bytes 524320 | tf_op jit(solution)/shard_map/ppermute | solution.py:365
  104.3 2.6 %collective-permute-done.16.refs_8_ = bf16[272,1024]{1,0:T(8,128)(2,1)} collective-permute-done((bf16[272,1024]{1,0:T(8,128)(2,1)}, bf16[272,1024]{1,0:T(8,128)(2,1)}, u32[]{:S(2)}, u32[]{:S(2)}) %collective-permute-start.16) | collective-permute-done | bytes 557088 | tf_op jit(solution)/shard_map/ppermute | solution.py:353
  106.9 14.8 %recur.1 = (f32[2,2048,128]{2,1,0:T(8,128)}, f32[2,2048,128]{2,1,0:T(8,128)}, f32[8,2,8,256]{3,2,1,0:T(8,128)}) custom-call(s32[5]{0:T(128)} %stack.38.meta, bf16[2,272,1024]{2,1,0:T(8,128)(2,1)} %constant_dynamic-update-slice_fusion.refs_0_.own, bf16[2,272,1024]{2,1,0:T(8,128)(2,1)} %copy-done.3, bf16[2,272,1024]{2,1,0:T(8,128)(2,1)} %collective-permute-done.5.refs_2_, ...), custom_call_target="tpu_custom_call" | custom-call | flops 6442450944 | bytes 15728640 | tf_op jit(solution)/shard_map/recur/pallas_call | solution.py:382
  121.7 4.6 %all-to-all-start.1 = ((f32[8,2,8,256]{3,2,1,0:T(8,128)}), f32[8,2,8,256]{3,2,1,0:T(8,128)S(1)}, u32[]{:S(2)}, u32[]{:S(2)}) async-start(f32[8,2,8,256]{3,2,1,0:T(8,128)} %get-tuple-element.50), calls=%async_computation.1 | async-start | bytes 262144 | tf_op jit(solution)/shard_map/all_to_all | solution.py:414
  126.3 2.2 %collective-permute-done.14.beside = bf16[8,2,4,16,1024]{4,3,2,1,0:T(8,128)(2,1)S(1)} collective-permute-done((bf16[8,2,4,16,1024]{4,3,2,1,0:T(8,128)(2,1)}, bf16[8,2,4,16,1024]{4,3,2,1,0:T(8,128)(2,1)S(1)}, u32[]{:S(2)}, u32[]{:S(2)}) %collective-permute-start.14) | collective-permute-done | bytes 2097184 | tf_op jit(solution)/shard_map/ppermute | solution.py:373
  129.6 8.7 %gate.1.gated = f32[8,2,256,256]{3,2,1,0:T(8,128)} custom-call(s32[5]{0:T(128)} %stack.38.meta, bf16[2,272,1024]{2,1,0:T(8,128)(2,1)} %constant_dynamic-update-slice_fusion.refs_0_.own, bf16[2,272,1024]{2,1,0:T(8,128)(2,1)} %copy-done.3, bf16[2,272,1024]{2,1,0:T(8,128)(2,1)} %collective-permute-done.5.refs_2_, ...), custom_call_target="tpu_custom_call" | custom-call | flops 17179869184 | bytes 62914560 | tf_op jit(solution)/shard_map/gate/pallas_call | solution.py:415
  139.0 4.0 %mix.1 = bf16[8,256,256]{2,1,0:T(8,128)(2,1)} custom-call(s32[5]{0:T(128)} %stack.38.meta, f32[8,2,256,256]{3,2,1,0:T(8,128)} %gate.1.gated, f32[8,2,8,256]{3,2,1,0:T(8,128)} %copy-done.6), custom_call_target="tpu_custom_call" | custom-call | flops 2097152 | bytes 5242880 | tf_op jit(solution)/shard_map/mix/pallas_call | solution.py:438
  143.0 2.9 %collective-permute-done.18.across = bf16[4,2,4,16,1024]{4,3,2,1,0:T(8,128)(2,1)} collective-permute-done((bf16[4,2,4,16,1024]{4,3,2,1,0:T(8,128)(2,1)}, bf16[4,2,4,16,1024]{4,3,2,1,0:T(8,128)(2,1)}, u32[]{:S(2)}, u32[]{:S(2)}) %collective-permute-start.18) | collective-permute-done | bytes 1048608 | tf_op jit(solution)/shard_map/ppermute | solution.py:411
  145.9 4.9 %all-to-all-start.2 = ((bf16[8,256,256]{2,1,0:T(8,128)(2,1)}), bf16[8,256,256]{2,1,0:T(8,128)(2,1)S(1)}, u32[]{:S(2)}, u32[]{:S(2)}) async-start(bf16[8,256,256]{2,1,0:T(8,128)(2,1)} %mix.1), calls=%async_computation.2 | async-start | bytes 2097152 | tf_op jit(solution)/shard_map/all_to_all | solution.py:455
  150.8 12.9 %all-to-all-done.2.mixed = bf16[8,256,256]{2,1,0:T(8,128)(2,1)S(1)} async-done(((bf16[8,256,256]{2,1,0:T(8,128)(2,1)}), bf16[8,256,256]{2,1,0:T(8,128)(2,1)S(1)}, u32[]{:S(2)}, u32[]{:S(2)}) %all-to-all-start.2) | async-done | bytes 1048608 | tf_op jit(solution)/shard_map/all_to_all | solution.py:455
  164.8 8.3 %head.1 = f32[2,256]{1,0:T(2,128)} custom-call(s32[5]{0:T(128)} %stack.38.meta, s32[2]{0:T(128)} %lengths.1, s32[2]{0:T(128)} %outcomes.1, s32[2,256]{1,0:T(2,128)} %moves.1, bf16[2,272,1024]{2,1,0:T(8,128)(2,1)} %constant_dynamic-update-slice_fusion.refs_0_.own, bf16[2,272,1024]{2,1,0:T(8,128)(2,1)} %copy-done.3, bf16[8,256,256]{2,1,0:T(8,128)(2,1)} %copy-done.1, ...), custom_call_target="tpu_custom_call" | custom-call | flops 2550136832 | bytes 12582912 | tf_op jit(solution)/shard_map/head/pallas_call | solution.py:457
  173.1 2.2 %collective-permute-start.22 = (f32[2,256]{1,0:T(2,128)}, f32[2,256]{1,0:T(2,128)S(1)}, u32[]{:S(2)}, u32[]{:S(2)}) collective-permute-start(f32[2,256]{1,0:T(2,128)} %head.1), channel_id=1, source_target_pairs={{0,1},{1,0},{2,3},{3,2},{4,5},{5,4},{6,7},{7,6},{8,9},{9,8},{10,11... | collective-permute-start | bytes 6152 | tf_op jit(solution)/shard_map/ppermute | solution.py:479
  (81 shorter events, 23.8 us)
Async XLA Ops:
  9.3 43.0 %all-to-all-start = ((bf16[32,4,16,256]{3,2,1,0:T(8,128)(2,1)}), bf16[32,4,16,256]{3,2,1,0:T(8,128)(2,1)}, u32[]{:S(2)}, u32[]{:S(2)}) async-start(bf16[32,4,16,256]{3,2,1,0:T(8,128)(2,1)} %bitcast.1), calls=%async_computation | async-start | bytes 2097152 | tf_op jit(solution)/shard_map/all_to_all | solution.py:346
  21.1 79.8 %all-gather.3.cloned.1.call-start = ((), (), s32[]{:S(2)}) async-start(), calls=%async_computation.3 | async-start | bytes 2228224 | tf_op jit(solution)/shard_map/all_gather | solution.py:352
  21.1 27.5 %collective-permute-start = (bf16[2,16,1024]{2,1,0:T(8,128)(2,1)S(1)}, bf16[2,16,1024]{2,1,0:T(8,128)(2,1)S(1)}, u32[]{:S(2)}, u32[]{:S(2)}) collective-permute-start(bf16[2,16,1024]{2,1,0:T(8,128)(2,1)S(1)} %slice.27), channel_id=1, source_target_pairs={{0,16},{16,32},{32,48},{48,64},{64,80},{80,96},{96,112},{112,128},... | collective-permute-start | bytes 196616 | tf_op jit(solution)/shard_map/ppermute | solution.py:343
  24.5 4.5 %collective-permute-start.1 = (bf16[16,1024]{1,0:T(8,128)(2,1)S(1)}, bf16[16,1024]{1,0:T(8,128)(2,1)S(1)}, u32[]{:S(2)}, u32[]{:S(2)}) collective-permute-start(bf16[16,1024]{1,0:T(8,128)(2,1)S(1)} %copy-done.7), channel_id=1, source_target_pairs={{0,1},{1,0},{128,129},{129,128},{2,3},{3,2},{130,131},{131,130},{4... | collective-permute-start | bytes 98312 | tf_op jit(solution)/shard_map/ppermute | solution.py:348
  25.9 4.6 %collective-permute-start.2 = (bf16[16,1024]{1,0:T(8,128)(2,1)S(1)}, bf16[16,1024]{1,0:T(8,128)(2,1)S(1)}, u32[]{:S(2)}, u32[]{:S(2)}) collective-permute-start(bf16[16,1024]{1,0:T(8,128)(2,1)S(1)} %copy-done.7), channel_id=1, source_target_pairs={{0,129},{129,0},{1,128},{128,1},{2,131},{131,2},{3,130},{130,3},{4... | collective-permute-start | bytes 98312 | tf_op jit(solution)/shard_map/ppermute | solution.py:348
  25.9 5.5 %collective-permute-start.3 = (bf16[16,1024]{1,0:T(8,128)(2,1)S(1)}, bf16[16,1024]{1,0:T(8,128)(2,1)S(1)}, u32[]{:S(2)}, u32[]{:S(2)}) collective-permute-start(bf16[16,1024]{1,0:T(8,128)(2,1)S(1)} %copy-done.7), channel_id=1, source_target_pairs={{0,128},{1,129},{128,0},{129,1},{2,130},{3,131},{130,2},{131,3},{4... | collective-permute-start | bytes 98312 | tf_op jit(solution)/shard_map/ppermute | solution.py:348
  51.0 26.5 %collective-permute-start.5 = (bf16[2,272,1024]{2,1,0:T(8,128)(2,1)}, bf16[2,272,1024]{2,1,0:T(8,128)(2,1)}, u32[]{:S(2)}, u32[]{:S(2)}) collective-permute-start(bf16[2,272,1024]{2,1,0:T(8,128)(2,1)} %constant_dynamic-update-slice_fusion.refs_0_.own), channel_id=1, source_target_pairs={{0,129},{129,0},{1,128},{128,1},{2,131},{131,2},{3,130},{130,3},{4... | collective-permute-start | bytes 3342344 | tf_op jit(solution)/shard_map/ppermute | solution.py:354
  51.0 27.6 %collective-permute-start.4 = (bf16[2,272,1024]{2,1,0:T(8,128)(2,1)}, bf16[2,272,1024]{2,1,0:T(8,128)(2,1)S(1)}, u32[]{:S(2)}, u32[]{:S(2)}) collective-permute-start(bf16[2,272,1024]{2,1,0:T(8,128)(2,1)} %constant_dynamic-update-slice_fusion.refs_0_.own), channel_id=1, source_target_pairs={{0,1},{1,0},{128,129},{129,128},{2,3},{3,2},{130,131},{131,130},{4... | collective-permute-start | bytes 3342344 | tf_op jit(solution)/shard_map/ppermute | solution.py:354
  52.3 26.4 %collective-permute-start.8 = (bf16[2,272,1024]{2,1,0:T(8,128)(2,1)}, bf16[2,272,1024]{2,1,0:T(8,128)(2,1)}, u32[]{:S(2)}, u32[]{:S(2)}) collective-permute-start(bf16[2,272,1024]{2,1,0:T(8,128)(2,1)} %constant_dynamic-update-slice_fusion.refs_0_.own), channel_id=1, source_target_pairs={{0,2},{2,0},{1,3},{3,1},{4,6},{6,4},{5,7},{7,5},{8,10},{10,8},{9,1... | collective-permute-start | bytes 3342344 | tf_op jit(solution)/shard_map/ppermute | solution.py:353
  52.3 27.1 %collective-permute-start.6 = (bf16[2,8,2,4,16,256]{5,4,3,2,1,0:T(8,128)(2,1)}, bf16[2,8,2,4,16,256]{5,4,3,2,1,0:T(8,128)(2,1)}, u32[]{:S(2)}, u32[]{:S(2)}) collective-permute-start(bf16[2,8,2,4,16,256]{5,4,3,2,1,0:T(8,128)(2,1)} %bitcast.2.refs_10_), channel_id=1, source_target_pairs={{0,4},{4,8},{8,12},{12,0},{1,5},{5,9},{9,13},{13,1},{2,6},{6,10},{... | collective-permute-start | bytes 3145736 | tf_op jit(solution)/shard_map/ppermute | solution.py:355
  53.8 25.6 %collective-permute-start.7 = (bf16[2,8,2,4,16,256]{5,4,3,2,1,0:T(8,128)(2,1)}, bf16[2,8,2,4,16,256]{5,4,3,2,1,0:T(8,128)(2,1)}, u32[]{:S(2)}, u32[]{:S(2)}) collective-permute-start(bf16[2,8,2,4,16,256]{5,4,3,2,1,0:T(8,128)(2,1)} %bitcast.2.refs_10_), channel_id=1, source_target_pairs={{0,12},{4,0},{8,4},{12,8},{1,13},{5,1},{9,5},{13,9},{2,14},{6,2},{... | collective-permute-start | bytes 3145736 | tf_op jit(solution)/shard_map/ppermute | solution.py:355
  79.4 21.5 %collective-permute-start.13 = (bf16[2,272,1024]{2,1,0:T(8,128)(2,1)S(1)}, bf16[2,272,1024]{2,1,0:T(8,128)(2,1)}, u32[]{:S(2)}, u32[]{:S(2)}) collective-permute-start(bf16[2,272,1024]{2,1,0:T(8,128)(2,1)S(1)} %collective-permute-done.4.refs_1_.pair), channel_id=1, source_target_pairs={{0,2},{2,0},{1,3},{3,1},{4,6},{6,4},{5,7},{7,5},{8,10},{10,8},{9,1... | collective-permute-start | bytes 3342344 | tf_op jit(solution)/shard_map/ppermute | solution.py:353
  79.4 20.7 %collective-permute-start.10 = (bf16[272,1024]{1,0:T(8,128)(2,1)S(1)}, bf16[272,1024]{1,0:T(8,128)(2,1)S(1)}, u32[]{:S(2)}, u32[]{:S(2)}) collective-permute-start(bf16[272,1024]{1,0:T(8,128)(2,1)S(1)} %slice_bitcast_fusion.1), channel_id=1, source_target_pairs={{0,129},{129,0},{1,128},{128,1},{2,131},{131,2},{3,130},{130,3},{4... | collective-permute-start | bytes 1671176 | tf_op jit(solution)/shard_map/ppermute | solution.py:364
  82.1 18.9 %collective-permute-start.9 = (bf16[272,1024]{1,0:T(8,128)(2,1)S(1)}, bf16[272,1024]{1,0:T(8,128)(2,1)}, u32[]{:S(2)}, u32[]{:S(2)}) collective-permute-start(bf16[272,1024]{1,0:T(8,128)(2,1)S(1)} %slice_bitcast_fusion), channel_id=1, source_target_pairs={{0,1},{1,0},{128,129},{129,128},{2,3},{3,2},{130,131},{131,130},{4... | collective-permute-start | bytes 1671176 | tf_op jit(solution)/shard_map/ppermute | solution.py:363
  83.9 15.1 %collective-permute-start.11 = (bf16[1,8,2,4,16,256]{5,4,3,2,1,0:T(8,128)(2,1)S(1)}, bf16[1,8,2,4,16,256]{5,4,3,2,1,0:T(8,128)(2,1)S(1)}, u32[]{:S(2)}, u32[]{:S(2)}) collective-permute-start(bf16[1,8,2,4,16,256]{5,4,3,2,1,0:T(8,128)(2,1)S(1)} %slice.30), channel_id=1, source_target_pairs={{0,4},{4,8},{8,12},{12,0},{1,5},{5,9},{9,13},{13,1},{2,6},{6,10},{... | collective-permute-start | bytes 1572872 | tf_op jit(solution)/shard_map/ppermute | solution.py:365
  86.5 13.6 %collective-permute-start.12 = (bf16[1,8,2,4,16,256]{5,4,3,2,1,0:T(8,128)(2,1)S(1)}, bf16[1,8,2,4,16,256]{5,4,3,2,1,0:T(8,128)(2,1)S(1)}, u32[]{:S(2)}, u32[]{:S(2)}) collective-permute-start(bf16[1,8,2,4,16,256]{5,4,3,2,1,0:T(8,128)(2,1)S(1)} %slice.31), channel_id=1, source_target_pairs={{0,12},{4,0},{8,4},{12,8},{1,13},{5,1},{9,5},{13,9},{2,14},{6,2},{... | collective-permute-start | bytes 1572872 | tf_op jit(solution)/shard_map/ppermute | solution.py:366
  100.9 27.5 %collective-permute-start.14 = (bf16[8,2,4,16,1024]{4,3,2,1,0:T(8,128)(2,1)}, bf16[8,2,4,16,1024]{4,3,2,1,0:T(8,128)(2,1)S(1)}, u32[]{:S(2)}, u32[]{:S(2)}) collective-permute-start(bf16[8,2,4,16,1024]{4,3,2,1,0:T(8,128)(2,1)} %bitcast.22), channel_id=1, source_target_pairs={{0,4},{2,14},{4,8},{6,2},{8,12},{10,6},{12,0},{14,10},{1,5},{3,15}... | collective-permute-start | bytes 6291464 | tf_op jit(solution)/shard_map/ppermute | solution.py:373
  102.2 4.7 %collective-permute-start.15 = (bf16[2,272,1024]{2,1,0:T(8,128)(2,1)}, bf16[2,272,1024]{2,1,0:T(8,128)(2,1)}, u32[]{:S(2)}, u32[]{:S(2)}) collective-permute-start(bf16[2,272,1024]{2,1,0:T(8,128)(2,1)} %collective-permute-done.5.refs_2_), channel_id=1, source_target_pairs={{0,2},{2,0},{1,3},{3,1},{4,6},{6,4},{5,7},{7,5},{8,10},{10,8},{9,1... | collective-permute-start | bytes 3342344 | tf_op jit(solution)/shard_map/ppermute | solution.py:353
  103.0 26.6 %collective-permute-start.19 = (bf16[1024,384]{1,0:T(8,128)(2,1)S(1)}, bf16[1024,384]{1,0:T(8,128)(2,1)}, u32[]{:S(2)}, u32[]{:S(2)}) collective-permute-start(bf16[1024,384]{1,0:T(8,128)(2,1)S(1)} %maximum_maximum_fusion.heads), channel_id=1, source_target_pairs={{0,1},{1,0},{2,3},{3,2},{4,5},{5,4},{6,7},{7,6},{8,9},{9,8},{10,11... | collective-permute-start | bytes 2359304 | tf_op jit(solution)/shard_map/ppermute | solution.py:413
  121.7 16.7 %all-to-all-start.1 = ((f32[8,2,8,256]{3,2,1,0:T(8,128)}), f32[8,2,8,256]{3,2,1,0:T(8,128)S(1)}, u32[]{:S(2)}, u32[]{:S(2)}) async-start(f32[8,2,8,256]{3,2,1,0:T(8,128)} %get-tuple-element.50), calls=%async_computation.1 | async-start | bytes 262144 | tf_op jit(solution)/shard_map/all_to_all | solution.py:414
  128.5 35.3 %collective-permute-start.20 = (bf16[8,2,4,16,1024]{4,3,2,1,0:T(8,128)(2,1)S(1)}, bf16[8,2,4,16,1024]{4,3,2,1,0:T(8,128)(2,1)}, u32[]{:S(2)}, u32[]{:S(2)}) collective-permute-start(bf16[8,2,4,16,1024]{4,3,2,1,0:T(8,128)(2,1)S(1)} %collective-permute-done.14.beside), channel_id=1, source_target_pairs={{0,2},{2,0},{1,3},{3,1},{4,6},{6,4},{5,7},{7,5},{8,10},{10,8},{9,1... | collective-permute-start | bytes 6291464 | tf_op jit(solution)/shard_map/ppermute | solution.py:353
  129.6 16.3 %collective-permute-start.18 = (bf16[4,2,4,16,1024]{4,3,2,1,0:T(8,128)(2,1)}, bf16[4,2,4,16,1024]{4,3,2,1,0:T(8,128)(2,1)}, u32[]{:S(2)}, u32[]{:S(2)}) collective-permute-start(bf16[4,2,4,16,1024]{4,3,2,1,0:T(8,128)(2,1)} %constant_dynamic-slice_fusion), channel_id=1, source_target_pairs={{0,4},{2,14},{4,8},{6,2},{8,12},{10,6},{12,0},{14,10},{1,5},{3,15}... | collective-permute-start | bytes 3145736 | tf_op jit(solution)/shard_map/ppermute | solution.py:411
  145.9 17.9 %collective-permute-start.21 = (bf16[4,2,4,16,1024]{4,3,2,1,0:T(8,128)(2,1)}, bf16[4,2,4,16,1024]{4,3,2,1,0:T(8,128)(2,1)}, u32[]{:S(2)}, u32[]{:S(2)}) collective-permute-start(bf16[4,2,4,16,1024]{4,3,2,1,0:T(8,128)(2,1)} %collective-permute-done.18.across), channel_id=1, source_target_pairs={{0,2},{2,0},{1,3},{3,1},{4,6},{6,4},{5,7},{7,5},{8,10},{10,8},{9,1... | collective-permute-start | bytes 3145736 | tf_op jit(solution)/shard_map/ppermute | solution.py:353
  145.9 17.9 %all-to-all-start.2 = ((bf16[8,256,256]{2,1,0:T(8,128)(2,1)}), bf16[8,256,256]{2,1,0:T(8,128)(2,1)S(1)}, u32[]{:S(2)}, u32[]{:S(2)}) async-start(bf16[8,256,256]{2,1,0:T(8,128)(2,1)} %mix.1), calls=%async_computation.2 | async-start | bytes 2097152 | tf_op jit(solution)/shard_map/all_to_all | solution.py:455
  (15 other events, 124.1 us)
Sparse Core Ops, SparseCore 0:
  49.5 38.6 all-gather.2
